TPU v7x, 32 devices: a whole 2x2x4 slice. The times are simulated.
32 devices in a mesh: ctx: 8 (over z, x), tp: 4 (over y, core).
Axes of the slice: x: 2, y: 2, z: 4, core: 2. Of those that a mesh axis runs over, the one named last changes fastest.
Arguments:
- inputs: bfloat16 [2048, 3, 4096], P('ctx', None, 'tp'), may hold values from -6 to 6
- short_filter: float32 [3, 3, 4096], P(None, None, 'tp'), may hold values from -2.5 to 2.5
- long_filter: bfloat16 [256, 128], P('tp'), may hold values from -0.5 to 0.5
- out_weight: bfloat16 [4096, 4096], P('tp'), may hold values from -0.09375 to 0.09375
- out_cotangent: bfloat16 [2048, 4096], P('ctx'), may hold values from -6 to 6
Outputs:
- result: bfloat16 [2048, 4096], P('ctx')
- grad_inputs: bfloat16 [2048, 3, 4096], P('ctx', None, 'tp')
- grad_short: float32 [3, 3, 4096], P(None, None, 'tp')
- grad_long: float32 [256, 128], P('tp')
All inputs are finite; a program needn't handle non-finite values.
Results may differ from a plain program's by a relative error of at most 0.009.
Values may be sent and summed in bfloat16 or wider, within the bound.
No kernel may reach another device: no remote copies, remote signals or barrier semaphores. Data moves between devices by JAX's collectives and lax.ppermute only.
A program may use at most 128 MiB of HBM per device.

v0:
```python
import jax
import jax.numpy as jnp
from jax import lax
from jax.sharding import PartitionSpec as P


def shifted(value, axis, steps):
    count = lax.axis_size(axis)
    initial, last = (max(0, -steps), min(count, count - steps))
    return lax.ppermute(value, axis, [(source, source + steps) for source in range(initial, last)])


def short_conv(extended, taps, count):
    span = taps.shape[0]
    total = taps[0] * extended[span - 1 : span - 1 + count]
    for lag in range(1, span):
        total = total + taps[lag] * extended[span - 1 - lag : span - 1 - lag + count]
    return total


def tap_table(filt, forward):
    span = filt.shape[1]
    row_pos = jnp.arange(span)[:, None]
    col_pos = jnp.arange(2 * span)[None, :]
    offset = row_pos - col_pos + span if forward else col_pos - row_pos
    valid = (offset >= 0) & (offset < span)
    picked = filt[:, jnp.clip(offset, 0, span - 1)]
    return jnp.where(valid[None], picked, jnp.zeros((), filt.dtype))


def block_conv(table, extended, blocks, group):
    span = table.shape[1]
    chans = extended.shape[1]
    first = extended[: blocks * span].reshape(blocks, span, chans // group, group)
    second = extended[span : (blocks + 1) * span].reshape(blocks, span, chans // group, group)
    total = jnp.einsum(
        "gij,bjgc->bigc", table[:, :, :span], first, preferred_element_type=jnp.float32
    )
    total = total + jnp.einsum(
        "gij,bjgc->bigc", table[:, :, span:], second, preferred_element_type=jnp.float32
    )
    return total.reshape(blocks * span, chans)


def rounded_term(values):
    return lax.optimization_barrier(values.astype(jnp.bfloat16)).astype(jnp.float32)


def local(inputs, short_filter, long_filter, out_weight, out_cotangent):
    count = inputs.shape[0]
    chans = inputs.shape[2]
    groups = long_filter.shape[0]
    span = long_filter.shape[1]
    lags = short_filter.shape[0]
    group = chans // groups
    blocks = count // span
    tokens_all = count * lax.axis_size("ctx")
    signal = inputs.astype(jnp.float32)
    zero_rows = jnp.zeros((lags - 1, 3, chans), jnp.float32)
    local_feat = short_conv(jnp.concatenate([zero_rows, signal], axis=0), short_filter, count)
    tail_gated = (local_feat[count - (span - 1) :, 1] * local_feat[count - (span - 1) :, 2]).astype(
        jnp.bfloat16
    )
    tail_inputs = inputs[count - (lags - 1) :].reshape(3 * (lags - 1), chans)
    sent = jnp.concatenate([tail_gated, tail_inputs], axis=0)
    taken = shifted(sent, "ctx", 1)
    gated_rim = taken[: span - 1]
    input_rim = taken[span - 1 :].reshape(lags - 1, 3, chans).astype(jnp.float32)
    signal_ext = jnp.concatenate([input_rim, signal], axis=0)
    feat = short_conv(signal_ext, short_filter, count)
    query, keyed, valued = (feat[:, 0], feat[:, 1], feat[:, 2])
    gated = (keyed * valued).astype(jnp.bfloat16)
    gated_ext = jnp.concatenate([jnp.zeros((1, chans), jnp.bfloat16), gated_rim, gated], axis=0)
    forward_table = tap_table(long_filter, True)
    mixed = block_conv(forward_table, gated_ext, blocks, group)
    gate_out = (query * mixed).astype(jnp.bfloat16)
    partial_value = rounded_term(jnp.dot(gate_out, out_weight, preferred_element_type=jnp.float32))
    result = lax.psum(partial_value.astype(jnp.bfloat16), "tp")
    grad_gate = lax.dot_general(
        out_cotangent, out_weight, (((1,), (1,)), ((), ())), preferred_element_type=jnp.float32
    )
    grad_mixed = (grad_gate * query).astype(jnp.bfloat16)
    grad_query = grad_gate * mixed
    backward_table = tap_table(long_filter, False)
    head_gated = block_conv(backward_table, grad_mixed, 1, group)[: lags - 1]
    head_feat = jnp.stack(
        [grad_query[: lags - 1], head_gated * valued[: lags - 1], head_gated * keyed[: lags - 1]],
        axis=1,
    ).astype(jnp.bfloat16)
    sent_back = jnp.concatenate(
        [grad_mixed[: span - 1], head_feat.reshape(3 * (lags - 1), chans)], axis=0
    )
    taken_back = shifted(sent_back, "ctx", -1)
    mixed_rim = taken_back[: span - 1]
    feat_rim = taken_back[span - 1 :].reshape(lags - 1, 3, chans)
    mixed_ext = jnp.concatenate(
        [grad_mixed, mixed_rim, jnp.zeros((1, chans), jnp.bfloat16)], axis=0
    )
    grad_gated = block_conv(backward_table, mixed_ext, blocks, group)
    grad_feat = jnp.stack([grad_query, grad_gated * valued, grad_gated * keyed], axis=1).astype(
        jnp.bfloat16
    )
    grad_feat_ext = lax.optimization_barrier(jnp.concatenate([grad_feat, feat_rim], axis=0)).astype(
        jnp.float32
    )
    grad_in = short_filter[0] * grad_feat_ext[:count]
    for lag in range(1, lags):
        grad_in = grad_in + short_filter[lag] * grad_feat_ext[lag : lag + count]
    grad_feat32 = grad_feat_ext[:count]
    short_rows = [
        jnp.sum(grad_feat32 * signal_ext[lags - 1 - lag : lags - 1 - lag + count], axis=0)
        for lag in range(lags)
    ]
    short_local = jnp.stack(short_rows, axis=0)
    mixed_blocks = grad_mixed.reshape(blocks, span, groups, group)
    earlier = gated_ext[:count].reshape(blocks, span, groups, group)
    current = gated_ext[span:].reshape(blocks, span, groups, group)
    products = jnp.concatenate(
        [
            jnp.einsum("bigc,bjgc->gij", mixed_blocks, earlier, preferred_element_type=jnp.float32),
            jnp.einsum("bigc,bjgc->gij", mixed_blocks, current, preferred_element_type=jnp.float32),
        ],
        axis=2,
    )
    flipped = products[:, :, ::-1].reshape(groups, 2 * span * span)
    skewed = flipped[:, span - 1 : span - 1 + span * (2 * span - 1)].reshape(
        groups, span, 2 * span - 1
    )[:, :, :span]
    long_local = jnp.sum(skewed, axis=1)
    long_total, short_total = lax.psum((long_local, short_local), "ctx")
    grad_short = short_total * float(tokens_all) ** (-0.5)
    grad_long = long_total * float(tokens_all * group) ** (-0.5)
    return (result, grad_in.astype(jnp.bfloat16), grad_short, grad_long)


def solution(mesh):
    in_specs = (
        P("ctx", None, "tp"),
        P(None, None, "tp"),
        P("tp", None),
        P("tp", None),
        P("ctx", None),
    )
    out_specs = (P("ctx", None), P("ctx", None, "tp"), P(None, None, "tp"), P("tp", None))
    return jax.shard_map(local, mesh=mesh, in_specs=in_specs, out_specs=out_specs, check_vma=False)
```

profile of v0, /device:TPU:25, one launch (start us, length us, event | category | flops | bytes accessed | tf_op | source)
XLA Modules:
  0.0 582.2 jit_solution(4579067291675489319)
XLA Ops:
  7.2 3.6 convert_element_type.48
  10.8 0.8 slice.132
  11.7 5.0 multiply_add_fusion.1
  16.7 0.1 fusion.39
  16.9 3.1 collective-permute-start
  20.2 0.1 copy.30
  20.4 115.0 %gather_fusion = bf16[32768,64]{1,0:T(8,128)(2,1)} fusion(bf16[64,128]{0,1:T(8,128)(2,1)S(1)} %copy.30, s32[32768]{0:T(1024)S(1)} %broadcast_clamp_fusion.1), kind=kCustom, calls=%fused_computation | custom fusion | bytes 8519680 | tf_op jit(solution)/shard_map/gather | solution.py:27
  135.4 10.1 %copy.63 = bf16[128,256,64]{1,0,2:T(8,128)(2,1)} copy(bf16[128,256,64]{2,1,0:T(8,128)(2,1)} %bitcast.111) | data formatting | bytes 8388608 | tf_op jit(solution)/shard_map/gather | solution.py:27
  145.6 115.0 %gather_fusion.1 = bf16[32768,64]{1,0:T(8,128)(2,1)} fusion(bf16[64,128]{0,1:T(8,128)(2,1)S(1)} %copy.30, s32[32768]{0:T(1024)S(1)} %broadcast_clamp_fusion), kind=kCustom, calls=%fused_computation.1 | custom fusion | bytes 8519680 | tf_op jit(solution)/shard_map/gather | solution.py:27
  260.6 10.1 %copy.64 = bf16[128,256,64]{1,0,2:T(8,128)(2,1)} copy(bf16[128,256,64]{2,1,0:T(8,128)(2,1)} %bitcast.110) | data formatting | bytes 8388608 | tf_op jit(solution)/shard_map/gather | solution.py:27
  270.6 4.6 select_bitcast_fusion.1
  275.2 2.2 select_bitcast_fusion
  277.5 5.0 multiply_add_fusion
  282.5 0.1 multiply_convert_fusion.5
  282.6 1.6 copy-done.3
  284.2 0.1 fusion.56
  284.3 1.0 copy.33
  285.3 1.2 convert_element_type.55
  286.5 0.9 pad_maximum_fusion.5
  287.4 2.0 copy.29
  289.5 1.2 reshape.165
  290.6 3.0 fusion.4
  293.6 2.8 fusion.23
  296.4 0.6 copy.35
  297.0 1.0 copy.88
  298.0 2.5 copy.36
  300.5 7.1 %multiply_convert_fusion.3 = (bf16[256,1024]{1,0:T(8,128)(2,1)}, bf16[256,1024]{1,0:T(8,128)(2,1)S(1)}) fusion(f32[256,1024]{1,0:T(8,128)} %copy.36, f32[256,3,1024]{2,0,1:T(8,128)} %copy-done.3, bf16[256,4096]{1,0:T(8,128)(2,1)S(1)} %copy-done, bf16[1024,4096]{1,0:T(8,128)(2,1)} %param.8), kind=kOutput, calls=%fused_computation.49 | convolution fusion | flops 2148532224 | bytes 13631488 | tf_op jit(solution)/shard_map/dot_general | solution.py:79
  307.7 0.2 copy.38
  307.9 0.1 reshape.167
  308.1 2.7 convolution_bitcast_fusion
  310.8 2.7 convolution_bitcast_fusion.1
  313.5 0.2 copy.43
  313.7 0.2 copy.42
  313.8 2.8 fusion.11
  316.7 2.8 fusion.27
  319.5 0.2 copy.65
  319.7 0.8 fusion.49
  320.6 3.1 collective-permute-start.1
  323.7 7.7 %pad_maximum_fusion = f32[64,128,256]{1,2,0:T(8,128)} fusion(f32[64,128,128]{1,2,0:T(8,128)} %convolution_bitcast_fusion, f32[64,128,128]{1,2,0:T(8,128)} %convolution_bitcast_fusion.1), kind=kLoop, calls=%fused_computation.2 | loop fusion | flops 2097152 | bytes 16777216 | tf_op jit(solution)/shard_map/concatenate | solution.py:118
  331.4 63.8 %rev.3 = f32[64,128,256]{1,2,0:T(8,128)} reverse(f32[64,128,256]{1,2,0:T(8,128)} %pad_maximum_fusion), dimensions={2} | reverse | bytes 16777216 | tf_op jit(solution)/shard_map/rev | solution.py:125
  395.2 9.2 %copy.69 = f32[8,8,128,256]{3,1,2,0:T(8,128)} copy(f32[8,8,128,256]{2,3,1,0:T(8,128)} %bitcast.108) | data formatting | bytes 16777216
  404.4 8.8 %slice.190 = f32[64,32640]{1,0:T(8,128)} slice(f32[64,32768]{1,0:T(8,128)} %bitcast.109), slice={[0:64], [127:32767]} | slice | bytes 16711680 | tf_op jit(solution)/shard_map/slice | solution.py:126
  413.2 15.9 %reshape.174 = f32[64,128,255]{2,1,0:T(8,128)} reshape(f32[64,32640]{1,0:T(8,128)} %slice.190) | data formatting | bytes 16711680 | tf_op jit(solution)/shard_map/reshape | solution.py:126
  429.1 3.3 slice_reduce_fusion
  432.5 0.2 copy.46
  432.8 0.1 reshape.170
  432.9 2.8 fusion.6
  435.7 2.8 fusion.19
  438.5 0.6 copy.48
  439.0 0.8 reshape.171
  439.9 0.3 copy.49
  440.2 1.9 multiply_convert_fusion.1
  442.1 0.1 pad_maximum_fusion.2
  442.3 0.4 convert_element_type.60
  442.7 1.5 copy-done.2
  444.2 0.5 copy-done.5
  444.6 3.1 multiply_reduce_fusion.1
  447.7 0.6 pad_maximum_fusion.9
  448.5 7.4 %convolution_convert_fusion = bf16[256,4096]{1,0:T(8,128)(2,1)} fusion(bf16[1024,4096]{1,0:T(8,128)(2,1)} %param.8, f32[256,1024]{1,0:T(8,128)S(1)} %copy-done.8, f32[256,3,1024]{2,0,1:T(8,128)} %copy-done.3), kind=kOutput, calls=%fused_computation.3 | convolution fusion | flops 2149056512 | bytes 12582912 | tf_op jit(solution)/shard_map/dot_general | solution.py:77
  455.9 59.3 %all-reduce.7.cloned.1.call-done = (f32[3,3,1024]{2,1,0:T(4,128)}, f32[64,128]{1,0:T(8,128)}) async-done(((f32[3,3,1024]{2,1,0:T(4,128)}, f32[64,128]{1,0:T(8,128)}), (f32[3,3,1024]{2,1,0:T(4,128)}, f32[64,128]{1,0:T(8,128)})) %all-reduce.7.cloned.1.call-update) | async-done | bytes 69648 | tf_op jit(solution)/shard_map/psum | solution.py:130
  515.2 1.4 broadcast_multiply_fusion.1
  516.5 1.4 broadcast_multiply_fusion
  518.0 54.3 %all-reduce.5.cloned.1.call-done = bf16[256,4096]{1,0:T(8,128)(2,1)} async-done(((bf16[256,4096]{1,0:T(8,128)(2,1)}), bf16[256,4096]{1,0:T(8,128)(2,1)}) %all-reduce.5.cloned.1.call-update) | async-done | bytes 2097168 | tf_op jit(solution)/shard_map/psum | solution.py:78
  572.2 3.1 copy.92
  (56 shorter events, 0.9 us)
Async XLA Ops:
  7.2 293.4 %copy-start = (bf16[256,4096]{1,0:T(8,128)(2,1)S(1)}, bf16[256,4096]{1,0:T(8,128)(2,1)}, u32[]{:S(2)}) copy-start(bf16[256,4096]{1,0:T(8,128)(2,1)} %param.9) | copy-start | bytes 6291460
  7.2 4.5 copy-start.10
  7.2 508.0 %all-reduce.7.cloned.1.call-start = ((), (), s32[]{:S(2)}) async-start(), calls=%async_computation.1 | async-start | bytes 163840 | tf_op jit(solution)/shard_map/psum | solution.py:130
  11.7 8.5 %copy-start.11 = (bf16[64,128]{1,0:T(8,128)(2,1)S(1)}, bf16[64,128]{1,0:T(8,128)(2,1)}, u32[]{:S(2)}) copy-start(bf16[64,128]{1,0:T(8,128)(2,1)} %param.7) | copy-start | bytes 49156
  16.9 260.6 %collective-permute-start = (bf16[133,1024]{1,0:T(8,128)(2,1)S(1)}, bf16[133,1024]{1,0:T(8,128)(2,1)S(1)}, u32[]{:S(2)}, u32[]{:S(2)}) collective-permute-start(bf16[133,1024]{1,0:T(8,128)(2,1)S(1)} %pad_maximum_fusion.7), channel_id=1, source_target_pairs={{0,4},{4,8},{8,12},{12,16},{16,20},{20,24},{24,28},{1,5},{5,9},{9,... | collective-permute-start | bytes 817160 | tf_op jit(solution)/shard_map/ppermute | solution.py:10
  270.6 4.6 copy-start.4
  282.5 1.7 copy-start.3
  290.6 5.8 copy-start.6
  307.9 2.9 copy-start.7
  313.8 6.6 %copy-start.9 = (bf16[256,1024]{1,0:T(8,128)(2,1)S(1)}, bf16[256,1024]{1,0:T(8,128)(2,1)}, u32[]{:S(2)}) copy-start(bf16[256,1024]{1,0:T(8,128)(2,1)} %get-tuple-element.14) | copy-start | bytes 1572868
  320.6 111.8 %collective-permute-start.1 = (bf16[133,1024]{1,0:T(8,128)(2,1)S(1)}, bf16[133,1024]{1,0:T(8,128)(2,1)S(1)}, u32[]{:S(2)}, u32[]{:S(2)}) collective-permute-start(bf16[133,1024]{1,0:T(8,128)(2,1)S(1)} %pad_maximum_fusion.8), channel_id=1, source_target_pairs={{4,0},{8,4},{12,8},{16,12},{20,16},{24,20},{28,24},{5,1},{9,5},{13... | collective-permute-start | bytes 817160 | tf_op jit(solution)/shard_map/ppermute | solution.py:10
  442.3 1.9 copy-start.2
  442.3 2.3 copy-start.5
  444.6 3.8 copy-start.8
  448.4 123.8 %all-reduce.5.cloned.1.call-start = ((), (), s32[]{:S(2)}) async-start(), calls=%async_computation | async-start | bytes 4194304 | tf_op jit(solution)/shard_map/psum | solution.py:78
  455.8 119.5 %copy-start.1 = (bf16[256,4096]{1,0:T(8,128)(2,1)S(1)}, bf16[256,4096]{1,0:T(8,128)(2,1)}, u32[]{:S(2)}) copy-start(bf16[256,4096]{1,0:T(8,128)(2,1)} %param.9) | copy-start | bytes 6291460
Sparse Core Ops, SparseCore 0:
  448.5 66.5 all-reduce.6
  518.1 54.0 all-reduce.4
where the time goes:
time: 590 us; the launch traced here: 582 us
  local copies, waits for them, and re-layouts  368 us (62%)
  waiting for transfers between devices  114 us (19%)
  other arithmetic  42.7 us (7%)
  matrix products  36.9 us (6%)
  between operations  14.5 us (2%)
  starting transfers between devices  6.26 us (1%)
    gather x4, local copies, waits for them, and re-layouts, tap_table(): picked = filt[:, jnp.clip(offset, 0, span - 1)]  250 us
    rev x1, local copies, waits for them, and re-layouts, local(): flipped = products[:, :, ::-1].reshape(groups, 2 * span * span)  63.8 us
    psum x1, waiting for transfers between devices, local(): long_total, short_total = lax.psum((long_local, short_local), 'ctx')  59.3 us
    psum x1, waiting for transfers between devices, local(): result = lax.psum(partial_value.astype(jnp.bfloat16), 'tp')  54.3 us
    unnamed x30, local copies, waits for them, and re-layouts  17.1 us
    reshape x1, local copies, waits for them, and re-layouts, local(): flipped[:, span - 1:span - 1 + span * (2 * span - 1)]  15.9 us
  transfers between devices with their start and end apart: 4, of which 2 were waited for; matrix products, arithmetic and copies ran while one was open for 65% of the time, Pallas kernels for 0%

commit v1 on v0

v1 whole, which is shorter than its diff:
```python
import functools

import jax
import jax.numpy as jnp
from jax import lax
from jax.experimental import pallas as pl
from jax.experimental.pallas import tpu as pltpu
from jax.sharding import PartitionSpec as P

LANES = 128
F32 = jnp.float32
BF16 = jnp.bfloat16
VMEM_LIMIT = 56 * 1024 * 1024


def pairwise(axis, step):
    return [(source, source ^ step) for source in range(lax.axis_size(axis))]


def shifted(value, axis, steps):
    count = lax.axis_size(axis)
    initial, last = (max(0, -steps), min(count, count - steps))
    return lax.ppermute(value, axis, [(source, source + steps) for source in range(initial, last)])


def params():
    return pltpu.CompilerParams(vmem_limit_bytes=VMEM_LIMIT)


def fill_signal(x_ref, ext_ref, rim_ref, row):
    rows = x_ref.shape[1]
    for part in range(3):
        if rim_ref is None:
            ext_ref[part, 0:8, :] = jnp.zeros((8, LANES), F32)
        else:
            ext_ref[part, 6:8, :] = rim_ref[row + 2 * part : row + 2 * part + 2, :].astype(F32)
        ext_ref[part, 8 : 8 + rows, :] = x_ref[part].astype(F32)


def features(ext_ref, taps_ref, part, start, rows):
    total = taps_ref[0, part : part + 1, :] * ext_ref[part, 8 + start : 8 + start + rows, :]
    for lag in range(1, 3):
        first = 8 + start - lag
        total = total + taps_ref[lag, part : part + 1, :] * ext_ref[part, first : first + rows, :]
    return total


def group_of_lane(rows, group):
    return lax.broadcasted_iota(jnp.int32, (rows, LANES), 1) // group


def reversal():
    source = lax.broadcasted_iota(jnp.int32, (LANES, LANES), 0)
    target = lax.broadcasted_iota(jnp.int32, (LANES, LANES), 1)
    return ((source + target) % LANES == 0)


def fill_table(table_ref, taps, forward):
    row = lax.broadcasted_iota(jnp.int32, (LANES, LANES), 0)
    col = lax.broadcasted_iota(jnp.int32, (LANES, LANES), 1)
    early = (col > row) if forward else (col >= row)
    for g in range(taps.shape[0]):
        wide = jnp.broadcast_to(taps[g : g + 1, :], (LANES, LANES))
        ring = pltpu.roll(wide, 0, 1, stride=1, stride_axis=0)
        table_ref[g * LANES : (g + 1) * LANES, 0:LANES] = jnp.where(early, ring, 0.0).astype(BF16)
        table_ref[g * LANES : (g + 1) * LANES, LANES:] = jnp.where(early, 0.0, ring).astype(BF16)


def pick_groups(wide, group, blocks):
    count = LANES // group
    lane = group_of_lane(LANES, group)
    outs = []
    for b in range(blocks):
        total = wide[0:LANES, b * LANES : (b + 1) * LANES]
        for g in range(1, count):
            total = jnp.where(
                lane == g, wide[g * LANES : (g + 1) * LANES, b * LANES : (b + 1) * LANES], total
            )
        outs.append(total)
    return jnp.concatenate(outs, axis=0)


def tail_kernel(x_ref, taps_ref, sent_ref, ext):
    rows = x_ref.shape[1]
    fill_signal(x_ref, ext, None, 0)
    start = rows - LANES
    keyed = features(ext, taps_ref, 1, start, LANES)
    valued = features(ext, taps_ref, 2, start, LANES)
    sent_ref[0:LANES, :] = (keyed * valued).astype(BF16)
    rim = [ext[part, 8 + rows - 2 : 8 + rows, :] for part in range(3)]
    rim.append(jnp.zeros((10, LANES), F32))
    sent_ref[LANES:, :] = jnp.concatenate(rim, axis=0).astype(BF16)


def forward_kernel(
    group, x_ref, taps_ref, filt_ref, halo_ref, gg_ref, gate_ref, gm_ref, gq_ref, back_ref, ext, gext, table
):
    rows = x_ref.shape[1]
    blocks = rows // LANES
    fill_signal(x_ref, ext, halo_ref, LANES)
    query = features(ext, taps_ref, 0, 0, rows)
    keyed = features(ext, taps_ref, 1, 0, rows)
    valued = features(ext, taps_ref, 2, 0, rows)
    gext[0:LANES, :] = halo_ref[0:LANES, :]
    gext[LANES:, :] = (keyed * valued).astype(BF16)
    filt = filt_ref[...]
    backward = jnp.dot(filt, reversal().astype(BF16), preferred_element_type=F32)
    fill_table(table, backward, True)
    stacked = jnp.concatenate(
        [gext[b * LANES : (b + 2) * LANES, :] for b in range(blocks)], axis=1
    )
    wide = jnp.dot(table[...], stacked, preferred_element_type=F32)
    mixed = pick_groups(wide, group, blocks)
    gate_ref[...] = (query * mixed).astype(BF16)
    grad_gate = gg_ref[...]
    grad_mixed = (grad_gate * query).astype(BF16)
    gm_ref[...] = grad_mixed
    grad_query = (grad_gate * mixed).astype(BF16)
    gq_ref[...] = grad_query
    count = LANES // group
    owner = (
        lax.broadcasted_iota(jnp.int32, (count, LANES), 1) // group
        == lax.broadcasted_iota(jnp.int32, (count, LANES), 0)
    ).astype(BF16)
    spread = lax.dot_general(
        filt, owner, (((0,), (0,)), ((), ())), preferred_element_type=F32
    )
    gm32 = grad_mixed.astype(F32)
    heads = [
        jnp.sum(spread * gm32[t : t + LANES], axis=0, keepdims=True) for t in range(2)
    ]
    head = jnp.concatenate(heads, axis=0)
    back_ref[0:LANES, :] = grad_mixed[0:LANES]
    back_ref[LANES:, :] = jnp.concatenate(
        [
            grad_query[0:2].astype(F32),
            head * valued[0:2],
            head * keyed[0:2],
            jnp.zeros((10, LANES), F32),
        ],
        axis=0,
    ).astype(BF16)


def backward_kernel(
    group, x_ref, taps_ref, filt_ref, halo_ref, gm_ref, gq_ref, back_ref,
    gin_ref, sums_ref, ext, gext, mext, gf, table, left,
):
    rows = x_ref.shape[1]
    blocks = rows // LANES
    count = LANES // group
    fill_signal(x_ref, ext, halo_ref, LANES)
    keyed = features(ext, taps_ref, 1, 0, rows)
    valued = features(ext, taps_ref, 2, 0, rows)
    gext[0:LANES, :] = halo_ref[0:LANES, :]
    gext[LANES:, :] = (keyed * valued).astype(BF16)
    mext[0:rows, :] = gm_ref[...]
    mext[rows:, :] = back_ref[0:LANES, :]
    fill_table(table, filt_ref[...].astype(F32), False)
    stacked = jnp.concatenate(
        [mext[b * LANES : (b + 2) * LANES, :] for b in range(blocks)], axis=1
    )
    wide = jnp.dot(table[...], stacked, preferred_element_type=F32)
    grad_gated = pick_groups(wide, group, blocks)
    parts = (
        gq_ref[...].astype(F32),
        (grad_gated * valued).astype(BF16).astype(F32),
        (grad_gated * keyed).astype(BF16).astype(F32),
    )
    short_rows = [[None] * 3 for _ in range(3)]
    for part in range(3):
        gf[part, 0:rows, :] = parts[part]
        gf[part, rows : rows + 2, :] = back_ref[
            LANES + 2 * part : LANES + 2 * part + 2, :
        ].astype(F32)
        total = taps_ref[0, part : part + 1, :] * parts[part]
        for lag in range(1, 3):
            total = total + taps_ref[lag, part : part + 1, :] * gf[part, lag : lag + rows, :]
        gin_ref[part] = total.astype(BF16)
        for lag in range(3):
            short_rows[lag][part] = jnp.sum(
                parts[part] * ext[part, 8 - lag : 8 - lag + rows, :], axis=0, keepdims=True
            )
    lane = group_of_lane(LANES, group)
    for g in range(count):
        own = lane == g
        for b in range(blocks):
            left[g * LANES : (g + 1) * LANES, b * LANES : (b + 1) * LANES] = jnp.where(
                own, gm_ref[b * LANES : (b + 1) * LANES, :], jnp.zeros((), BF16)
            )
    row = lax.broadcasted_iota(jnp.int32, (LANES, LANES), 0)
    col = lax.broadcasted_iota(jnp.int32, (LANES, LANES), 1)
    upside = jnp.concatenate([gext[b * LANES : (b + 1) * LANES, :] for b in range(blocks + 1)], axis=1)
    upside = jnp.dot(
        (row + col == LANES - 1).astype(BF16), upside, preferred_element_type=F32
    ).astype(BF16)
    right = jnp.concatenate([upside[:, 0 : blocks * LANES], upside[:, LANES:]], axis=0)
    products = lax.dot_general(
        left[...], right, (((1,), (1,)), ((), ())), preferred_element_type=F32
    )
    early = row + col < LANES - 1
    lag_rows = []
    for g in range(count):
        own = products[g * LANES : (g + 1) * LANES, :]
        ring = jnp.where(early, own[:, 0:LANES], own[:, LANES:])
        ring = pltpu.roll(ring, 0, 1, stride=1, stride_axis=0)
        lag_rows.append(jnp.sum(ring, axis=0, keepdims=True))
    sums_ref[0:8, :] = pltpu.roll(jnp.concatenate(lag_rows, axis=0), 1, 1)
    flat = [short_rows[lag][part] for lag in range(3) for part in range(3)]
    flat.append(jnp.zeros((7, LANES), F32))
    sums_ref[8:24, :] = jnp.concatenate(flat, axis=0)


def unpack_kernel(short_scale, long_scale, a_ref, b_ref, short_ref, long_ref):
    total = a_ref[...] + b_ref[...]
    long_ref[...] = total[0:8] * long_scale
    for lag in range(3):
        for part in range(3):
            at = 8 + 3 * lag + part
            short_ref[lag, part : part + 1, :] = total[at : at + 1] * short_scale


def cot_kernel(c_ref, w_ref, o_ref):
    o_ref[...] = lax.dot_general(
        c_ref[...], w_ref[...], (((1,), (1,)), ((), ())), preferred_element_type=F32
    )


def half_kernel(which_ref, g_ref, w_ref, o_ref):
    o_ref[...] = jnp.dot(g_ref[...], w_ref[...], preferred_element_type=F32).astype(BF16)


def grad_gate_of(cotangent, weight):
    rows, width = cotangent.shape
    chans = weight.shape[0]
    step = min(256, chans)
    return pl.pallas_call(
        cot_kernel,
        out_shape=jax.ShapeDtypeStruct((rows, chans), F32),
        grid=(chans // step,),
        in_specs=[
            pl.BlockSpec((rows, width), lambda j: (0, 0)),
            pl.BlockSpec((step, width), lambda j: (j, 0)),
        ],
        out_specs=pl.BlockSpec((rows, step), lambda j: (0, j)),
        compiler_params=params(),
        name="grad_gate",
    )(cotangent, weight)


def half_product(which, gate, weight):
    rows, chans = gate.shape
    half = weight.shape[1] // 2
    step = 512
    tiles = half // step
    return pl.pallas_call(
        half_kernel,
        out_shape=jax.ShapeDtypeStruct((rows, half), BF16),
        grid_spec=pltpu.PrefetchScalarGridSpec(
            num_scalar_prefetch=1,
            grid=(tiles,),
            in_specs=[
                pl.BlockSpec((rows, chans), lambda j, which: (0, 0)),
                pl.BlockSpec((chans, step), lambda j, which: (0, which[0] * tiles + j)),
            ],
            out_specs=pl.BlockSpec((rows, step), lambda j, which: (0, j)),
        ),
        compiler_params=params(),
        name="half_product",
    )(which, gate, weight)


def local(inputs, short_filter, long_filter, out_weight, out_cotangent):
    rows, _, chans = inputs.shape
    groups, span = long_filter.shape
    group = chans // groups
    count = LANES // group
    tiles = chans // LANES
    tokens_all = rows * lax.axis_size("ctx")
    n_tp = lax.axis_size("tp")
    signal = inputs.transpose(1, 0, 2)
    rim_rows = LANES + 16

    x_spec = pl.BlockSpec((3, rows, LANES), lambda j: (0, 0, j))
    taps_spec = pl.BlockSpec((3, 3, LANES), lambda j: (0, 0, j))
    filt_spec = pl.BlockSpec((count, LANES), lambda j: (j, 0))
    rim_spec = pl.BlockSpec((rim_rows, LANES), lambda j: (0, j))
    full_spec = pl.BlockSpec((rows, LANES), lambda j: (0, j))
    ext_scratch = pltpu.VMEM((3, rows + 8, LANES), F32)

    sent = pl.pallas_call(
        tail_kernel,
        out_shape=jax.ShapeDtypeStruct((rim_rows, chans), BF16),
        grid=(tiles,),
        in_specs=[x_spec, taps_spec],
        out_specs=rim_spec,
        scratch_shapes=[ext_scratch],
        compiler_params=params(),
        name="tail",
    )(signal, short_filter)
    halo = shifted(sent, "ctx", 1)
    grad_gate = grad_gate_of(out_cotangent, out_weight)
    rows_bf16 = jax.ShapeDtypeStruct((rows, chans), BF16)
    gate_out, grad_mixed, grad_query, sent_back = pl.pallas_call(
        functools.partial(forward_kernel, group),
        out_shape=(rows_bf16, rows_bf16, rows_bf16, jax.ShapeDtypeStruct((rim_rows, chans), BF16)),
        grid=(tiles,),
        in_specs=[x_spec, taps_spec, filt_spec, rim_spec, full_spec],
        out_specs=(full_spec, full_spec, full_spec, rim_spec),
        scratch_shapes=[
            ext_scratch,
            pltpu.VMEM((rows + LANES, LANES), BF16),
            pltpu.VMEM((count * LANES, 2 * LANES), BF16),
        ],
        compiler_params=params(),
        name="forward",
    )(signal, short_filter, long_filter, halo, grad_gate)

    me = lax.axis_index("tp")
    core = lax.rem(me, 2)
    other = half_product(jnp.reshape(1 - core, (1,)), gate_out, out_weight)
    theirs = lax.ppermute(other, "tp", pairwise("tp", 1))
    mine = half_product(jnp.reshape(core, (1,)), gate_out, out_weight)
    mine = (mine.astype(F32) + theirs.astype(F32)).astype(BF16)
    step = 2
    while step < n_tp:
        got = lax.ppermute(mine, "tp", pairwise("tp", step))
        mine = (mine.astype(F32) + got.astype(F32)).astype(BF16)
        step *= 2
    sibling = lax.ppermute(mine, "tp", pairwise("tp", 1))
    result = jnp.where(
        core == 0,
        jnp.concatenate([mine, sibling], axis=1),
        jnp.concatenate([sibling, mine], axis=1),
    )

    back = shifted(sent_back, "ctx", -1)
    grad_in, sums = pl.pallas_call(
        functools.partial(backward_kernel, group),
        out_shape=(
            jax.ShapeDtypeStruct((3, rows, chans), BF16),
            jax.ShapeDtypeStruct((24, chans), F32),
        ),
        grid=(tiles,),
        in_specs=[x_spec, taps_spec, filt_spec, rim_spec, full_spec, full_spec, rim_spec],
        out_specs=(x_spec, pl.BlockSpec((24, LANES), lambda j: (0, j))),
        scratch_shapes=[
            ext_scratch,
            pltpu.VMEM((rows + LANES, LANES), BF16),
            pltpu.VMEM((rows + LANES, LANES), BF16),
            pltpu.VMEM((3, rows + 8, LANES), F32),
            pltpu.VMEM((count * LANES, 2 * LANES), BF16),
            pltpu.VMEM((count * LANES, (rows // LANES) * LANES), BF16),
        ],
        compiler_params=params(),
        name="backward",
    )(signal, short_filter, long_filter, halo, grad_mixed, grad_query, back)

    n_ctx = lax.axis_size("ctx")
    if n_ctx & (n_ctx - 1) == 0:
        hop = 1
        got = jnp.zeros_like(sums)
        while hop < n_ctx:
            got = lax.ppermute(sums, "ctx", pairwise("ctx", hop))
            hop *= 2
            if hop < n_ctx:
                sums = sums + got
    else:
        sums = lax.psum(sums, "ctx")
        got = jnp.zeros_like(sums)
    sums_spec = pl.BlockSpec((24, LANES), lambda j: (0, j))
    grad_short, grad_long = pl.pallas_call(
        functools.partial(
            unpack_kernel, float(tokens_all) ** (-0.5), float(tokens_all * group) ** (-0.5)
        ),
        out_shape=(
            jax.ShapeDtypeStruct((3, 3, chans), F32),
            jax.ShapeDtypeStruct((groups, span), F32),
        ),
        grid=(tiles,),
        in_specs=[sums_spec, sums_spec],
        out_specs=(taps_spec, filt_spec),
        compiler_params=params(),
        name="unpack",
    )(sums, got)
    return (result, grad_in.transpose(1, 0, 2), grad_short, grad_long)


def solution(mesh):
    in_specs = (
        P("ctx", None, "tp"),
        P(None, None, "tp"),
        P("tp", None),
        P("tp", None),
        P("ctx", None),
    )
    out_specs = (P("ctx", None), P("ctx", None, "tp"), P(None, None, "tp"), P("tp", None))
    return jax.shard_map(local, mesh=mesh, in_specs=in_specs, out_specs=out_specs, check_vma=False)
```

time: 590 us -> 111 us (0.19)
  the two profiles are of different devices: /device:TPU:25 before, /device:TPU:0 now
where the time goes in v1:
time: 111 us; the launch traced here: 109 us
  Pallas kernels  43.7 us (39%)
  waiting for transfers between devices  42.2 us (38%)
  starting transfers between devices  15.7 us (14%)
  other arithmetic  5.04 us (5%)
  local copies, waits for them, and re-layouts  2.08 us (2%)
    ppermute x1, waiting for transfers between devices, local(): got = lax.ppermute(mine, 'tp', pairwise('tp', step))  24 us
    ppermute x2, waiting for transfers between devices, shifted(): lax.ppermute(value, axis, [(source, source + steps) for source in range(i...  10.1 us
    pallas_call x2, Pallas kernels, half_product(): pl.pallas_call(half_kernel, out_shape=jax.ShapeDtypeStruct((rows, half),...  9.92 us
    pallas_call x1, Pallas kernels, local(): pl.pallas_call(functools.partial(backward_kernel, group), out_shape=(jax....  9.26 us
    pallas_call x1, Pallas kernels, local(): pl.pallas_call(functools.partial(forward_kernel, group), out_shape=(rows_...  8.16 us
    ppermute x3, waiting for transfers between devices, local(): got = lax.ppermute(sums, 'ctx', pairwise('ctx', hop))  8.05 us
    ppermute x3, starting transfers between devices, local(): got = lax.ppermute(sums, 'ctx', pairwise('ctx', hop))  7.88 us
    pallas_call x1, Pallas kernels, grad_gate_of(): pl.pallas_call(cot_kernel, out_shape=jax.ShapeDtypeStruct((rows, chans),...  7.04 us
  transfers between devices with their start and end apart: 8, of which 5 were waited for; matrix products, arithmetic and copies ran while one was open for 1% of the time, Pallas kernels for 23%

profile of v1, /device:TPU:0, one launch (start us, length us, event | category | flops | bytes accessed | tf_op | source)
XLA Modules:
  0.0 109.5 jit_solution(12685439161100053567)
XLA Ops:
  0.6 5.2 %tail.1 = bf16[144,1024]{1,0:T(8,128)(2,1)} custom-call(bf16[3,256,1024]{2,1,0:T(8,128)(2,1)} %bitcast.4, f32[3,3,1024]{2,1,0:T(4,128)} %taps_ref.5), custom_call_target="tpu_custom_call" | custom-call | tf_op jit(solution)/shard_map/tail/pallas_call | solution.py:291
  5.9 4.8 %collective-permute-start = (bf16[144,1024]{1,0:T(8,128)(2,1)}, bf16[144,1024]{1,0:T(8,128)(2,1)S(1)}, u32[]{:S(2)}, u32[]{:S(2)}) collective-permute-start(bf16[144,1024]{1,0:T(8,128)(2,1)} %tail.1), channel_id=1, source_target_pairs={{0,4},{4,8},{8,12},{12,16},{16,20},{20,24},{24,28},{1,5},{5,9},{9,... | collective-permute-start | bytes 884744 | tf_op jit(solution)/shard_map/ppermute | solution.py:23
  10.7 7.0 %grad_gate.1.gg_ref = f32[256,1024]{1,0:T(8,128)} custom-call(bf16[256,4096]{1,0:T(8,128)(2,1)} %c_ref.1, bf16[1024,4096]{1,0:T(8,128)(2,1)} %w_ref.5), custom_call_target="tpu_custom_call" | custom-call | tf_op jit(solution)/shard_map/grad_gate/pallas_call | solution.py:237
  17.8 0.0 collective-permute-done.halo_ref
  17.8 0.0 copy-start
  17.8 0.7 copy-done
  18.5 8.2 %forward.1 = (bf16[256,1024]{1,0:T(8,128)(2,1)}, bf16[256,1024]{1,0:T(8,128)(2,1)}, bf16[256,1024]{1,0:T(8,128)(2,1)}, bf16[144,1024]{1,0:T(8,128)(2,1)}) custom-call(bf16[3,256,1024]{2,1,0:T(8,128)(2,1)} %bitcast.5, f32[3,3,1024]{2,1,0:T(4,128)} %taps_ref.5, bf16[64,128]{1,0:T(8,128)(2,1)} %filt_ref.3, bf16[144,1024]{1,0:T(8,128)(2,1)} %copy-done, ...), custom_call_target="tpu_custom_call" | custom-call | tf_op jit(solution)/shard_map/forward/pallas_call | solution.py:304
  26.6 5.0 %half_product.3 = bf16[256,2048]{1,0:T(8,128)(2,1)} custom-call(s32[1]{0:T(128)} %bitcast.2.which_ref, bf16[256,1024]{1,0:T(8,128)(2,1)} %get-tuple-element.12.g_ref, bf16[1024,4096]{1,0:T(8,128)(2,1)} %w_ref.5), custom_call_target="tpu_custom_call" | custom-call | tf_op jit(solution)/shard_map/half_product/pallas_call | solution.py:256
  31.6 0.0 collective-permute-start.1
  31.6 5.0 %half_product.2 = bf16[256,2048]{1,0:T(8,128)(2,1)} custom-call(s32[1]{0:T(128)} %bitcast.which_ref, bf16[256,1024]{1,0:T(8,128)(2,1)} %get-tuple-element.12.g_ref, bf16[1024,4096]{1,0:T(8,128)(2,1)} %w_ref.5), custom_call_target="tpu_custom_call" | custom-call | tf_op jit(solution)/shard_map/half_product/pallas_call | solution.py:256
  36.6 0.0 collective-permute-done.1
  36.6 1.6 %add_convert_fusion.1 = bf16[256,2048]{1,0:T(8,128)(2,1)S(1)} fusion(bf16[256,2048]{1,0:T(8,128)(2,1)S(1)} %collective-permute-done.1, bf16[256,2048]{1,0:T(8,128)(2,1)} %half_product.2), kind=kLoop, calls=%fused_computation.2 | loop fusion | flops 2097152 | bytes 3145728 | tf_op jit(solution)/shard_map/convert_element_type | solution.py:324
  38.2 0.0 copy-start.4
  38.2 1.6 %collective-permute-start.2 = (bf16[256,2048]{1,0:T(8,128)(2,1)S(1)}, bf16[256,2048]{1,0:T(8,128)(2,1)S(1)}, u32[]{:S(2)}, u32[]{:S(2)}) collective-permute-start(bf16[256,2048]{1,0:T(8,128)(2,1)S(1)} %add_convert_fusion.1), channel_id=1, source_target_pairs={{0,2},{1,3},{2,0},{3,1},{4,6},{5,7},{6,4},{7,5},{8,10},{9,11},{10,... | collective-permute-start | bytes 3145736 | tf_op jit(solution)/shard_map/ppermute | solution.py:327
  39.8 24.0 %collective-permute-done.2 = bf16[256,2048]{1,0:T(8,128)(2,1)S(1)} collective-permute-done((bf16[256,2048]{1,0:T(8,128)(2,1)S(1)}, bf16[256,2048]{1,0:T(8,128)(2,1)S(1)}, u32[]{:S(2)}, u32[]{:S(2)}) %collective-permute-start.2) | collective-permute-done | bytes 1048608 | tf_op jit(solution)/shard_map/ppermute | solution.py:327
  63.8 0.4 add_convert_fusion
  64.2 0.1 collective-permute-start.3
  64.3 0.0 copy-done.4
  64.3 1.3 %collective-permute-start.4 = (bf16[144,1024]{1,0:T(8,128)(2,1)S(1)}, bf16[144,1024]{1,0:T(8,128)(2,1)S(1)}, u32[]{:S(2)}, u32[]{:S(2)}) collective-permute-start(bf16[144,1024]{1,0:T(8,128)(2,1)S(1)} %copy-done.4), channel_id=1, source_target_pairs={{4,0},{8,4},{12,8},{16,12},{20,16},{24,20},{28,24},{5,1},{9,5},{13... | collective-permute-start | bytes 884744 | tf_op jit(solution)/shard_map/ppermute | solution.py:23
  65.6 10.1 %collective-permute-done.4.back_ref = bf16[144,1024]{1,0:T(8,128)(2,1)S(1)} collective-permute-done((bf16[144,1024]{1,0:T(8,128)(2,1)S(1)}, bf16[144,1024]{1,0:T(8,128)(2,1)S(1)}, u32[]{:S(2)}, u32[]{:S(2)}) %collective-permute-start.4) | collective-permute-done | bytes 294944 | tf_op jit(solution)/shard_map/ppermute | solution.py:23
  75.7 0.0 copy-start.2
  75.7 0.7 copy-done.2
  76.4 9.3 %backward.1 = (bf16[3,256,1024]{2,1,0:T(8,128)(2,1)}, f32[24,1024]{1,0:T(8,128)}) custom-call(bf16[3,256,1024]{2,1,0:T(8,128)(2,1)} %bitcast.6, f32[3,3,1024]{2,1,0:T(4,128)} %taps_ref.5, bf16[64,128]{1,0:T(8,128)(2,1)} %filt_ref.3, bf16[144,1024]{1,0:T(8,128)(2,1)} %copy-done, bf16[256,1024]{1,0:T(8,128)(2,1)} %get-tuple-element.13.gm_ref, ...), custom_call_target="tpu_custom_call" | custom-call | tf_op jit(solution)/shard_map/backward/pallas_call | solution.py:338
  85.7 2.6 %collective-permute-start.5 = (f32[24,1024]{1,0:T(8,128)}, f32[24,1024]{1,0:T(8,128)S(1)}, u32[]{:S(2)}, u32[]{:S(2)}) collective-permute-start(f32[24,1024]{1,0:T(8,128)} %get-tuple-element.17), channel_id=1, source_target_pairs={{0,4},{4,0},{8,12},{12,8},{16,20},{20,16},{24,28},{28,24},{1,5},{5... | collective-permute-start | bytes 294920 | tf_op jit(solution)/shard_map/ppermute | solution.py:364
  88.3 2.9 %collective-permute-done.5 = f32[24,1024]{1,0:T(8,128)S(1)} collective-permute-done((f32[24,1024]{1,0:T(8,128)}, f32[24,1024]{1,0:T(8,128)S(1)}, u32[]{:S(2)}, u32[]{:S(2)}) %collective-permute-start.5) | collective-permute-done | bytes 98336 | tf_op jit(solution)/shard_map/ppermute | solution.py:364
  91.2 0.9 add.14
  92.1 2.1 %collective-permute-start.6 = (f32[24,1024]{1,0:T(8,128)S(1)}, f32[24,1024]{1,0:T(8,128)S(1)}, u32[]{:S(2)}, u32[]{:S(2)}) collective-permute-start(f32[24,1024]{1,0:T(8,128)S(1)} %add.14), channel_id=1, source_target_pairs={{0,8},{4,12},{8,0},{12,4},{16,24},{20,28},{24,16},{28,20},{1,9},{5... | collective-permute-start | bytes 294920 | tf_op jit(solution)/shard_map/ppermute | solution.py:364
  94.2 2.6 %collective-permute-done.6 = f32[24,1024]{1,0:T(8,128)S(1)} collective-permute-done((f32[24,1024]{1,0:T(8,128)S(1)}, f32[24,1024]{1,0:T(8,128)S(1)}, u32[]{:S(2)}, u32[]{:S(2)}) %collective-permute-start.6) | collective-permute-done | bytes 98336 | tf_op jit(solution)/shard_map/ppermute | solution.py:364
  96.8 0.0 copy-start.1
  96.9 3.1 %collective-permute-start.7 = (f32[24,1024]{1,0:T(8,128)S(1)}, f32[24,1024]{1,0:T(8,128)S(1)}, u32[]{:S(2)}, u32[]{:S(2)}) collective-permute-start(f32[24,1024]{1,0:T(8,128)S(1)} %add.15.a_ref), channel_id=1, source_target_pairs={{0,16},{4,20},{8,24},{12,28},{16,0},{20,4},{24,8},{28,12},{1,17},{... | collective-permute-start | bytes 294920 | tf_op jit(solution)/shard_map/ppermute | solution.py:364
  100.0 2.6 %collective-permute-done.7.b_ref = f32[24,1024]{1,0:T(8,128)S(1)} collective-permute-done((f32[24,1024]{1,0:T(8,128)S(1)}, f32[24,1024]{1,0:T(8,128)S(1)}, u32[]{:S(2)}, u32[]{:S(2)}) %collective-permute-start.7) | collective-permute-done | bytes 98336 | tf_op jit(solution)/shard_map/ppermute | solution.py:364
  102.6 0.0 copy-done.1
  102.6 0.0 copy-start.3
  102.6 0.6 copy-done.3
  103.2 4.1 %unpack.1 = (f32[3,3,1024]{2,1,0:T(4,128)}, f32[64,128]{1,0:T(8,128)}) custom-call(f32[24,1024]{1,0:T(8,128)} %copy-done.1, f32[24,1024]{1,0:T(8,128)} %copy-done.3), custom_call_target="tpu_custom_call" | custom-call | tf_op jit(solution)/shard_map/unpack/pallas_call | solution.py:372
  107.3 0.0 collective-permute-done.3
  107.3 2.1 %maximum_select_fusion = bf16[256,4096]{1,0:T(8,128)(2,1)} fusion(bf16[256,2048]{1,0:T(8,128)(2,1)S(1)} %collective-permute-done.3, bf16[256,2048]{1,0:T(8,128)(2,1)S(1)} %add_convert_fusion, pred[]{:T(512)S(6)} %eq.3), kind=kLoop, calls=%fused_computation | loop fusion | flops 9437184 | bytes 4194305 | tf_op jit(solution)/shard_map/jit(_where)/select_n | solution.py:331
  (1 shorter events, 0.0 us)
Async XLA Ops:
  5.9 11.9 %collective-permute-start = (bf16[144,1024]{1,0:T(8,128)(2,1)}, bf16[144,1024]{1,0:T(8,128)(2,1)S(1)}, u32[]{:S(2)}, u32[]{:S(2)}) collective-permute-start(bf16[144,1024]{1,0:T(8,128)(2,1)} %tail.1), channel_id=1, source_target_pairs={{0,4},{4,8},{8,12},{12,16},{16,20},{20,24},{24,28},{1,5},{5,9},{9,... | collective-permute-start | bytes 884744 | tf_op jit(solution)/shard_map/ppermute | solution.py:23
  17.8 0.7 copy-start
  31.6 5.0 %collective-permute-start.1 = (bf16[256,2048]{1,0:T(8,128)(2,1)}, bf16[256,2048]{1,0:T(8,128)(2,1)S(1)}, u32[]{:S(2)}, u32[]{:S(2)}) collective-permute-start(bf16[256,2048]{1,0:T(8,128)(2,1)} %half_product.3), channel_id=1, source_target_pairs={{0,1},{1,0},{2,3},{3,2},{4,5},{5,4},{6,7},{7,6},{8,9},{9,8},{10,11... | collective-permute-start | bytes 3145736 | tf_op jit(solution)/shard_map/ppermute | solution.py:322
  38.2 26.1 %copy-start.4 = (bf16[144,1024]{1,0:T(8,128)(2,1)S(1)}, bf16[144,1024]{1,0:T(8,128)(2,1)}, u32[]{:S(2)}) copy-start(bf16[144,1024]{1,0:T(8,128)(2,1)} %get-tuple-element.15) | copy-start | bytes 884740
  38.2 25.6 %collective-permute-start.2 = (bf16[256,2048]{1,0:T(8,128)(2,1)S(1)}, bf16[256,2048]{1,0:T(8,128)(2,1)S(1)}, u32[]{:S(2)}, u32[]{:S(2)}) collective-permute-start(bf16[256,2048]{1,0:T(8,128)(2,1)S(1)} %add_convert_fusion.1), channel_id=1, source_target_pairs={{0,2},{1,3},{2,0},{3,1},{4,6},{5,7},{6,4},{7,5},{8,10},{9,11},{10,... | collective-permute-start | bytes 3145736 | tf_op jit(solution)/shard_map/ppermute | solution.py:327
  64.2 43.1 %collective-permute-start.3 = (bf16[256,2048]{1,0:T(8,128)(2,1)S(1)}, bf16[256,2048]{1,0:T(8,128)(2,1)S(1)}, u32[]{:S(2)}, u32[]{:S(2)}) collective-permute-start(bf16[256,2048]{1,0:T(8,128)(2,1)S(1)} %add_convert_fusion), channel_id=1, source_target_pairs={{0,1},{1,0},{2,3},{3,2},{4,5},{5,4},{6,7},{7,6},{8,9},{9,8},{10,11... | collective-permute-start | bytes 3145736 | tf_op jit(solution)/shard_map/ppermute | solution.py:330
  64.3 11.4 %collective-permute-start.4 = (bf16[144,1024]{1,0:T(8,128)(2,1)S(1)}, bf16[144,1024]{1,0:T(8,128)(2,1)S(1)}, u32[]{:S(2)}, u32[]{:S(2)}) collective-permute-start(bf16[144,1024]{1,0:T(8,128)(2,1)S(1)} %copy-done.4), channel_id=1, source_target_pairs={{4,0},{8,4},{12,8},{16,12},{20,16},{24,20},{28,24},{5,1},{9,5},{13... | collective-permute-start | bytes 884744 | tf_op jit(solution)/shard_map/ppermute | solution.py:23
  75.7 0.7 copy-start.2
  85.7 5.5 %collective-permute-start.5 = (f32[24,1024]{1,0:T(8,128)}, f32[24,1024]{1,0:T(8,128)S(1)}, u32[]{:S(2)}, u32[]{:S(2)}) collective-permute-start(f32[24,1024]{1,0:T(8,128)} %get-tuple-element.17), channel_id=1, source_target_pairs={{0,4},{4,0},{8,12},{12,8},{16,20},{20,16},{24,28},{28,24},{1,5},{5... | collective-permute-start | bytes 294920 | tf_op jit(solution)/shard_map/ppermute | solution.py:364
  92.1 4.7 %collective-permute-start.6 = (f32[24,1024]{1,0:T(8,128)S(1)}, f32[24,1024]{1,0:T(8,128)S(1)}, u32[]{:S(2)}, u32[]{:S(2)}) collective-permute-start(f32[24,1024]{1,0:T(8,128)S(1)} %add.14), channel_id=1, source_target_pairs={{0,8},{4,12},{8,0},{12,4},{16,24},{20,28},{24,16},{28,20},{1,9},{5... | collective-permute-start | bytes 294920 | tf_op jit(solution)/shard_map/ppermute | solution.py:364
  96.8 5.7 %copy-start.1 = (f32[24,1024]{1,0:T(8,128)}, f32[24,1024]{1,0:T(8,128)S(1)}, u32[]{:S(2)}) copy-start(f32[24,1024]{1,0:T(8,128)S(1)} %add.15.a_ref) | copy-start | bytes 294916
  96.9 5.7 %collective-permute-start.7 = (f32[24,1024]{1,0:T(8,128)S(1)}, f32[24,1024]{1,0:T(8,128)S(1)}, u32[]{:S(2)}, u32[]{:S(2)}) collective-permute-start(f32[24,1024]{1,0:T(8,128)S(1)} %add.15.a_ref), channel_id=1, source_target_pairs={{0,16},{4,20},{8,24},{12,28},{16,0},{20,4},{24,8},{28,12},{1,17},{... | collective-permute-start | bytes 294920 | tf_op jit(solution)/shard_map/ppermute | solution.py:364
  102.6 0.6 copy-start.3

commit v2 on v0

v2 whole, which is shorter than its diff:
```python
import functools

import jax
import jax.numpy as jnp
from jax import lax
from jax.experimental import pallas as pl
from jax.experimental.pallas import tpu as pltpu
from jax.sharding import PartitionSpec as P

LANES = 128
RIM = 16
COST = 1024
F32 = jnp.float32
BF16 = jnp.bfloat16
VMEM_LIMIT = 24 * 1024 * 1024


def pairwise(axis, step):
    return [(source, source ^ step) for source in range(lax.axis_size(axis))]


def shifted(value, axis, steps):
    count = lax.axis_size(axis)
    initial, last = (max(0, -steps), min(count, count - steps))
    return lax.ppermute(value, axis, [(source, source + steps) for source in range(initial, last)])


def call(body, name, outs, scratch=(), scalars=0, far=0, operands=0, cost=COST):
    specs = [pl.BlockSpec(memory_space=pltpu.SMEM)] * scalars
    specs += [pl.BlockSpec(memory_space=pltpu.HBM)] * far
    specs += [pl.BlockSpec(memory_space=pltpu.VMEM)] * operands
    return pl.pallas_call(
        body,
        out_shape=outs,
        in_specs=specs,
        out_specs=jax.tree.map(lambda _: pl.BlockSpec(memory_space=pltpu.VMEM), outs),
        scratch_shapes=scratch,
        compiler_params=pltpu.CompilerParams(vmem_limit_bytes=VMEM_LIMIT),
        cost_estimate=pl.CostEstimate(flops=0, transcendentals=0, bytes_accessed=cost),
        name=name,
    )


def shape(dims, dtype):
    return jax.ShapeDtypeStruct(dims, dtype)


def each_tile(chans, body):
    def step(j, carry):
        body(j, pl.ds(pl.multiple_of(j * LANES, LANES), LANES))
        return carry

    lax.fori_loop(0, chans // LANES, step, 0)


def feature(ext_ref, taps_ref, lanes, part, start, rows):
    total = taps_ref[0, part : part + 1, lanes] * ext_ref[part, 8 + start : 8 + start + rows, :]
    for lag in range(1, 3):
        first = 8 + start - lag
        tap = taps_ref[lag, part : part + 1, lanes]
        total = total + tap * ext_ref[part, first : first + rows, :]
    return total


def group_of_lane(rows, group):
    return lax.broadcasted_iota(jnp.int32, (rows, LANES), 1) // group


def square(axis):
    return lax.broadcasted_iota(jnp.int32, (LANES, LANES), axis)


def fill_table(table_ref, taps, forward):
    early = (square(1) > square(0)) if forward else (square(1) >= square(0))
    for g in range(taps.shape[0]):
        wide = jnp.broadcast_to(taps[g : g + 1, :], (LANES, LANES))
        ring = pltpu.roll(wide, 0, 1, stride=1, stride_axis=0)
        table_ref[g * LANES : (g + 1) * LANES, 0:LANES] = jnp.where(early, ring, 0.0).astype(BF16)
        table_ref[g * LANES : (g + 1) * LANES, LANES:] = jnp.where(early, 0.0, ring).astype(BF16)


def pick_groups(wide, group, blocks):
    lane = group_of_lane(LANES, group)
    outs = []
    for b in range(blocks):
        total = wide[0:LANES, b * LANES : (b + 1) * LANES]
        for g in range(1, LANES // group):
            part = wide[g * LANES : (g + 1) * LANES, b * LANES : (b + 1) * LANES]
            total = jnp.where(lane == g, part, total)
        outs.append(total)
    return jnp.concatenate(outs, axis=0)


def side_by_side(ref, blocks, lanes):
    return jnp.concatenate([ref[b * LANES : (b + 2) * LANES, lanes] for b in range(blocks)], axis=1)


def spread_taps(filt, group, reverse):
    count = filt.shape[0]
    owner = (
        group_of_lane(count, group) == lax.broadcasted_iota(jnp.int32, (count, LANES), 0)
    ).astype(BF16)
    if reverse:
        flip = (square(0) + square(1) == LANES - 1).astype(BF16)
        filt = jnp.dot(filt, flip, preferred_element_type=F32).astype(BF16)
    return lax.dot_general(filt, owner, (((0,), (0,)), ((), ())), preferred_element_type=F32)


def tail_kernel(
    x_hbm, taps_hbm, filt_hbm, sent_ref, x_ref, taps_ref, filt_ref, ext, sems
):
    _, rows, chans = x_ref.shape
    first = rows - LANES - RIM
    near = (pl.ds(1, 2), pl.ds(first, LANES + RIM))
    copies = [
        pltpu.make_async_copy(taps_hbm, taps_ref, sems.at[0]),
        pltpu.make_async_copy(x_hbm.at[near], x_ref.at[near], sems.at[1]),
        pltpu.make_async_copy(x_hbm.at[0], x_ref.at[0], sems.at[2]),
        pltpu.make_async_copy(
            x_hbm.at[1:3, 0:first], x_ref.at[1:3, 0:first], sems.at[3]
        ),
        pltpu.make_async_copy(filt_hbm, filt_ref, sems.at[4]),
    ]
    for copy in copies:
        copy.start()
    for copy in copies[:3]:
        copy.wait()

    def tile(j, lanes):
        for part in range(3):
            ext[part, 8:, :] = x_ref[part, first:, lanes].astype(F32)
        keyed = feature(ext, taps_ref, lanes, 1, RIM, LANES)
        valued = feature(ext, taps_ref, lanes, 2, RIM, LANES)
        sent_ref[0:LANES, lanes] = (keyed * valued).astype(BF16)
        end = 8 + RIM + LANES
        rim = [ext[part, end - 2 : end, :] for part in range(3)]
        rim.append(jnp.zeros((RIM - 6, LANES), F32))
        sent_ref[LANES:, lanes] = jnp.concatenate(rim, axis=0).astype(BF16)

    each_tile(chans, tile)
    for copy in copies[3:]:
        copy.wait()


def grad_gate_kernel(
    c_hbm, w_hbm, x_ref, taps_ref, gg_ref, back_ref, w_ref, c_ref, ext, c_sem, w_sems
):
    chans = w_ref.shape[0]
    chunks = w_sems.shape[0]
    wide = chans // chunks
    span = LANES + RIM

    def chunk(j):
        rows = pl.ds(pl.multiple_of(j * wide, wide), wide)
        return pltpu.make_async_copy(w_hbm.at[rows], w_ref.at[rows], w_sems.at[j])

    load = pltpu.make_async_copy(c_hbm, c_ref, c_sem)
    load.start()
    for j in range(chunks):
        chunk(j).start()
    load.wait()

    def product(j, carry):
        chunk(j).wait()
        cols = pl.ds(pl.multiple_of(j * wide, wide), wide)
        gg_ref[:, cols] = lax.dot_general(
            c_ref[...], w_ref[cols, :], (((1,), (1,)), ((), ())), preferred_element_type=F32
        )
        return carry

    lax.fori_loop(0, chunks, product, 0)

    def tile(j, lanes):
        ext[0, 0:8, :] = jnp.zeros((8, LANES), F32)
        ext[0, 8:, :] = x_ref[0, 0:span, lanes].astype(F32)
        query = feature(ext, taps_ref, lanes, 0, 0, span)
        back_ref[0:span, lanes] = (gg_ref[0:span, lanes] * query).astype(BF16)
        grad = gg_ref[0:2, lanes]
        high = grad.astype(BF16).astype(F32)
        rim = [x_ref[part, 0:RIM, lanes].astype(F32)[0:2] for part in range(3)]
        rim += [high, grad - high, jnp.zeros((RIM - 10, LANES), F32)]
        back_ref[span:, lanes] = jnp.concatenate(rim, axis=0).astype(BF16)

    each_tile(chans, tile)


def forward_kernel(
    group, which_ref, x_ref, taps_ref, filt_ref, halo_ref, w_ref,
    send_ref, gate_ref, mixed_ref, gext_ref, ext, table,
):
    _, rows, chans = x_ref.shape
    blocks = rows // LANES
    count = LANES // group

    def tile(j, lanes):
        for part in range(3):
            at = LANES + 2 * part
            ext[part, 6:8, :] = halo_ref[at : at + 2, lanes].astype(F32)
            ext[part, 8:, :] = x_ref[part, :, lanes].astype(F32)
        keyed = feature(ext, taps_ref, lanes, 1, 0, rows)
        valued = feature(ext, taps_ref, lanes, 2, 0, rows)
        gext_ref[0:LANES, lanes] = halo_ref[0:LANES, lanes]
        gext_ref[LANES:, lanes] = (keyed * valued).astype(BF16)
        filt = filt_ref[pl.ds(pl.multiple_of(j * count, count), count), :]
        turned = ((square(0) + square(1)) % LANES == 0).astype(BF16)
        fill_table(table, jnp.dot(filt, turned, preferred_element_type=F32), True)
        wide = jnp.dot(
            table[...], side_by_side(gext_ref, blocks, lanes), preferred_element_type=F32
        )
        mixed = pick_groups(wide, group, blocks)
        mixed_ref[:, lanes] = mixed
        query = feature(ext, taps_ref, lanes, 0, 0, rows)
        gate_ref[:, lanes] = (query * mixed).astype(BF16)

    each_tile(chans, tile)
    half = w_ref.shape[1] // 2
    cols = pl.ds(pl.multiple_of(which_ref[0] * half, half), half)
    send_ref[...] = jnp.dot(
        gate_ref[...], w_ref[:, cols], preferred_element_type=F32
    ).astype(BF16)


def keep_kernel(which_ref, gate_ref, w_ref, keep_ref):
    half = w_ref.shape[1] // 2
    cols = pl.ds(pl.multiple_of(which_ref[0] * half, half), half)
    keep_ref[...] = jnp.dot(
        gate_ref[...], w_ref[:, cols], preferred_element_type=F32
    ).astype(BF16)


def backward_kernel(
    group, x_ref, taps_ref, filt_ref, halo_ref, gg_ref, mixed_ref, gext_ref, back_ref,
    gin_ref, sums_ref, ext, mext, gf, table, left,
):
    _, rows, chans = x_ref.shape
    blocks = rows // LANES
    count = LANES // group
    span = LANES + RIM

    def tile(j, lanes):
        for part in range(3):
            at = LANES + 2 * part
            ext[part, 6:8, :] = halo_ref[at : at + 2, lanes].astype(F32)
            ext[part, 8 : 8 + rows, :] = x_ref[part, :, lanes].astype(F32)
            at = span + 2 * part
            ext[part, 8 + rows : 10 + rows, :] = back_ref[at : at + 2, lanes].astype(F32)
        query = feature(ext, taps_ref, lanes, 0, 0, rows)
        keyed = feature(ext, taps_ref, lanes, 1, 0, rows)
        valued = feature(ext, taps_ref, lanes, 2, 0, rows)
        query_next = feature(ext, taps_ref, lanes, 0, rows, 2)
        keyed_next = feature(ext, taps_ref, lanes, 1, rows, 2)
        valued_next = feature(ext, taps_ref, lanes, 2, rows, 2)
        gg_next = back_ref[span + 6 : span + 8, lanes].astype(F32) + back_ref[
            span + 8 : span + 10, lanes
        ].astype(F32)
        grad_mixed = (gg_ref[:, lanes] * query).astype(BF16)
        head = back_ref[0:span, lanes].astype(F32)
        mixed_next = (gg_next * query_next).astype(BF16).astype(F32)
        head = jnp.concatenate([mixed_next, head[2:]], axis=0)
        mext[0:rows, :] = grad_mixed
        mext[rows:, :] = head[0:LANES].astype(BF16)
        filt = filt_ref[pl.ds(pl.multiple_of(j * count, count), count), :]
        fill_table(table, filt.astype(F32), False)
        wide = jnp.dot(
            table[...], side_by_side(mext, blocks, slice(None)), preferred_element_type=F32
        )
        grad_gated = pick_groups(wide, group, blocks)
        taps = spread_taps(filt, group, False)
        taps_turned = spread_taps(filt, group, True)
        recent = gext_ref[rows:, lanes].astype(F32)
        gated_next = (keyed_next * valued_next).astype(BF16).astype(F32)
        recent = jnp.concatenate([recent, gated_next], axis=0)
        grads_next, mixes_next = [], []
        for t in range(2):
            grads_next.append(jnp.sum(taps * head[t : t + LANES], axis=0, keepdims=True))
            mixes_next.append(
                jnp.sum(taps_turned * recent[t + 1 : t + 1 + LANES], axis=0, keepdims=True)
            )
        grad_next = jnp.concatenate(grads_next, axis=0)
        mix_next = jnp.concatenate(mixes_next, axis=0)
        parts = (
            (gg_ref[:, lanes] * mixed_ref[:, lanes]).astype(BF16).astype(F32),
            (grad_gated * valued).astype(BF16).astype(F32),
            (grad_gated * keyed).astype(BF16).astype(F32),
        )
        following = (gg_next * mix_next, grad_next * valued_next, grad_next * keyed_next)
        short_rows = [[None] * 3 for _ in range(3)]
        for part in range(3):
            gf[part, 0:rows, :] = parts[part]
            gf[part, rows : rows + 2, :] = following[part].astype(BF16).astype(F32)
            total = taps_ref[0, part : part + 1, lanes] * parts[part]
            for lag in range(1, 3):
                tap = taps_ref[lag, part : part + 1, lanes]
                total = total + tap * gf[part, lag : lag + rows, :]
            gin_ref[part, :, lanes] = total.astype(BF16)
            for lag in range(3):
                short_rows[lag][part] = jnp.sum(
                    parts[part] * ext[part, 8 - lag : 8 - lag + rows, :], axis=0, keepdims=True
                )
        lane = group_of_lane(LANES, group)
        for g in range(count):
            for b in range(blocks):
                left[g * LANES : (g + 1) * LANES, b * LANES : (b + 1) * LANES] = jnp.where(
                    lane == g, grad_mixed[b * LANES : (b + 1) * LANES, :], jnp.zeros((), BF16)
                )
        ends = [gext_ref[b * LANES : (b + 1) * LANES, lanes] for b in range(blocks + 1)]
        flip = (square(0) + square(1) == LANES - 1).astype(BF16)
        upside = jnp.dot(
            flip, jnp.concatenate(ends, axis=1), preferred_element_type=F32
        ).astype(BF16)
        right = jnp.concatenate([upside[:, 0 : blocks * LANES], upside[:, LANES:]], axis=0)
        products = lax.dot_general(
            left[...], right, (((1,), (1,)), ((), ())), preferred_element_type=F32
        )
        early = square(0) + square(1) < LANES - 1
        lag_rows = []
        for g in range(count):
            own = products[g * LANES : (g + 1) * LANES, :]
            ring = jnp.where(early, own[:, 0:LANES], own[:, LANES:])
            ring = pltpu.roll(ring, 0, 1, stride=1, stride_axis=0)
            lag_rows.append(jnp.sum(ring, axis=0, keepdims=True))
        sums_ref[0:8, lanes] = pltpu.roll(jnp.concatenate(lag_rows, axis=0), 1, 1)
        flat = [short_rows[lag][part] for lag in range(3) for part in range(3)]
        flat.append(jnp.zeros((7, LANES), F32))
        sums_ref[8:24, lanes] = jnp.concatenate(flat, axis=0)

    each_tile(chans, tile)


def unpack_kernel(group, short_scale, long_scale, a_ref, b_ref, short_ref, long_ref):
    chans = a_ref.shape[1]
    count = LANES // group
    total = a_ref[...] + b_ref[...]
    for j in range(chans // LANES):
        long_ref[j * count : (j + 1) * count, :] = (
            total[0:8, j * LANES : (j + 1) * LANES] * long_scale
        )
    for lag in range(3):
        for part in range(3):
            at = 8 + 3 * lag + part
            short_ref[lag, part : part + 1, :] = total[at : at + 1] * short_scale


def local(inputs, short_filter, long_filter, out_weight, out_cotangent):
    rows, _, chans = inputs.shape
    groups, span = long_filter.shape
    width = out_weight.shape[1]
    group = chans // groups
    count = LANES // group
    tokens_all = rows * lax.axis_size("ctx")
    n_tp = lax.axis_size("tp")
    signal = inputs.transpose(1, 0, 2)
    signal, short_filter, long_filter, out_weight, out_cotangent = [
        pltpu.with_memory_space_constraint(value, pltpu.HBM)
        for value in (signal, short_filter, long_filter, out_weight, out_cotangent)
    ]
    table = pltpu.VMEM((count * LANES, 2 * LANES), BF16)

    sent, signal, short_filter, long_filter = call(
        tail_kernel,
        "tail",
        (
            shape((LANES + RIM, chans), BF16),
            shape(signal.shape, BF16),
            shape(short_filter.shape, F32),
            shape(long_filter.shape, BF16),
        ),
        [pltpu.VMEM((3, 8 + RIM + LANES, LANES), F32), pltpu.SemaphoreType.DMA((5,))],
        far=3,
    )(signal, short_filter, long_filter)
    halo = shifted(sent, "ctx", 1)
    grad_gate, sent_back, out_weight = call(
        grad_gate_kernel,
        "grad_gate",
        (
            shape((rows, chans), F32),
            shape((LANES + 2 * RIM, chans), BF16),
            shape(out_weight.shape, BF16),
        ),
        [
            pltpu.VMEM(out_cotangent.shape, BF16),
            pltpu.VMEM((1, 8 + RIM + LANES, LANES), F32),
            pltpu.SemaphoreType.DMA,
            pltpu.SemaphoreType.DMA((max(1, chans // 256),)),
        ],
        far=2,
        operands=2,
    )(out_cotangent, out_weight, signal, short_filter)
    back = shifted(sent_back, "ctx", -1)
    core = lax.rem(lax.axis_index("tp"), 2)
    other, gate_out, mixed, gated = call(
        functools.partial(forward_kernel, group),
        "forward",
        (
            shape((rows, width // 2), BF16),
            shape((rows, chans), BF16),
            shape((rows, chans), F32),
            shape((LANES + rows, chans), BF16),
        ),
        [pltpu.VMEM((3, 8 + rows, LANES), F32), table],
        scalars=1,
        operands=5,
    )(jnp.reshape(1 - core, (1,)), signal, short_filter, long_filter, halo, out_weight)
    theirs = lax.ppermute(other, "tp", pairwise("tp", 1))
    mine = call(keep_kernel, "keep", shape((rows, width // 2), BF16), scalars=1, operands=2)(
        jnp.reshape(core, (1,)), gate_out, out_weight
    )
    theirs, back = lax.optimization_barrier((theirs, back))
    mine = (mine.astype(F32) + theirs.astype(F32)).astype(BF16)
    step = 2
    got = lax.ppermute(mine, "tp", pairwise("tp", step))

    grad_in, sums = call(
        functools.partial(backward_kernel, group),
        "backward",
        (shape((3, rows, chans), BF16), shape((24, chans), F32)),
        [
            pltpu.VMEM((3, rows + 16, LANES), F32),
            pltpu.VMEM((rows + LANES, LANES), BF16),
            pltpu.VMEM((3, rows + 8, LANES), F32),
            table,
            pltpu.VMEM((count * LANES, (rows // LANES) * LANES), BF16),
        ],
        operands=8,
        cost=200_000_000,
    )(signal, short_filter, long_filter, halo, grad_gate, mixed, gated, back)

    n_ctx = lax.axis_size("ctx")
    if n_ctx & (n_ctx - 1) == 0:
        hop = 1
        rest = jnp.zeros_like(sums)
        while hop < n_ctx:
            rest = lax.ppermute(sums, "ctx", pairwise("ctx", hop))
            hop *= 2
            if hop < n_ctx:
                sums = sums + rest
    else:
        sums = lax.psum(sums, "ctx")
        rest = jnp.zeros_like(sums)
    got, sums, rest = lax.optimization_barrier((got, sums, rest))
    mine = (mine.astype(F32) + got.astype(F32)).astype(BF16)
    step *= 2
    while step < n_tp:
        got = lax.ppermute(mine, "tp", pairwise("tp", step))
        mine = (mine.astype(F32) + got.astype(F32)).astype(BF16)
        step *= 2
    sibling = lax.ppermute(mine, "tp", pairwise("tp", 1))
    result = jnp.where(
        core == 0,
        jnp.concatenate([mine, sibling], axis=1),
        jnp.concatenate([sibling, mine], axis=1),
    )
    grad_short, grad_long = call(
        functools.partial(
            unpack_kernel, group, float(tokens_all) ** (-0.5), float(tokens_all * group) ** (-0.5)
        ),
        "unpack",
        (shape((3, 3, chans), F32), shape((groups, span), F32)),
        operands=2,
    )(sums, rest)
    return (result, grad_in.transpose(1, 0, 2), grad_short, grad_long)


def solution(mesh):
    in_specs = (
        P("ctx", None, "tp"),
        P(None, None, "tp"),
        P("tp", None),
        P("tp", None),
        P("ctx", None),
    )
    out_specs = (P("ctx", None), P("ctx", None, "tp"), P(None, None, "tp"), P("tp", None))
    return jax.shard_map(local, mesh=mesh, in_specs=in_specs, out_specs=out_specs, check_vma=False)
```

time: 590 us -> 65.8 us (0.11); the launches traced: 582 us -> 65.6 us
  local copies, waits for them, and re-layouts: 368 us -> 0 us
  waiting for transfers between devices: 114 us -> 22.8 us
  other arithmetic: 42.7 us -> 2.93 us
  matrix products: 36.9 us -> 0 us
  Pallas kernels: 0 us -> 26.7 us
  between operations: 14.5 us -> 0.71 us
  starting transfers between devices: 6.26 us -> 12.5 us
    gather x4 -> x0, local copies, waits for them, and re-layouts: 250 us -> none  [tap_table(): picked = filt[:, jnp.clip(offset, 0, span - 1)]]
    psum x2 -> x0, waiting for transfers between devices: 114 us -> none  [the longest x1 59.3 us: local(): long_total, short_total = lax.psum((long_local, short_local), 'ctx')]
    rev x1 -> x0, local copies, waits for them, and re-layouts: 63.8 us -> none  [local(): flipped = products[:, :, ::-1].reshape(groups, 2 * span * span)]
    dot_general x10 -> x0, matrix products: 36.9 us -> none  [the longest x3 8.57 us: block_conv(): jnp.einsum('gij,bjgc->bigc', table[:, :, span:], second, preferred_elemen...]
    pallas_call x0 -> x6, Pallas kernels: none -> 26.7 us  [the longest x1 10.5 us: local(): call(functools.partial(backward_kernel, group), 'backward', (shape((3, ro...]
    reshape x10 -> x0, local copies, waits for them, and re-layouts: 21.1 us -> none  [the longest x1 15.9 us: local(): flipped[:, span - 1:span - 1 + span * (2 * span - 1)]]
    unnamed x30 -> x0, local copies, waits for them, and re-layouts: 17.1 us -> none
    ppermute x0 -> x6, waiting for transfers between devices: none -> 14.2 us  [the longest x3 12.6 us: local(): rest = lax.ppermute(sums, 'ctx', pairwise('ctx', hop))]
  transfers between devices with their start and end apart: 4 -> 8, of which waited for: 2 -> 6; matrix products, arithmetic and copies ran while one was open for 65% -> 0% of each run, Pallas kernels for 0% -> 29%
where the time goes in v2:
time: 65.8 us; the launch traced here: 65.6 us
  Pallas kernels  26.7 us (41%)
  waiting for transfers between devices  22.8 us (35%)
  starting transfers between devices  12.5 us (19%)
  other arithmetic  2.93 us (4%)
  between operations  0.71 us (1%)
    ppermute x3, waiting for transfers between devices, local(): rest = lax.ppermute(sums, 'ctx', pairwise('ctx', hop))  12.6 us
    pallas_call x1, Pallas kernels, local(): call(functools.partial(backward_kernel, group), 'backward', (shape((3, ro...  10.5 us
    ppermute x2, waiting for transfers between devices, shifted(): lax.ppermute(value, axis, [(source, source + steps) for source in range(i...  8.53 us
    pallas_call x1, Pallas kernels, local(): call(grad_gate_kernel, 'grad_gate', (shape((rows, chans), F32), shape((LA...  6.81 us
    pallas_call x1, Pallas kernels, local(): call(functools.partial(forward_kernel, group), 'forward', (shape((rows, w...  5.69 us
    ppermute x2, starting transfers between devices, shifted(): lax.ppermute(value, axis, [(source, source + steps) for source in range(i...  5.21 us
    ppermute x1, starting transfers between devices, local(): sibling = lax.ppermute(mine, 'tp', pairwise('tp', 1))  4.01 us
    select_n x1, other arithmetic, local(): jnp.where(core == 0, jnp.concatenate([mine, sibling], axis=1), jnp.concat...  2.12 us
  transfers between devices with their start and end apart: 8, of which 6 were waited for; matrix products, arithmetic and copies ran while one was open for 0% of the time, Pallas kernels for 29%

profile of v2, /device:TPU:25, one launch (start us, length us, event | category | flops | bytes accessed | tf_op | source)
XLA Modules:
  0.0 65.6 jit_solution(17888565696819034414)
XLA Ops:
  0.6 1.8 %tail.1 = (bf16[144,1024]{1,0:T(8,128)(2,1)S(1)}, bf16[3,256,1024]{2,1,0:T(8,128)(2,1)S(1)}, f32[3,3,1024]{2,1,0:T(4,128)S(1)}, bf16[64,128]{1,0:T(8,128)(2,1)S(1)}) custom-call(bf16[3,256,1024]{2,1,0:T(8,128)(2,1)} %bitcast.4, f32[3,3,1024]{2,1,0:T(4,128)} %taps_hbm.1, bf16[64,128]{1,0:T(8,128)(2,1)} %filt_hbm.1), custom_call_target="tpu_custom_call" | custom-call | bytes 1024 | tf_op jit(solution)/shard_map/tail/pallas_call | solution.py:359
  2.4 3.1 %collective-permute-start = (bf16[144,1024]{1,0:T(8,128)(2,1)S(1)}, bf16[144,1024]{1,0:T(8,128)(2,1)S(1)}, u32[]{:S(2)}, u32[]{:S(2)}) collective-permute-start(bf16[144,1024]{1,0:T(8,128)(2,1)S(1)} %get-tuple-element.27), channel_id=1, source_target_pairs={{0,4},{4,8},{8,12},{12,16},{16,20},{20,24},{24,28},{1,5},{5,9},{9,... | collective-permute-start | bytes 884744 | tf_op jit(solution)/shard_map/ppermute | solution.py:25
  5.5 6.8 %grad_gate.1 = (f32[256,1024]{1,0:T(8,128)S(1)}, bf16[160,1024]{1,0:T(8,128)(2,1)S(1)}, bf16[1024,4096]{1,0:T(8,128)(2,1)S(1)}) custom-call(bf16[256,4096]{1,0:T(8,128)(2,1)} %c_hbm.1, bf16[1024,4096]{1,0:T(8,128)(2,1)} %w_hbm.1, bf16[3,256,1024]{2,1,0:T(8,128)(2,1)S(1)} %get-tuple-element.24.x_ref, f32[3,3,1024]{2,1,0:T(4,128)S(1)} %get-tuple-element.25.taps_ref), custom_call_target="tpu_custom_call" | custom-call | bytes 1024 | tf_op jit(solution)/shard_map/grad_gate/pallas_call | solution.py:372
  12.3 0.7 %collective-permute-done.halo_ref = bf16[144,1024]{1,0:T(8,128)(2,1)S(1)} collective-permute-done((bf16[144,1024]{1,0:T(8,128)(2,1)S(1)}, bf16[144,1024]{1,0:T(8,128)(2,1)S(1)}, u32[]{:S(2)}, u32[]{:S(2)}) %collective-permute-start) | collective-permute-done | bytes 294944 | tf_op jit(solution)/shard_map/ppermute | solution.py:25
  13.1 5.7 %forward.1 = (bf16[256,2048]{1,0:T(8,128)(2,1)S(1)}, bf16[256,1024]{1,0:T(8,128)(2,1)S(1)}, f32[256,1024]{1,0:T(8,128)S(1)}, bf16[384,1024]{1,0:T(8,128)(2,1)S(1)}) custom-call(s32[1]{0:T(128)} %bitcast.1.which_ref, bf16[3,256,1024]{2,1,0:T(8,128)(2,1)S(1)} %get-tuple-element.24.x_ref, f32[3,3,1024]{2,1,0:T(4,128)S(1)} %get-tuple-element.25.taps_ref, ...), custom_call_target="tpu_custom_call" | custom-call | bytes 1024 | tf_op jit(solution)/shard_map/forward/pallas_call | solution.py:391
  18.8 1.6 %collective-permute-start.1 = (bf16[256,2048]{1,0:T(8,128)(2,1)S(1)}, bf16[256,2048]{1,0:T(8,128)(2,1)S(1)}, u32[]{:S(2)}, u32[]{:S(2)}) collective-permute-start(bf16[256,2048]{1,0:T(8,128)(2,1)S(1)} %get-tuple-element.30), channel_id=1, source_target_pairs={{0,1},{1,0},{2,3},{3,2},{4,5},{5,4},{6,7},{7,6},{8,9},{9,8},{10,11... | collective-permute-start | bytes 3145736 | tf_op jit(solution)/shard_map/ppermute | solution.py:404
  20.4 2.1 %collective-permute-start.2 = (bf16[160,1024]{1,0:T(8,128)(2,1)S(1)}, bf16[160,1024]{1,0:T(8,128)(2,1)S(1)}, u32[]{:S(2)}, u32[]{:S(2)}) collective-permute-start(bf16[160,1024]{1,0:T(8,128)(2,1)S(1)} %get-tuple-element.31), channel_id=1, source_target_pairs={{4,0},{8,4},{12,8},{16,12},{20,16},{24,20},{28,24},{5,1},{9,5},{13... | collective-permute-start | bytes 983048 | tf_op jit(solution)/shard_map/ppermute | solution.py:25
  22.5 1.3 %keep.1 = bf16[256,2048]{1,0:T(8,128)(2,1)S(1)} custom-call(s32[1]{0:T(128)} %bitcast.which_ref, bf16[256,1024]{1,0:T(8,128)(2,1)S(1)} %get-tuple-element.29.gate_ref, bf16[1024,4096]{1,0:T(8,128)(2,1)S(1)} %get-tuple-element.28.w_ref), custom_call_target="tpu_custom_call" | custom-call | bytes 1024 | tf_op jit(solution)/shard_map/keep/pallas_call | solution.py:405
  23.8 7.8 %collective-permute-done.2.back_ref = bf16[160,1024]{1,0:T(8,128)(2,1)S(1)} collective-permute-done((bf16[160,1024]{1,0:T(8,128)(2,1)S(1)}, bf16[160,1024]{1,0:T(8,128)(2,1)S(1)}, u32[]{:S(2)}, u32[]{:S(2)}) %collective-permute-start.2) | collective-permute-done | bytes 327712 | tf_op jit(solution)/shard_map/ppermute | solution.py:25
  31.6 0.0 collective-permute-done.1
  31.6 0.4 add_convert_fusion.1
  32.0 1.3 %collective-permute-start.3 = (bf16[256,2048]{1,0:T(8,128)(2,1)S(1)}, bf16[256,2048]{1,0:T(8,128)(2,1)S(1)}, u32[]{:S(2)}, u32[]{:S(2)}) collective-permute-start(bf16[256,2048]{1,0:T(8,128)(2,1)S(1)} %add_convert_fusion.1), channel_id=1, source_target_pairs={{0,2},{1,3},{2,0},{3,1},{4,6},{5,7},{6,4},{7,5},{8,10},{9,11},{10,... | collective-permute-start | bytes 3145736 | tf_op jit(solution)/shard_map/ppermute | solution.py:411
  33.3 10.5 %backward.1 = (bf16[3,256,1024]{2,1,0:T(8,128)(2,1)}, f32[24,1024]{1,0:T(8,128)S(1)}) custom-call(bf16[3,256,1024]{2,1,0:T(8,128)(2,1)S(1)} %get-tuple-element.24.x_ref, f32[3,3,1024]{2,1,0:T(4,128)S(1)} %get-tuple-element.25.taps_ref, bf16[64,128]{1,0:T(8,128)(2,1)S(1)} %get-tuple-element.26.filt_ref, bf16[144,1024]{1,0:T(8,128)(2,1)S(1)} %collective-permute-done.halo_ref, ...), custom_call_target="tpu_custom_call" | custom-call | bytes 200000000 | tf_op jit(solution)/shard_map/backward/pallas_call | solution.py:413
  43.8 0.0 collective-permute-start.4
  43.8 3.8 %collective-permute-done.4 = f32[24,1024]{1,0:T(8,128)S(1)} collective-permute-done((f32[24,1024]{1,0:T(8,128)S(1)}, f32[24,1024]{1,0:T(8,128)S(1)}, u32[]{:S(2)}, u32[]{:S(2)}) %collective-permute-start.4) | collective-permute-done | bytes 98336 | tf_op jit(solution)/shard_map/ppermute | solution.py:433
  47.6 0.2 collective-permute-start.5
  47.8 3.6 %collective-permute-done.5 = f32[24,1024]{1,0:T(8,128)S(1)} collective-permute-done((f32[24,1024]{1,0:T(8,128)S(1)}, f32[24,1024]{1,0:T(8,128)S(1)}, u32[]{:S(2)}, u32[]{:S(2)}) %collective-permute-start.5) | collective-permute-done | bytes 98336 | tf_op jit(solution)/shard_map/ppermute | solution.py:433
  51.4 0.1 collective-permute-start.6
  51.5 5.3 %collective-permute-done.6.b_ref = f32[24,1024]{1,0:T(8,128)S(1)} collective-permute-done((f32[24,1024]{1,0:T(8,128)S(1)}, f32[24,1024]{1,0:T(8,128)S(1)}, u32[]{:S(2)}, u32[]{:S(2)}) %collective-permute-start.6) | collective-permute-done | bytes 98336 | tf_op jit(solution)/shard_map/ppermute | solution.py:433
  56.8 0.0 collective-permute-done.3
  56.8 0.4 add_convert_fusion
  57.2 4.0 %collective-permute-start.7 = (bf16[256,2048]{1,0:T(8,128)(2,1)S(1)}, bf16[256,2048]{1,0:T(8,128)(2,1)S(1)}, u32[]{:S(2)}, u32[]{:S(2)}) collective-permute-start(bf16[256,2048]{1,0:T(8,128)(2,1)S(1)} %add_convert_fusion), channel_id=1, source_target_pairs={{0,1},{1,0},{2,3},{3,2},{4,5},{5,4},{6,7},{7,6},{8,9},{9,8},{10,11... | collective-permute-start | bytes 3145736 | tf_op jit(solution)/shard_map/ppermute | solution.py:447
  61.2 0.6 unpack.1
  61.9 1.6 %collective-permute-done.7 = bf16[256,2048]{1,0:T(8,128)(2,1)S(1)} collective-permute-done((bf16[256,2048]{1,0:T(8,128)(2,1)S(1)}, bf16[256,2048]{1,0:T(8,128)(2,1)S(1)}, u32[]{:S(2)}, u32[]{:S(2)}) %collective-permute-start.7) | collective-permute-done | bytes 1048608 | tf_op jit(solution)/shard_map/ppermute | solution.py:447
  63.5 2.1 %maximum_select_fusion = bf16[256,4096]{1,0:T(8,128)(2,1)} fusion(bf16[256,2048]{1,0:T(8,128)(2,1)S(1)} %collective-permute-done.7, bf16[256,2048]{1,0:T(8,128)(2,1)S(1)} %add_convert_fusion, pred[]{:T(512)S(6)} %eq.3), kind=kLoop, calls=%fused_computation | loop fusion | flops 9437184 | bytes 4194305 | tf_op jit(solution)/shard_map/jit(_where)/select_n | solution.py:448
  (2 shorter events, 0.0 us)
Async XLA Ops:
  2.4 10.7 %collective-permute-start = (bf16[144,1024]{1,0:T(8,128)(2,1)S(1)}, bf16[144,1024]{1,0:T(8,128)(2,1)S(1)}, u32[]{:S(2)}, u32[]{:S(2)}) collective-permute-start(bf16[144,1024]{1,0:T(8,128)(2,1)S(1)} %get-tuple-element.27), channel_id=1, source_target_pairs={{0,4},{4,8},{8,12},{12,16},{16,20},{20,24},{24,28},{1,5},{5,9},{9,... | collective-permute-start | bytes 884744 | tf_op jit(solution)/shard_map/ppermute | solution.py:25
  18.8 12.8 %collective-permute-start.1 = (bf16[256,2048]{1,0:T(8,128)(2,1)S(1)}, bf16[256,2048]{1,0:T(8,128)(2,1)S(1)}, u32[]{:S(2)}, u32[]{:S(2)}) collective-permute-start(bf16[256,2048]{1,0:T(8,128)(2,1)S(1)} %get-tuple-element.30), channel_id=1, source_target_pairs={{0,1},{1,0},{2,3},{3,2},{4,5},{5,4},{6,7},{7,6},{8,9},{9,8},{10,11... | collective-permute-start | bytes 3145736 | tf_op jit(solution)/shard_map/ppermute | solution.py:404
  20.4 11.2 %collective-permute-start.2 = (bf16[160,1024]{1,0:T(8,128)(2,1)S(1)}, bf16[160,1024]{1,0:T(8,128)(2,1)S(1)}, u32[]{:S(2)}, u32[]{:S(2)}) collective-permute-start(bf16[160,1024]{1,0:T(8,128)(2,1)S(1)} %get-tuple-element.31), channel_id=1, source_target_pairs={{4,0},{8,4},{12,8},{16,12},{20,16},{24,20},{28,24},{5,1},{9,5},{13... | collective-permute-start | bytes 983048 | tf_op jit(solution)/shard_map/ppermute | solution.py:25
  32.0 24.8 %collective-permute-start.3 = (bf16[256,2048]{1,0:T(8,128)(2,1)S(1)}, bf16[256,2048]{1,0:T(8,128)(2,1)S(1)}, u32[]{:S(2)}, u32[]{:S(2)}) collective-permute-start(bf16[256,2048]{1,0:T(8,128)(2,1)S(1)} %add_convert_fusion.1), channel_id=1, source_target_pairs={{0,2},{1,3},{2,0},{3,1},{4,6},{5,7},{6,4},{7,5},{8,10},{9,11},{10,... | collective-permute-start | bytes 3145736 | tf_op jit(solution)/shard_map/ppermute | solution.py:411
  43.8 3.8 %collective-permute-start.4 = (f32[24,1024]{1,0:T(8,128)S(1)}, f32[24,1024]{1,0:T(8,128)S(1)}, u32[]{:S(2)}, u32[]{:S(2)}) collective-permute-start(f32[24,1024]{1,0:T(8,128)S(1)} %get-tuple-element.37), channel_id=1, source_target_pairs={{0,4},{4,0},{8,12},{12,8},{16,20},{20,16},{24,28},{28,24},{1,5},{5... | collective-permute-start | bytes 294920 | tf_op jit(solution)/shard_map/ppermute | solution.py:433
  47.6 3.8 %collective-permute-start.5 = (f32[24,1024]{1,0:T(8,128)S(1)}, f32[24,1024]{1,0:T(8,128)S(1)}, u32[]{:S(2)}, u32[]{:S(2)}) collective-permute-start(f32[24,1024]{1,0:T(8,128)S(1)} %add.13), channel_id=1, source_target_pairs={{0,8},{4,12},{8,0},{12,4},{16,24},{20,28},{24,16},{28,20},{1,9},{5... | collective-permute-start | bytes 294920 | tf_op jit(solution)/shard_map/ppermute | solution.py:433
  51.4 5.4 %collective-permute-start.6 = (f32[24,1024]{1,0:T(8,128)S(1)}, f32[24,1024]{1,0:T(8,128)S(1)}, u32[]{:S(2)}, u32[]{:S(2)}) collective-permute-start(f32[24,1024]{1,0:T(8,128)S(1)} %add.14.a_ref), channel_id=1, source_target_pairs={{0,16},{4,20},{8,24},{12,28},{16,0},{20,4},{24,8},{28,12},{1,17},{... | collective-permute-start | bytes 294920 | tf_op jit(solution)/shard_map/ppermute | solution.py:433
  57.2 6.3 %collective-permute-start.7 = (bf16[256,2048]{1,0:T(8,128)(2,1)S(1)}, bf16[256,2048]{1,0:T(8,128)(2,1)S(1)}, u32[]{:S(2)}, u32[]{:S(2)}) collective-permute-start(bf16[256,2048]{1,0:T(8,128)(2,1)S(1)} %add_convert_fusion), channel_id=1, source_target_pairs={{0,1},{1,0},{2,3},{3,2},{4,5},{5,4},{6,7},{7,6},{8,9},{9,8},{10,11... | collective-permute-start | bytes 3145736 | tf_op jit(solution)/shard_map/ppermute | solution.py:447

commit v3 on v2

--- a/solution.py
+++ b/solution.py
@@ -10,9 +10,10 @@
 LANES = 128
 RIM = 16
 COST = 1024
+PIECES = 2
 F32 = jnp.float32
 BF16 = jnp.bfloat16
-VMEM_LIMIT = 24 * 1024 * 1024
+VMEM_LIMIT = 12 * 1024 * 1024
 
 
 def pairwise(axis, step):
@@ -50,7 +51,7 @@
         body(j, pl.ds(pl.multiple_of(j * LANES, LANES), LANES))
         return carry
 
-    lax.fori_loop(0, chans // LANES, step, 0)
+    lax.fori_loop(0, chans // LANES, step, 0, unroll=2)
 
 
 def feature(ext_ref, taps_ref, lanes, part, start, rows):
@@ -156,12 +157,17 @@
 
     load = pltpu.make_async_copy(c_hbm, c_ref, c_sem)
     load.start()
-    for j in range(chunks):
+    for j in range(min(2, chunks)):
         chunk(j).start()
     load.wait()
 
     def product(j, carry):
         chunk(j).wait()
+
+        @pl.when(j + 2 < chunks)
+        def _():
+            chunk(j + 2).start()
+
         cols = pl.ds(pl.multiple_of(j * wide, wide), wide)
         gg_ref[:, cols] = lax.dot_general(
             c_ref[...], w_ref[cols, :], (((1,), (1,)), ((), ())), preferred_element_type=F32
@@ -186,8 +192,9 @@
 
 def forward_kernel(
     group, which_ref, x_ref, taps_ref, filt_ref, halo_ref, w_ref,
-    send_ref, gate_ref, mixed_ref, gext_ref, ext, table,
+    *refs,
 ):
+    sends, (gate_ref, mixed_ref, feat_ref, gext_ref, ext, table) = refs[:PIECES], refs[PIECES:]
     _, rows, chans = x_ref.shape
     blocks = rows // LANES
     count = LANES // group
@@ -199,6 +206,8 @@
             ext[part, 8:, :] = x_ref[part, :, lanes].astype(F32)
         keyed = feature(ext, taps_ref, lanes, 1, 0, rows)
         valued = feature(ext, taps_ref, lanes, 2, 0, rows)
+        feat_ref[1, :, lanes] = keyed
+        feat_ref[2, :, lanes] = valued
         gext_ref[0:LANES, lanes] = halo_ref[0:LANES, lanes]
         gext_ref[LANES:, lanes] = (keyed * valued).astype(BF16)
         filt = filt_ref[pl.ds(pl.multiple_of(j * count, count), count), :]
@@ -210,27 +219,67 @@
         mixed = pick_groups(wide, group, blocks)
         mixed_ref[:, lanes] = mixed
         query = feature(ext, taps_ref, lanes, 0, 0, rows)
+        feat_ref[0, :, lanes] = query
         gate_ref[:, lanes] = (query * mixed).astype(BF16)
 
     each_tile(chans, tile)
+    project(which_ref[0], gate_ref, w_ref, sends)
+
+
+def project(which, gate_ref, w_ref, out_refs):
     half = w_ref.shape[1] // 2
-    cols = pl.ds(pl.multiple_of(which_ref[0] * half, half), half)
-    send_ref[...] = jnp.dot(
-        gate_ref[...], w_ref[:, cols], preferred_element_type=F32
-    ).astype(BF16)
-
-
-def keep_kernel(which_ref, gate_ref, w_ref, keep_ref):
-    half = w_ref.shape[1] // 2
-    cols = pl.ds(pl.multiple_of(which_ref[0] * half, half), half)
-    keep_ref[...] = jnp.dot(
-        gate_ref[...], w_ref[:, cols], preferred_element_type=F32
-    ).astype(BF16)
+    part = half // len(out_refs)
+    for i, out_ref in enumerate(out_refs):
+        cols = pl.ds(pl.multiple_of(which * half + i * part, part), part)
+        out_ref[...] = jnp.dot(
+            gate_ref[...], w_ref[:, cols], preferred_element_type=F32
+        ).astype(BF16)
+
+
+def keep_kernel(which_ref, gate_ref, w_ref, *keep_refs):
+    project(which_ref[0], gate_ref, w_ref, keep_refs)
+
+
+def lags_kernel(group, filt_ref, gg_ref, feat_ref, gext_ref, gm_ref, lags_ref, tables_ref, left):
+    rows, chans = gg_ref.shape
+    blocks = rows // LANES
+    count = LANES // group
+
+    def tile(j, lanes):
+        filt = filt_ref[pl.ds(pl.multiple_of(j * count, count), count), :]
+        fill_table(tables_ref.at[j], filt.astype(F32), False)
+        grad_mixed = (gg_ref[:, lanes] * feat_ref[0, :, lanes]).astype(BF16)
+        gm_ref[:, lanes] = grad_mixed
+        lane = group_of_lane(LANES, group)
+        for g in range(count):
+            for b in range(blocks):
+                left[g * LANES : (g + 1) * LANES, b * LANES : (b + 1) * LANES] = jnp.where(
+                    lane == g, grad_mixed[b * LANES : (b + 1) * LANES, :], jnp.zeros((), BF16)
+                )
+        ends = [gext_ref[b * LANES : (b + 1) * LANES, lanes] for b in range(blocks + 1)]
+        flip = (square(0) + square(1) == LANES - 1).astype(BF16)
+        upside = jnp.dot(
+            flip, jnp.concatenate(ends, axis=1), preferred_element_type=F32
+        ).astype(BF16)
+        right = jnp.concatenate([upside[:, 0 : blocks * LANES], upside[:, LANES:]], axis=0)
+        products = lax.dot_general(
+            left[...], right, (((1,), (1,)), ((), ())), preferred_element_type=F32
+        )
+        early = square(0) + square(1) < LANES - 1
+        lag_rows = []
+        for g in range(count):
+            own = products[g * LANES : (g + 1) * LANES, :]
+            ring = jnp.where(early, own[:, 0:LANES], own[:, LANES:])
+            ring = pltpu.roll(ring, 0, 1, stride=1, stride_axis=0)
+            lag_rows.append(jnp.sum(ring, axis=0, keepdims=True))
+        lags_ref[:, lanes] = pltpu.roll(jnp.concatenate(lag_rows, axis=0), 1, 1)
+
+    each_tile(chans, tile)
 
 
 def backward_kernel(
-    group, x_ref, taps_ref, filt_ref, halo_ref, gg_ref, mixed_ref, gext_ref, back_ref,
-    gin_ref, sums_ref, ext, mext, gf, table, left,
+    group, x_ref, taps_ref, filt_ref, halo_ref, gg_ref, mixed_ref, feat_ref, gext_ref, back_ref,
+    gm_ref, lags_ref, tables_ref, gin_ref, sums_ref, ext, mext, gf,
 ):
     _, rows, chans = x_ref.shape
     blocks = rows // LANES
@@ -244,27 +293,24 @@
             ext[part, 8 : 8 + rows, :] = x_ref[part, :, lanes].astype(F32)
             at = span + 2 * part
             ext[part, 8 + rows : 10 + rows, :] = back_ref[at : at + 2, lanes].astype(F32)
-        query = feature(ext, taps_ref, lanes, 0, 0, rows)
-        keyed = feature(ext, taps_ref, lanes, 1, 0, rows)
-        valued = feature(ext, taps_ref, lanes, 2, 0, rows)
+        keyed = feat_ref[1, :, lanes]
+        valued = feat_ref[2, :, lanes]
         query_next = feature(ext, taps_ref, lanes, 0, rows, 2)
         keyed_next = feature(ext, taps_ref, lanes, 1, rows, 2)
         valued_next = feature(ext, taps_ref, lanes, 2, rows, 2)
         gg_next = back_ref[span + 6 : span + 8, lanes].astype(F32) + back_ref[
             span + 8 : span + 10, lanes
         ].astype(F32)
-        grad_mixed = (gg_ref[:, lanes] * query).astype(BF16)
         head = back_ref[0:span, lanes].astype(F32)
         mixed_next = (gg_next * query_next).astype(BF16).astype(F32)
         head = jnp.concatenate([mixed_next, head[2:]], axis=0)
-        mext[0:rows, :] = grad_mixed
+        mext[0:rows, :] = gm_ref[:, lanes]
         mext[rows:, :] = head[0:LANES].astype(BF16)
-        filt = filt_ref[pl.ds(pl.multiple_of(j * count, count), count), :]
-        fill_table(table, filt.astype(F32), False)
         wide = jnp.dot(
-            table[...], side_by_side(mext, blocks, slice(None)), preferred_element_type=F32
+            tables_ref[j], side_by_side(mext, blocks, slice(None)), preferred_element_type=F32
         )
         grad_gated = pick_groups(wide, group, blocks)
+        filt = filt_ref[pl.ds(pl.multiple_of(j * count, count), count), :]
         taps = spread_taps(filt, group, False)
         taps_turned = spread_taps(filt, group, True)
         recent = gext_ref[rows:, lanes].astype(F32)
@@ -297,47 +343,27 @@
                 short_rows[lag][part] = jnp.sum(
                     parts[part] * ext[part, 8 - lag : 8 - lag + rows, :], axis=0, keepdims=True
                 )
-        lane = group_of_lane(LANES, group)
-        for g in range(count):
-            for b in range(blocks):
-                left[g * LANES : (g + 1) * LANES, b * LANES : (b + 1) * LANES] = jnp.where(
-                    lane == g, grad_mixed[b * LANES : (b + 1) * LANES, :], jnp.zeros((), BF16)
-                )
-        ends = [gext_ref[b * LANES : (b + 1) * LANES, lanes] for b in range(blocks + 1)]
-        flip = (square(0) + square(1) == LANES - 1).astype(BF16)
-        upside = jnp.dot(
-            flip, jnp.concatenate(ends, axis=1), preferred_element_type=F32
-        ).astype(BF16)
-        right = jnp.concatenate([upside[:, 0 : blocks * LANES], upside[:, LANES:]], axis=0)
-        products = lax.dot_general(
-            left[...], right, (((1,), (1,)), ((), ())), preferred_element_type=F32
-        )
-        early = square(0) + square(1) < LANES - 1
-        lag_rows = []
-        for g in range(count):
-            own = products[g * LANES : (g + 1) * LANES, :]
-            ring = jnp.where(early, own[:, 0:LANES], own[:, LANES:])
-            ring = pltpu.roll(ring, 0, 1, stride=1, stride_axis=0)
-            lag_rows.append(jnp.sum(ring, axis=0, keepdims=True))
-        sums_ref[0:8, lanes] = pltpu.roll(jnp.concatenate(lag_rows, axis=0), 1, 1)
-        flat = [short_rows[lag][part] for lag in range(3) for part in range(3)]
-        flat.append(jnp.zeros((7, LANES), F32))
-        sums_ref[8:24, lanes] = jnp.concatenate(flat, axis=0)
+        flat = [lags_ref[:, lanes]] + [short_rows[lag][part] for lag in range(3) for part in range(3)]
+        flat.append(jnp.zeros((15, LANES), F32))
+        sums_ref[:, lanes] = jnp.concatenate(flat, axis=0).astype(sums_ref.dtype)
 
     each_tile(chans, tile)
 
 
-def unpack_kernel(group, short_scale, long_scale, a_ref, b_ref, short_ref, long_ref):
-    chans = a_ref.shape[1]
+def unpack_kernel(group, short_scale, long_scale, *refs):
+    short_ref, long_ref = refs[-2:]
+    totals = [ref[...].astype(F32) for ref in refs[:-2]]
+    while len(totals) > 1:
+        totals = [sum(totals[i : i + 2]) for i in range(0, len(totals), 2)]
+    total = totals[0]
     count = LANES // group
-    total = a_ref[...] + b_ref[...]
-    for j in range(chans // LANES):
+    for j in range(total.shape[1] // LANES):
         long_ref[j * count : (j + 1) * count, :] = (
-            total[0:8, j * LANES : (j + 1) * LANES] * long_scale
+            total[0:count, j * LANES : (j + 1) * LANES] * long_scale
         )
     for lag in range(3):
         for part in range(3):
-            at = 8 + 3 * lag + part
+            at = count + 3 * lag + part
             short_ref[lag, part : part + 1, :] = total[at : at + 1] * short_scale
 
 
@@ -388,67 +414,85 @@
     )(out_cotangent, out_weight, signal, short_filter)
     back = shifted(sent_back, "ctx", -1)
     core = lax.rem(lax.axis_index("tp"), 2)
-    other, gate_out, mixed, gated = call(
+    piece = shape((rows, width // 2 // PIECES), BF16)
+    *other, gate_out, mixed, feat, gated = call(
         functools.partial(forward_kernel, group),
         "forward",
-        (
-            shape((rows, width // 2), BF16),
+        (piece,) * PIECES
+        + (
             shape((rows, chans), BF16),
             shape((rows, chans), F32),
+            shape((3, rows, chans), F32),
             shape((LANES + rows, chans), BF16),
         ),
         [pltpu.VMEM((3, 8 + rows, LANES), F32), table],
         scalars=1,
         operands=5,
     )(jnp.reshape(1 - core, (1,)), signal, short_filter, long_filter, halo, out_weight)
-    theirs = lax.ppermute(other, "tp", pairwise("tp", 1))
-    mine = call(keep_kernel, "keep", shape((rows, width // 2), BF16), scalars=1, operands=2)(
+    theirs = [lax.ppermute(value, "tp", pairwise("tp", 1)) for value in other]
+    kept = call(keep_kernel, "keep", (piece,) * PIECES, scalars=1, operands=2)(
         jnp.reshape(core, (1,)), gate_out, out_weight
     )
-    theirs, back = lax.optimization_barrier((theirs, back))
-    mine = (mine.astype(F32) + theirs.astype(F32)).astype(BF16)
+    mine = [
+        (a.astype(F32) + b.astype(F32)).astype(BF16) for a, b in zip(kept, theirs, strict=True)
+    ]
     step = 2
-    got = lax.ppermute(mine, "tp", pairwise("tp", step))
-
+    got = [lax.ppermute(value, "tp", pairwise("tp", step)) for value in mine]
+
+    grad_mixed, lags, tables = call(
+        functools.partial(lags_kernel, group),
+        "lags",
+        (
+            shape((rows, chans), BF16),
+            shape((count, chans), F32),
+            shape((chans // LANES, count * LANES, 2 * LANES), BF16),
+        ),
+        [pltpu.VMEM((count * LANES, (rows // LANES) * LANES), BF16)],
+        operands=4,
+    )(long_filter, grad_gate, feat, gated)
+    n_ctx = lax.axis_size("ctx")
+    by_pairs = n_ctx & (n_ctx - 1) == 0
     grad_in, sums = call(
         functools.partial(backward_kernel, group),
         "backward",
-        (shape((3, rows, chans), BF16), shape((24, chans), F32)),
+        (shape((3, rows, chans), BF16), shape((32, chans), BF16 if by_pairs else F32)),
         [
             pltpu.VMEM((3, rows + 16, LANES), F32),
             pltpu.VMEM((rows + LANES, LANES), BF16),
             pltpu.VMEM((3, rows + 8, LANES), F32),
-            table,
-            pltpu.VMEM((count * LANES, (rows // LANES) * LANES), BF16),
         ],
-        operands=8,
-        cost=200_000_000,
-    )(signal, short_filter, long_filter, halo, grad_gate, mixed, gated, back)
-
-    n_ctx = lax.axis_size("ctx")
-    if n_ctx & (n_ctx - 1) == 0:
+        operands=12,
+    )(
+        signal, short_filter, long_filter, halo, grad_gate, mixed, feat, gated, back,
+        grad_mixed, lags, tables,
+    )
+    if by_pairs:
         hop = 1
-        rest = jnp.zeros_like(sums)
-        while hop < n_ctx:
+        while hop < max(2, n_ctx // 4):
             rest = lax.ppermute(sums, "ctx", pairwise("ctx", hop))
+            sums = (sums.astype(F32) + rest.astype(F32)).astype(BF16)
             hop *= 2
-            if hop < n_ctx:
-                sums = sums + rest
+        terms = [sums]
+        for other_hop in range(hop, n_ctx, hop):
+            terms.append(lax.ppermute(sums, "ctx", pairwise("ctx", other_hop)))
     else:
-        sums = lax.psum(sums, "ctx")
-        rest = jnp.zeros_like(sums)
-    got, sums, rest = lax.optimization_barrier((got, sums, rest))
-    mine = (mine.astype(F32) + got.astype(F32)).astype(BF16)
+        terms = [lax.psum(sums, "ctx")]
+    got, terms[:4] = lax.optimization_barrier((got, terms[:4]))
+    mine = [
+        (a.astype(F32) + b.astype(F32)).astype(BF16) for a, b in zip(mine, got, strict=True)
+    ]
     step *= 2
     while step < n_tp:
-        got = lax.ppermute(mine, "tp", pairwise("tp", step))
-        mine = (mine.astype(F32) + got.astype(F32)).astype(BF16)
+        got = [lax.ppermute(value, "tp", pairwise("tp", step)) for value in mine]
+        mine = [
+            (a.astype(F32) + b.astype(F32)).astype(BF16) for a, b in zip(mine, got, strict=True)
+        ]
         step *= 2
-    sibling = lax.ppermute(mine, "tp", pairwise("tp", 1))
+    sibling = [lax.ppermute(value, "tp", pairwise("tp", 1)) for value in mine]
     result = jnp.where(
         core == 0,
-        jnp.concatenate([mine, sibling], axis=1),
-        jnp.concatenate([sibling, mine], axis=1),
+        jnp.concatenate(mine + sibling, axis=1),
+        jnp.concatenate(sibling + mine, axis=1),
     )
     grad_short, grad_long = call(
         functools.partial(
@@ -456,8 +500,8 @@
         ),
         "unpack",
         (shape((3, 3, chans), F32), shape((groups, span), F32)),
-        operands=2,
-    )(sums, rest)
+        operands=len(terms),
+    )(*terms)
     return (result, grad_in.transpose(1, 0, 2), grad_short, grad_long)
 
 

time: 65.8 us -> 58.9 us (0.90)
  the two profiles are of different devices: /device:TPU:25 before, /device:TPU:0 now
where the time goes in v3:
time: 58.9 us; the launch traced here: 58.7 us
  Pallas kernels  26.9 us (46%)
  starting transfers between devices  17.1 us (29%)
  waiting for transfers between devices  11.6 us (20%)
  other arithmetic  2.34 us (4%)
  between operations  0.75 us (1%)
    pallas_call x1, Pallas kernels, local(): call(functools.partial(backward_kernel, group), 'backward', (shape((3, ro...  6.87 us
    ppermute x2, starting transfers between devices, shifted(): lax.ppermute(value, axis, [(source, source + steps) for source in range(i...  6.14 us
    ppermute x3, waiting for transfers between devices, local(): terms.append(lax.ppermute(sums, 'ctx', pairwise('ctx', other_hop)))  6.06 us
    pallas_call x1, Pallas kernels, local(): call(grad_gate_kernel, 'grad_gate', (shape((rows, chans), F32), shape((LA...  5.83 us
    pallas_call x1, Pallas kernels, local(): call(functools.partial(lags_kernel, group), 'lags', (shape((rows, chans),...  5.51 us
    pallas_call x1, Pallas kernels, local(): call(functools.partial(forward_kernel, group), 'forward', (piece,) * PIEC...  5.05 us
    ppermute x3, starting transfers between devices, local(): terms.append(lax.ppermute(sums, 'ctx', pairwise('ctx', other_hop)))  4.95 us
    ppermute x1, starting transfers between devices, local(): rest = lax.ppermute(sums, 'ctx', pairwise('ctx', hop))  2.63 us
  transfers between devices with their start and end apart: 12, of which 8 were waited for; matrix products, arithmetic and copies ran while one was open for 1% of the time, Pallas kernels for 34%

profile of v3, /device:TPU:0, one launch (start us, length us, event | category | flops | bytes accessed | tf_op | source)
XLA Modules:
  0.0 58.7 jit_solution(8209592803045240497)
XLA Ops:
  0.6 1.7 %tail.1 = (bf16[144,1024]{1,0:T(8,128)(2,1)S(1)}, bf16[3,256,1024]{2,1,0:T(8,128)(2,1)S(1)}, f32[3,3,1024]{2,1,0:T(4,128)S(1)}, bf16[64,128]{1,0:T(8,128)(2,1)S(1)}) custom-call(bf16[3,256,1024]{2,1,0:T(8,128)(2,1)} %bitcast.4, f32[3,3,1024]{2,1,0:T(4,128)} %taps_hbm.1, bf16[64,128]{1,0:T(8,128)(2,1)} %filt_hbm.1), custom_call_target="tpu_custom_call" | custom-call | bytes 1024 | tf_op jit(solution)/shard_map/tail/pallas_call | solution.py:385
  2.4 4.9 %collective-permute-start = (bf16[144,1024]{1,0:T(8,128)(2,1)S(1)}, bf16[144,1024]{1,0:T(8,128)(2,1)S(1)}, u32[]{:S(2)}, u32[]{:S(2)}) collective-permute-start(bf16[144,1024]{1,0:T(8,128)(2,1)S(1)} %get-tuple-element.35), channel_id=1, source_target_pairs={{0,4},{4,8},{8,12},{12,16},{16,20},{20,24},{24,28},{1,5},{5,9},{9,... | collective-permute-start | bytes 884744 | tf_op jit(solution)/shard_map/ppermute | solution.py:26
  7.2 5.8 %grad_gate.1 = (f32[256,1024]{1,0:T(8,128)S(1)}, bf16[160,1024]{1,0:T(8,128)(2,1)S(1)}, bf16[1024,4096]{1,0:T(8,128)(2,1)S(1)}) custom-call(bf16[256,4096]{1,0:T(8,128)(2,1)} %c_hbm.1, bf16[1024,4096]{1,0:T(8,128)(2,1)} %w_hbm.1, bf16[3,256,1024]{2,1,0:T(8,128)(2,1)S(1)} %get-tuple-element.32.x_ref, f32[3,3,1024]{2,1,0:T(4,128)S(1)} %get-tuple-element.33.taps_ref), custom_call_target="tpu_custom_call" | custom-call | bytes 1024 | tf_op jit(solution)/shard_map/grad_gate/pallas_call | solution.py:398
  13.1 0.4 collective-permute-done.halo_ref
  13.5 5.0 %forward.1 = (bf16[256,1024]{1,0:T(8,128)(2,1)S(1)}, bf16[256,1024]{1,0:T(8,128)(2,1)S(1)}, bf16[256,1024]{1,0:T(8,128)(2,1)S(1)}, f32[256,1024]{1,0:T(8,128)S(1...) custom-call(s32[1]{0:T(128)} %bitcast.1.which_ref, bf16[3,256,1024]{2,1,0:T(8,128)(2,1)S(1)} %get-tuple-element.32.x_ref, ...), custom_call_target="tpu_custom_call" | custom-call | bytes 1024 | tf_op jit(solution)/shard_map/forward/pallas_call | solution.py:418
  18.5 0.1 collective-permute-start.1
  18.6 0.5 collective-permute-start.3
  19.1 1.3 %collective-permute-start.5 = (bf16[160,1024]{1,0:T(8,128)(2,1)S(1)}, bf16[160,1024]{1,0:T(8,128)(2,1)S(1)}, u32[]{:S(2)}, u32[]{:S(2)}) collective-permute-start(bf16[160,1024]{1,0:T(8,128)(2,1)S(1)} %get-tuple-element.46), channel_id=1, source_target_pairs={{4,0},{8,4},{12,8},{16,12},{20,16},{24,20},{28,24},{5,1},{9,5},{13... | collective-permute-start | bytes 983048 | tf_op jit(solution)/shard_map/ppermute | solution.py:26
  20.4 1.3 %keep.1 = (bf16[256,1024]{1,0:T(8,128)(2,1)S(1)}, bf16[256,1024]{1,0:T(8,128)(2,1)S(1)}) custom-call(s32[1]{0:T(128)} %bitcast.which_ref, bf16[256,1024]{1,0:T(8,128)(2,1)S(1)} %get-tuple-element.37.gate_ref, bf16[1024,4096]{1,0:T(8,128)(2,1)S(1)} %get-tuple-element.36.w_ref), custom_call_target="tpu_custom_call" | custom-call | bytes 1024 | tf_op jit(solution)/shard_map/keep/pallas_call | solution.py:433
  21.7 0.0 collective-permute-done.1
  21.7 0.2 add_convert_fusion.3
  21.9 1.6 %collective-permute-start.2 = (bf16[256,1024]{1,0:T(8,128)(2,1)S(1)}, bf16[256,1024]{1,0:T(8,128)(2,1)S(1)}, u32[]{:S(2)}, u32[]{:S(2)}) collective-permute-start(bf16[256,1024]{1,0:T(8,128)(2,1)S(1)} %add_convert_fusion.3), channel_id=1, source_target_pairs={{0,2},{1,3},{2,0},{3,1},{4,6},{5,7},{6,4},{7,5},{8,10},{9,11},{10,... | collective-permute-start | bytes 1572872 | tf_op jit(solution)/shard_map/ppermute | solution.py:440
  23.5 0.0 collective-permute-done.3
  23.5 0.2 add_convert_fusion.2
  23.7 0.6 collective-permute-start.4
  24.3 5.5 %lags.1 = (bf16[256,1024]{1,0:T(8,128)(2,1)S(1)}, f32[8,1024]{1,0:T(8,128)S(1)}, bf16[8,1024,256]{2,1,0:T(8,128)(2,1)S(1)}) custom-call(bf16[64,128]{1,0:T(8,128)(2,1)S(1)} %get-tuple-element.34.filt_ref, f32[256,1024]{1,0:T(8,128)S(1)} %get-tuple-element.42.gg_ref, f32[3,256,1024]{2,1,0:T(8,128)S(1)} %get-tuple-element.44.feat_ref, ...), custom_call_target="tpu_custom_call" | custom-call | bytes 1024 | tf_op jit(solution)/shard_map/lags/pallas_call | solution.py:442
  29.8 1.7 %collective-permute-done.5.back_ref = bf16[160,1024]{1,0:T(8,128)(2,1)S(1)} collective-permute-done((bf16[160,1024]{1,0:T(8,128)(2,1)S(1)}, bf16[160,1024]{1,0:T(8,128)(2,1)S(1)}, u32[]{:S(2)}, u32[]{:S(2)}) %collective-permute-start.5) | collective-permute-done | bytes 327712 | tf_op jit(solution)/shard_map/ppermute | solution.py:26
  31.4 6.9 %backward.1 = (bf16[3,256,1024]{2,1,0:T(8,128)(2,1)}, bf16[32,1024]{1,0:T(8,128)(2,1)S(1)}) custom-call(bf16[3,256,1024]{2,1,0:T(8,128)(2,1)S(1)} %get-tuple-element.32.x_ref, f32[3,3,1024]{2,1,0:T(4,128)S(1)} %get-tuple-element.33.taps_ref, bf16[64,128]{1,0:T(8,128)(2,1)S(1)} %get-tuple-element.34.filt_ref, ...), custom_call_target="tpu_custom_call" | custom-call | bytes 1024 | tf_op jit(solution)/shard_map/backward/pallas_call | solution.py:455
  38.3 2.6 %collective-permute-start.6 = (bf16[32,1024]{1,0:T(8,128)(2,1)S(1)}, bf16[32,1024]{1,0:T(8,128)(2,1)S(1)}, u32[]{:S(2)}, u32[]{:S(2)}) collective-permute-start(bf16[32,1024]{1,0:T(8,128)(2,1)S(1)} %get-tuple-element.50), channel_id=1, source_target_pairs={{0,4},{4,0},{8,12},{12,8},{16,20},{20,16},{24,28},{28,24},{1,5},{5... | collective-permute-start | bytes 196616 | tf_op jit(solution)/shard_map/ppermute | solution.py:472
  40.9 2.2 %collective-permute-done.6 = bf16[32,1024]{1,0:T(8,128)(2,1)S(1)} collective-permute-done((bf16[32,1024]{1,0:T(8,128)(2,1)S(1)}, bf16[32,1024]{1,0:T(8,128)(2,1)S(1)}, u32[]{:S(2)}, u32[]{:S(2)}) %collective-permute-start.6) | collective-permute-done | bytes 65568 | tf_op jit(solution)/shard_map/ppermute | solution.py:472
  43.2 2.4 %collective-permute-start.7 = (bf16[32,1024]{1,0:T(8,128)(2,1)S(1)}, bf16[32,1024]{1,0:T(8,128)(2,1)S(1)}, u32[]{:S(2)}, u32[]{:S(2)}) collective-permute-start(bf16[32,1024]{1,0:T(8,128)(2,1)S(1)} %add_convert_fusion.4.refs_0_), channel_id=1, source_target_pairs={{0,8},{4,12},{8,0},{12,4},{16,24},{20,28},{24,16},{28,20},{1,9},{5... | collective-permute-start | bytes 196616 | tf_op jit(solution)/shard_map/ppermute | solution.py:477
  45.6 2.6 %collective-permute-start.8 = (bf16[32,1024]{1,0:T(8,128)(2,1)S(1)}, bf16[32,1024]{1,0:T(8,128)(2,1)S(1)}, u32[]{:S(2)}, u32[]{:S(2)}) collective-permute-start(bf16[32,1024]{1,0:T(8,128)(2,1)S(1)} %add_convert_fusion.4.refs_0_), channel_id=1, source_target_pairs={{0,16},{4,20},{8,24},{12,28},{16,0},{20,4},{24,8},{28,12},{1,17},{... | collective-permute-start | bytes 196616 | tf_op jit(solution)/shard_map/ppermute | solution.py:477
  48.1 0.0 collective-permute-start.9
  48.2 0.3 collective-permute-done.7.refs_1_
  48.4 3.7 %collective-permute-done.8.refs_2_ = bf16[32,1024]{1,0:T(8,128)(2,1)S(1)} collective-permute-done((bf16[32,1024]{1,0:T(8,128)(2,1)S(1)}, bf16[32,1024]{1,0:T(8,128)(2,1)S(1)}, u32[]{:S(2)}, u32[]{:S(2)}) %collective-permute-start.8) | collective-permute-done | bytes 65568 | tf_op jit(solution)/shard_map/ppermute | solution.py:477
  52.1 2.1 %collective-permute-done.9.refs_3_ = bf16[32,1024]{1,0:T(8,128)(2,1)S(1)} collective-permute-done((bf16[32,1024]{1,0:T(8,128)(2,1)S(1)}, bf16[32,1024]{1,0:T(8,128)(2,1)S(1)}, u32[]{:S(2)}, u32[]{:S(2)}) %collective-permute-start.9) | collective-permute-done | bytes 65568 | tf_op jit(solution)/shard_map/ppermute | solution.py:477
  54.2 0.0 collective-permute-done.2
  54.2 0.0 collective-permute-done.4
  54.2 0.2 add_convert_fusion
  54.4 0.1 collective-permute-start.11
  54.5 0.2 add_convert_fusion.1
  54.7 0.6 collective-permute-start.10
  55.3 0.7 %unpack.1 = (f32[3,3,1024]{2,1,0:T(4,128)}, f32[64,128]{1,0:T(8,128)}) custom-call(bf16[32,1024]{1,0:T(8,128)(2,1)S(1)} %add_convert_fusion.4.refs_0_, bf16[32,1024]{1,0:T(8,128)(2,1)S(1)} %collective-permute-done.7.refs_1_, bf16[32,1024]{1,0:T(8,128)(2,1)S(1)} %collective-permute-done.8.refs_2_, bf16[32,1024]{1,0:T(8,128)(2,1)S(1)} %collective-permute-done.9.refs_3_), custom_call_target="tpu_custom_call" | custom-call | bytes 1024 | tf_op jit(solution)/shard_map/unpack/pallas_call | solution.py:497
  55.9 0.5 collective-permute-done.11
  56.4 0.7 %collective-permute-done.10 = bf16[256,1024]{1,0:T(8,128)(2,1)S(1)} collective-permute-done((bf16[256,1024]{1,0:T(8,128)(2,1)S(1)}, bf16[256,1024]{1,0:T(8,128)(2,1)S(1)}, u32[]{:S(2)}, u32[]{:S(2)}) %collective-permute-start.10) | collective-permute-done | bytes 524320 | tf_op jit(solution)/shard_map/ppermute | solution.py:491
  57.1 1.6 %maximum_select_fusion = bf16[256,4096]{1,0:T(8,128)(2,1)} fusion(bf16[256,1024]{1,0:T(8,128)(2,1)S(1)} %collective-permute-done.11, bf16[256,1024]{1,0:T(8,128)(2,1)S(1)} %collective-permute-done.10, bf16[256,1024]{1,0:T(8,128)(2,1)S(1)} %add_convert_fusion, bf16[256,1024]{1,0:T(8,128)(2,1)S(1)} %add_convert_fusion.1, pred[]{:T(512)S(6)} %eq.3), kind=kLoop, calls=%fused_computation | loop fusion | flops 17825792 | bytes 4194305 | tf_op jit(solution)/shard_map/jit(_where)/select_n | solution.py:492
  (1 shorter events, 0.0 us)
Async XLA Ops:
  2.4 11.1 %collective-permute-start = (bf16[144,1024]{1,0:T(8,128)(2,1)S(1)}, bf16[144,1024]{1,0:T(8,128)(2,1)S(1)}, u32[]{:S(2)}, u32[]{:S(2)}) collective-permute-start(bf16[144,1024]{1,0:T(8,128)(2,1)S(1)} %get-tuple-element.35), channel_id=1, source_target_pairs={{0,4},{4,8},{8,12},{12,16},{16,20},{20,24},{24,28},{1,5},{5,9},{9,... | collective-permute-start | bytes 884744 | tf_op jit(solution)/shard_map/ppermute | solution.py:26
  18.5 3.2 %collective-permute-start.1 = (bf16[256,1024]{1,0:T(8,128)(2,1)S(1)}, bf16[256,1024]{1,0:T(8,128)(2,1)S(1)}, u32[]{:S(2)}, u32[]{:S(2)}) collective-permute-start(bf16[256,1024]{1,0:T(8,128)(2,1)S(1)} %get-tuple-element.39), channel_id=1, source_target_pairs={{0,1},{1,0},{2,3},{3,2},{4,5},{5,4},{6,7},{7,6},{8,9},{9,8},{10,11... | collective-permute-start | bytes 1572872 | tf_op jit(solution)/shard_map/ppermute | solution.py:432
  18.6 4.9 %collective-permute-start.3 = (bf16[256,1024]{1,0:T(8,128)(2,1)S(1)}, bf16[256,1024]{1,0:T(8,128)(2,1)S(1)}, u32[]{:S(2)}, u32[]{:S(2)}) collective-permute-start(bf16[256,1024]{1,0:T(8,128)(2,1)S(1)} %get-tuple-element.41), channel_id=1, source_target_pairs={{0,1},{1,0},{2,3},{3,2},{4,5},{5,4},{6,7},{7,6},{8,9},{9,8},{10,11... | collective-permute-start | bytes 1572872 | tf_op jit(solution)/shard_map/ppermute | solution.py:432
  19.1 12.3 %collective-permute-start.5 = (bf16[160,1024]{1,0:T(8,128)(2,1)S(1)}, bf16[160,1024]{1,0:T(8,128)(2,1)S(1)}, u32[]{:S(2)}, u32[]{:S(2)}) collective-permute-start(bf16[160,1024]{1,0:T(8,128)(2,1)S(1)} %get-tuple-element.46), channel_id=1, source_target_pairs={{4,0},{8,4},{12,8},{16,12},{20,16},{24,20},{28,24},{5,1},{9,5},{13... | collective-permute-start | bytes 983048 | tf_op jit(solution)/shard_map/ppermute | solution.py:26
  21.9 32.3 %collective-permute-start.2 = (bf16[256,1024]{1,0:T(8,128)(2,1)S(1)}, bf16[256,1024]{1,0:T(8,128)(2,1)S(1)}, u32[]{:S(2)}, u32[]{:S(2)}) collective-permute-start(bf16[256,1024]{1,0:T(8,128)(2,1)S(1)} %add_convert_fusion.3), channel_id=1, source_target_pairs={{0,2},{1,3},{2,0},{3,1},{4,6},{5,7},{6,4},{7,5},{8,10},{9,11},{10,... | collective-permute-start | bytes 1572872 | tf_op jit(solution)/shard_map/ppermute | solution.py:440
  23.7 30.5 %collective-permute-start.4 = (bf16[256,1024]{1,0:T(8,128)(2,1)S(1)}, bf16[256,1024]{1,0:T(8,128)(2,1)S(1)}, u32[]{:S(2)}, u32[]{:S(2)}) collective-permute-start(bf16[256,1024]{1,0:T(8,128)(2,1)S(1)} %add_convert_fusion.2), channel_id=1, source_target_pairs={{0,2},{1,3},{2,0},{3,1},{4,6},{5,7},{6,4},{7,5},{8,10},{9,11},{10,... | collective-permute-start | bytes 1572872 | tf_op jit(solution)/shard_map/ppermute | solution.py:440
  38.3 4.9 %collective-permute-start.6 = (bf16[32,1024]{1,0:T(8,128)(2,1)S(1)}, bf16[32,1024]{1,0:T(8,128)(2,1)S(1)}, u32[]{:S(2)}, u32[]{:S(2)}) collective-permute-start(bf16[32,1024]{1,0:T(8,128)(2,1)S(1)} %get-tuple-element.50), channel_id=1, source_target_pairs={{0,4},{4,0},{8,12},{12,8},{16,20},{20,16},{24,28},{28,24},{1,5},{5... | collective-permute-start | bytes 196616 | tf_op jit(solution)/shard_map/ppermute | solution.py:472
  43.2 5.2 %collective-permute-start.7 = (bf16[32,1024]{1,0:T(8,128)(2,1)S(1)}, bf16[32,1024]{1,0:T(8,128)(2,1)S(1)}, u32[]{:S(2)}, u32[]{:S(2)}) collective-permute-start(bf16[32,1024]{1,0:T(8,128)(2,1)S(1)} %add_convert_fusion.4.refs_0_), channel_id=1, source_target_pairs={{0,8},{4,12},{8,0},{12,4},{16,24},{20,28},{24,16},{28,20},{1,9},{5... | collective-permute-start | bytes 196616 | tf_op jit(solution)/shard_map/ppermute | solution.py:477
  45.6 6.6 %collective-permute-start.8 = (bf16[32,1024]{1,0:T(8,128)(2,1)S(1)}, bf16[32,1024]{1,0:T(8,128)(2,1)S(1)}, u32[]{:S(2)}, u32[]{:S(2)}) collective-permute-start(bf16[32,1024]{1,0:T(8,128)(2,1)S(1)} %add_convert_fusion.4.refs_0_), channel_id=1, source_target_pairs={{0,16},{4,20},{8,24},{12,28},{16,0},{20,4},{24,8},{28,12},{1,17},{... | collective-permute-start | bytes 196616 | tf_op jit(solution)/shard_map/ppermute | solution.py:477
  48.1 6.1 %collective-permute-start.9 = (bf16[32,1024]{1,0:T(8,128)(2,1)S(1)}, bf16[32,1024]{1,0:T(8,128)(2,1)S(1)}, u32[]{:S(2)}, u32[]{:S(2)}) collective-permute-start(bf16[32,1024]{1,0:T(8,128)(2,1)S(1)} %add_convert_fusion.4.refs_0_), channel_id=1, source_target_pairs={{0,24},{4,28},{8,16},{12,20},{16,8},{20,12},{24,0},{28,4},{1,25},{... | collective-permute-start | bytes 196616 | tf_op jit(solution)/shard_map/ppermute | solution.py:477
  54.4 2.0 %collective-permute-start.11 = (bf16[256,1024]{1,0:T(8,128)(2,1)S(1)}, bf16[256,1024]{1,0:T(8,128)(2,1)S(1)}, u32[]{:S(2)}, u32[]{:S(2)}) collective-permute-start(bf16[256,1024]{1,0:T(8,128)(2,1)S(1)} %add_convert_fusion), channel_id=1, source_target_pairs={{0,1},{1,0},{2,3},{3,2},{4,5},{5,4},{6,7},{7,6},{8,9},{9,8},{10,11... | collective-permute-start | bytes 1572872 | tf_op jit(solution)/shard_map/ppermute | solution.py:491
  54.7 2.4 %collective-permute-start.10 = (bf16[256,1024]{1,0:T(8,128)(2,1)S(1)}, bf16[256,1024]{1,0:T(8,128)(2,1)S(1)}, u32[]{:S(2)}, u32[]{:S(2)}) collective-permute-start(bf16[256,1024]{1,0:T(8,128)(2,1)S(1)} %add_convert_fusion.1), channel_id=1, source_target_pairs={{0,1},{1,0},{2,3},{3,2},{4,5},{5,4},{6,7},{7,6},{8,9},{9,8},{10,11... | collective-permute-start | bytes 1572872 | tf_op jit(solution)/shard_map/ppermute | solution.py:491

commit v4 on v3

--- a/solution.py
+++ b/solution.py
@@ -240,7 +240,18 @@
     project(which_ref[0], gate_ref, w_ref, keep_refs)
 
 
-def lags_kernel(group, filt_ref, gg_ref, feat_ref, gext_ref, gm_ref, lags_ref, tables_ref, left):
+def short_sums(grad, ext_ref, part):
+    rows = grad.shape[0]
+    return [
+        jnp.sum(grad * ext_ref[part, 8 - lag : 8 - lag + rows, :], axis=0, keepdims=True)
+        for lag in range(3)
+    ]
+
+
+def lags_kernel(
+    group, filt_ref, x_ref, halo_ref, gg_ref, mixed_ref, feat_ref, gext_ref,
+    gm_ref, gq_ref, lags_ref, tables_ref, left, ext,
+):
     rows, chans = gg_ref.shape
     blocks = rows // LANES
     count = LANES // group
@@ -250,6 +261,11 @@
         fill_table(tables_ref.at[j], filt.astype(F32), False)
         grad_mixed = (gg_ref[:, lanes] * feat_ref[0, :, lanes]).astype(BF16)
         gm_ref[:, lanes] = grad_mixed
+        grad_query = (gg_ref[:, lanes] * mixed_ref[:, lanes]).astype(BF16)
+        gq_ref[:, lanes] = grad_query
+        ext[0, 6:8, :] = halo_ref[LANES : LANES + 2, lanes].astype(F32)
+        ext[0, 8:, :] = x_ref[0, :, lanes].astype(F32)
+        sums = short_sums(grad_query.astype(F32), ext, 0)
         lane = group_of_lane(LANES, group)
         for g in range(count):
             for b in range(blocks):
@@ -272,80 +288,103 @@
             ring = jnp.where(early, own[:, 0:LANES], own[:, LANES:])
             ring = pltpu.roll(ring, 0, 1, stride=1, stride_axis=0)
             lag_rows.append(jnp.sum(ring, axis=0, keepdims=True))
-        lags_ref[:, lanes] = pltpu.roll(jnp.concatenate(lag_rows, axis=0), 1, 1)
+        lags = pltpu.roll(jnp.concatenate(lag_rows, axis=0), 1, 1)
+        sums.append(jnp.zeros((16 - count - 3, LANES), F32))
+        lags_ref[:, lanes] = jnp.concatenate([lags] + sums, axis=0)
 
     each_tile(chans, tile)
 
 
+def next_rows(ext_ref, taps_ref, x_ref, back_ref, lanes, parts):
+    rows = x_ref.shape[1]
+    span = LANES + RIM
+    outs = []
+    for part in parts:
+        recent = x_ref[part, rows - RIM :, lanes].astype(F32)
+        at = span + 2 * part
+        ext_ref[part, 0:8, :] = recent[RIM - 8 :]
+        ext_ref[part, 8:10, :] = back_ref[at : at + 2, lanes].astype(F32)
+        outs.append(feature(ext_ref, taps_ref, lanes, part, 0, 2))
+    high = back_ref[span + 6 : span + 8, lanes].astype(F32)
+    low = back_ref[span + 8 : span + 10, lanes].astype(F32)
+    return outs, high + low
+
+
+def next_mixed(back_ref, lanes, grad, query):
+    head = back_ref[0 : LANES + RIM, lanes].astype(F32)
+    first = (grad * query).astype(BF16).astype(F32)
+    return jnp.concatenate([first, head[2:]], axis=0)
+
+
 def backward_kernel(
-    group, x_ref, taps_ref, filt_ref, halo_ref, gg_ref, mixed_ref, feat_ref, gext_ref, back_ref,
-    gm_ref, lags_ref, tables_ref, gin_ref, sums_ref, ext, mext, gf,
+    group, x_ref, taps_ref, halo_ref, feat_ref, back_ref, gm_ref, lags_ref, tables_ref,
+    gkv_ref, sums_ref, ext, mext, near,
 ):
     _, rows, chans = x_ref.shape
     blocks = rows // LANES
     count = LANES // group
-    span = LANES + RIM
 
     def tile(j, lanes):
-        for part in range(3):
+        for part in range(1, 3):
             at = LANES + 2 * part
             ext[part, 6:8, :] = halo_ref[at : at + 2, lanes].astype(F32)
-            ext[part, 8 : 8 + rows, :] = x_ref[part, :, lanes].astype(F32)
-            at = span + 2 * part
-            ext[part, 8 + rows : 10 + rows, :] = back_ref[at : at + 2, lanes].astype(F32)
-        keyed = feat_ref[1, :, lanes]
-        valued = feat_ref[2, :, lanes]
-        query_next = feature(ext, taps_ref, lanes, 0, rows, 2)
-        keyed_next = feature(ext, taps_ref, lanes, 1, rows, 2)
-        valued_next = feature(ext, taps_ref, lanes, 2, rows, 2)
-        gg_next = back_ref[span + 6 : span + 8, lanes].astype(F32) + back_ref[
-            span + 8 : span + 10, lanes
-        ].astype(F32)
-        head = back_ref[0:span, lanes].astype(F32)
-        mixed_next = (gg_next * query_next).astype(BF16).astype(F32)
-        head = jnp.concatenate([mixed_next, head[2:]], axis=0)
+            ext[part, 8:, :] = x_ref[part, :, lanes].astype(F32)
+        (query_next,), gg_next = next_rows(near, taps_ref, x_ref, back_ref, lanes, (0,))
+        head = next_mixed(back_ref, lanes, gg_next, query_next)
         mext[0:rows, :] = gm_ref[:, lanes]
         mext[rows:, :] = head[0:LANES].astype(BF16)
         wide = jnp.dot(
             tables_ref[j], side_by_side(mext, blocks, slice(None)), preferred_element_type=F32
         )
         grad_gated = pick_groups(wide, group, blocks)
+        sums = [None] * 3
+        for part in range(1, 3):
+            grad = (grad_gated * feat_ref[3 - part, :, lanes]).astype(BF16)
+            gkv_ref[part - 1, :, lanes] = grad
+            sums[part] = short_sums(grad.astype(F32), ext, part)
+        early = lags_ref[:, lanes]
+        flat = [early[0:count]]
+        for lag in range(3):
+            flat += [early[count + lag : count + lag + 1], sums[1][lag], sums[2][lag]]
+        flat.append(jnp.zeros((32 - count - 9, LANES), F32))
+        sums_ref[:, lanes] = jnp.concatenate(flat, axis=0).astype(sums_ref.dtype)
+
+    each_tile(chans, tile)
+
+
+def inputs_kernel(
+    group, x_ref, taps_ref, filt_ref, gext_ref, back_ref, gq_ref, gkv_ref, gin_ref, near, gf
+):
+    _, rows, chans = x_ref.shape
+    count = LANES // group
+
+    def tile(j, lanes):
+        (query, keyed, valued), grad = next_rows(
+            near, taps_ref, x_ref, back_ref, lanes, (0, 1, 2)
+        )
+        head = next_mixed(back_ref, lanes, grad, query)
         filt = filt_ref[pl.ds(pl.multiple_of(j * count, count), count), :]
         taps = spread_taps(filt, group, False)
         taps_turned = spread_taps(filt, group, True)
         recent = gext_ref[rows:, lanes].astype(F32)
-        gated_next = (keyed_next * valued_next).astype(BF16).astype(F32)
-        recent = jnp.concatenate([recent, gated_next], axis=0)
-        grads_next, mixes_next = [], []
+        recent = jnp.concatenate([recent, (keyed * valued).astype(BF16).astype(F32)], axis=0)
+        gated, mixed = [], []
         for t in range(2):
-            grads_next.append(jnp.sum(taps * head[t : t + LANES], axis=0, keepdims=True))
-            mixes_next.append(
+            gated.append(jnp.sum(taps * head[t : t + LANES], axis=0, keepdims=True))
+            mixed.append(
                 jnp.sum(taps_turned * recent[t + 1 : t + 1 + LANES], axis=0, keepdims=True)
             )
-        grad_next = jnp.concatenate(grads_next, axis=0)
-        mix_next = jnp.concatenate(mixes_next, axis=0)
-        parts = (
-            (gg_ref[:, lanes] * mixed_ref[:, lanes]).astype(BF16).astype(F32),
-            (grad_gated * valued).astype(BF16).astype(F32),
-            (grad_gated * keyed).astype(BF16).astype(F32),
-        )
-        following = (gg_next * mix_next, grad_next * valued_next, grad_next * keyed_next)
-        short_rows = [[None] * 3 for _ in range(3)]
+        gated, mixed = jnp.concatenate(gated, axis=0), jnp.concatenate(mixed, axis=0)
+        following = (grad * mixed, gated * valued, gated * keyed)
         for part in range(3):
-            gf[part, 0:rows, :] = parts[part]
+            own = gq_ref[:, lanes] if part == 0 else gkv_ref[part - 1, :, lanes]
+            gf[part, 0:rows, :] = own.astype(F32)
             gf[part, rows : rows + 2, :] = following[part].astype(BF16).astype(F32)
-            total = taps_ref[0, part : part + 1, lanes] * parts[part]
+            total = taps_ref[0, part : part + 1, lanes] * gf[part, 0:rows, :]
             for lag in range(1, 3):
                 tap = taps_ref[lag, part : part + 1, lanes]
                 total = total + tap * gf[part, lag : lag + rows, :]
             gin_ref[part, :, lanes] = total.astype(BF16)
-            for lag in range(3):
-                short_rows[lag][part] = jnp.sum(
-                    parts[part] * ext[part, 8 - lag : 8 - lag + rows, :], axis=0, keepdims=True
-                )
-        flat = [lags_ref[:, lanes]] + [short_rows[lag][part] for lag in range(3) for part in range(3)]
-        flat.append(jnp.zeros((15, LANES), F32))
-        sums_ref[:, lanes] = jnp.concatenate(flat, axis=0).astype(sums_ref.dtype)
 
     each_tile(chans, tile)
 
@@ -439,45 +478,51 @@
     step = 2
     got = [lax.ppermute(value, "tp", pairwise("tp", step)) for value in mine]
 
-    grad_mixed, lags, tables = call(
+    ext = pltpu.VMEM((3, rows + 8, LANES), F32)
+    near = pltpu.VMEM((3, 16, LANES), F32)
+    grad_mixed, grad_query, lags, tables = call(
         functools.partial(lags_kernel, group),
         "lags",
         (
             shape((rows, chans), BF16),
-            shape((count, chans), F32),
+            shape((rows, chans), BF16),
+            shape((16, chans), F32),
             shape((chans // LANES, count * LANES, 2 * LANES), BF16),
         ),
-        [pltpu.VMEM((count * LANES, (rows // LANES) * LANES), BF16)],
-        operands=4,
-    )(long_filter, grad_gate, feat, gated)
+        [pltpu.VMEM((count * LANES, (rows // LANES) * LANES), BF16), ext],
+        operands=7,
+    )(long_filter, signal, halo, grad_gate, mixed, feat, gated)
     n_ctx = lax.axis_size("ctx")
     by_pairs = n_ctx & (n_ctx - 1) == 0
-    grad_in, sums = call(
+    grad_rest, sums = call(
         functools.partial(backward_kernel, group),
         "backward",
-        (shape((3, rows, chans), BF16), shape((32, chans), BF16 if by_pairs else F32)),
-        [
-            pltpu.VMEM((3, rows + 16, LANES), F32),
-            pltpu.VMEM((rows + LANES, LANES), BF16),
-            pltpu.VMEM((3, rows + 8, LANES), F32),
-        ],
-        operands=12,
-    )(
-        signal, short_filter, long_filter, halo, grad_gate, mixed, feat, gated, back,
-        grad_mixed, lags, tables,
-    )
+        (shape((2, rows, chans), BF16), shape((32, chans), BF16 if by_pairs else F32)),
+        [ext, pltpu.VMEM((rows + LANES, LANES), BF16), near],
+        operands=8,
+    )(signal, short_filter, halo, feat, back, grad_mixed, lags, tables)
+    grad_in = call(
+        functools.partial(inputs_kernel, group),
+        "inputs",
+        shape((3, rows, chans), BF16),
+        [near, pltpu.VMEM((3, rows + 8, LANES), F32)],
+        operands=7,
+    )(signal, short_filter, long_filter, gated, back, grad_query, grad_rest)
     if by_pairs:
         hop = 1
-        while hop < max(2, n_ctx // 4):
-            rest = lax.ppermute(sums, "ctx", pairwise("ctx", hop))
-            sums = (sums.astype(F32) + rest.astype(F32)).astype(BF16)
-            hop *= 2
         terms = [sums]
-        for other_hop in range(hop, n_ctx, hop):
-            terms.append(lax.ppermute(sums, "ctx", pairwise("ctx", other_hop)))
+        while hop < n_ctx:
+            if len(terms) > 1:
+                pairs = [a.astype(F32) + b.astype(F32) for a, b in zip(terms[::2], terms[1::2])]
+                terms = [sum(pairs).astype(BF16)]
+            radix = min(4, n_ctx // hop)
+            terms += [
+                lax.ppermute(terms[0], "ctx", pairwise("ctx", i * hop)) for i in range(1, radix)
+            ]
+            hop *= radix
     else:
         terms = [lax.psum(sums, "ctx")]
-    got, terms[:4] = lax.optimization_barrier((got, terms[:4]))
+    got, terms, grad_in = lax.optimization_barrier((got, terms, grad_in))
     mine = [
         (a.astype(F32) + b.astype(F32)).astype(BF16) for a, b in zip(mine, got, strict=True)
     ]

time: 58.9 us -> 54.5 us (0.925)
  waiting for transfers between devices: 11.6 us -> 6.63 us
    ppermute x4, waiting for transfers between devices: 8.3 us -> 3.63 us  [local(): lax.ppermute(terms[0], 'ctx', pairwise('ctx', i * hop))]
    pallas_call x1 -> x2, Pallas kernels: 6.87 us -> 6.64 us  [the longest x1 3.55 us: local(): call(functools.partial(inputs_kernel, group), 'inputs', shape((3, rows, c...]
  transfers between devices with their start and end apart: 12 -> 12, of which waited for: 8 -> 6; matrix products, arithmetic and copies ran while one was open for 1% -> 1% of each run, Pallas kernels for 34% -> 37%
where the time goes in v4:
time: 54.5 us; the launch traced here: 54.3 us
  Pallas kernels  27 us (50%)
  starting transfers between devices  17.5 us (32%)
  waiting for transfers between devices  6.63 us (12%)
  other arithmetic  2.37 us (4%)
  between operations  0.76 us (1%)
    ppermute x4, starting transfers between devices, local(): lax.ppermute(terms[0], 'ctx', pairwise('ctx', i * hop))  8 us
    ppermute x2, starting transfers between devices, shifted(): lax.ppermute(value, axis, [(source, source + steps) for source in range(i...  6.14 us
    pallas_call x1, Pallas kernels, local(): call(grad_gate_kernel, 'grad_gate', (shape((rows, chans), F32), shape((LA...  5.82 us
    pallas_call x1, Pallas kernels, local(): call(functools.partial(lags_kernel, group), 'lags', (shape((rows, chans),...  5.82 us
    pallas_call x1, Pallas kernels, local(): call(functools.partial(forward_kernel, group), 'forward', (piece,) * PIEC...  5.05 us
    ppermute x4, waiting for transfers between devices, local(): lax.ppermute(terms[0], 'ctx', pairwise('ctx', i * hop))  3.63 us
    pallas_call x1, Pallas kernels, local(): call(functools.partial(inputs_kernel, group), 'inputs', shape((3, rows, c...  3.55 us
    pallas_call x1, Pallas kernels, local(): call(functools.partial(backward_kernel, group), 'backward', (shape((2, ro...  3.09 us
  transfers between devices with their start and end apart: 12, of which 6 were waited for; matrix products, arithmetic and copies ran while one was open for 1% of the time, Pallas kernels for 37%

profile of v4, /device:TPU:0, one launch (start us, length us, event | category | flops | bytes accessed | tf_op | source)
XLA Modules:
  0.0 54.3 jit_solution(17284070364027251942)
XLA Ops:
  0.6 1.7 %tail.1 = (bf16[144,1024]{1,0:T(8,128)(2,1)S(1)}, bf16[3,256,1024]{2,1,0:T(8,128)(2,1)S(1)}, f32[3,3,1024]{2,1,0:T(4,128)S(1)}, bf16[64,128]{1,0:T(8,128)(2,1)S(1)}) custom-call(bf16[3,256,1024]{2,1,0:T(8,128)(2,1)} %bitcast.4, f32[3,3,1024]{2,1,0:T(4,128)} %taps_hbm.1, bf16[64,128]{1,0:T(8,128)(2,1)} %filt_hbm.1), custom_call_target="tpu_custom_call" | custom-call | bytes 1024 | tf_op jit(solution)/shard_map/tail/pallas_call | solution.py:424
  2.4 4.9 %collective-permute-start = (bf16[144,1024]{1,0:T(8,128)(2,1)S(1)}, bf16[144,1024]{1,0:T(8,128)(2,1)S(1)}, u32[]{:S(2)}, u32[]{:S(2)}) collective-permute-start(bf16[144,1024]{1,0:T(8,128)(2,1)S(1)} %get-tuple-element.35), channel_id=1, source_target_pairs={{0,4},{4,8},{8,12},{12,16},{16,20},{20,24},{24,28},{1,5},{5,9},{9,... | collective-permute-start | bytes 884744 | tf_op jit(solution)/shard_map/ppermute | solution.py:26
  7.2 5.8 %grad_gate.1 = (f32[256,1024]{1,0:T(8,128)S(1)}, bf16[160,1024]{1,0:T(8,128)(2,1)S(1)}, bf16[1024,4096]{1,0:T(8,128)(2,1)S(1)}) custom-call(bf16[256,4096]{1,0:T(8,128)(2,1)} %c_hbm.1, bf16[1024,4096]{1,0:T(8,128)(2,1)} %w_hbm.1, bf16[3,256,1024]{2,1,0:T(8,128)(2,1)S(1)} %get-tuple-element.32.x_ref, f32[3,3,1024]{2,1,0:T(4,128)S(1)} %get-tuple-element.33.taps_ref), custom_call_target="tpu_custom_call" | custom-call | bytes 1024 | tf_op jit(solution)/shard_map/grad_gate/pallas_call | solution.py:437
  13.1 0.4 collective-permute-done.halo_ref
  13.5 5.0 %forward.1 = (bf16[256,1024]{1,0:T(8,128)(2,1)S(1)}, bf16[256,1024]{1,0:T(8,128)(2,1)S(1)}, bf16[256,1024]{1,0:T(8,128)(2,1)S(1)}, f32[256,1024]{1,0:T(8,128)S(1...) custom-call(s32[1]{0:T(128)} %bitcast.1.which_ref, bf16[3,256,1024]{2,1,0:T(8,128)(2,1)S(1)} %get-tuple-element.32.x_ref, ...), custom_call_target="tpu_custom_call" | custom-call | bytes 1024 | tf_op jit(solution)/shard_map/forward/pallas_call | solution.py:457
  18.5 0.1 collective-permute-start.1
  18.6 0.5 collective-permute-start.3
  19.1 1.3 %collective-permute-start.5 = (bf16[160,1024]{1,0:T(8,128)(2,1)S(1)}, bf16[160,1024]{1,0:T(8,128)(2,1)S(1)}, u32[]{:S(2)}, u32[]{:S(2)}) collective-permute-start(bf16[160,1024]{1,0:T(8,128)(2,1)S(1)} %get-tuple-element.43), channel_id=1, source_target_pairs={{4,0},{8,4},{12,8},{16,12},{20,16},{24,20},{28,24},{5,1},{9,5},{13... | collective-permute-start | bytes 983048 | tf_op jit(solution)/shard_map/ppermute | solution.py:26
  20.4 1.3 %keep.1 = (bf16[256,1024]{1,0:T(8,128)(2,1)S(1)}, bf16[256,1024]{1,0:T(8,128)(2,1)S(1)}) custom-call(s32[1]{0:T(128)} %bitcast.which_ref, bf16[256,1024]{1,0:T(8,128)(2,1)S(1)} %get-tuple-element.37.gate_ref, bf16[1024,4096]{1,0:T(8,128)(2,1)S(1)} %get-tuple-element.36.w_ref), custom_call_target="tpu_custom_call" | custom-call | bytes 1024 | tf_op jit(solution)/shard_map/keep/pallas_call | solution.py:472
  21.7 0.0 collective-permute-done.1
  21.7 0.2 add_convert_fusion.3
  21.9 1.6 %collective-permute-start.2 = (bf16[256,1024]{1,0:T(8,128)(2,1)S(1)}, bf16[256,1024]{1,0:T(8,128)(2,1)S(1)}, u32[]{:S(2)}, u32[]{:S(2)}) collective-permute-start(bf16[256,1024]{1,0:T(8,128)(2,1)S(1)} %add_convert_fusion.3), channel_id=1, source_target_pairs={{0,2},{1,3},{2,0},{3,1},{4,6},{5,7},{6,4},{7,5},{8,10},{9,11},{10,... | collective-permute-start | bytes 1572872 | tf_op jit(solution)/shard_map/ppermute | solution.py:479
  23.5 0.0 collective-permute-done.3
  23.5 0.2 add_convert_fusion.2
  23.7 0.6 %collective-permute-start.4 = (bf16[256,1024]{1,0:T(8,128)(2,1)S(1)}, bf16[256,1024]{1,0:T(8,128)(2,1)S(1)}, u32[]{:S(2)}, u32[]{:S(2)}) collective-permute-start(bf16[256,1024]{1,0:T(8,128)(2,1)S(1)} %add_convert_fusion.2), channel_id=1, source_target_pairs={{0,2},{1,3},{2,0},{3,1},{4,6},{5,7},{6,4},{7,5},{8,10},{9,11},{10,... | collective-permute-start | bytes 1572872 | tf_op jit(solution)/shard_map/ppermute | solution.py:479
  24.3 5.8 %lags.1 = (bf16[256,1024]{1,0:T(8,128)(2,1)S(1)}, bf16[256,1024]{1,0:T(8,128)(2,1)S(1)}, f32[16,1024]{1,0:T(8,128)S(1)}, bf16[8,1024,256]{2,1,0:T(8,128)(2,1)S(1)}) custom-call(bf16[64,128]{1,0:T(8,128)(2,1)S(1)} %get-tuple-element.34.filt_ref, bf16[3,256,1024]{2,1,0:T(8,128)(2,1)S(1)} %get-tuple-element.32.x_ref, ...), custom_call_target="tpu_custom_call" | custom-call | bytes 1024 | tf_op jit(solution)/shard_map/lags/pallas_call | solution.py:483
  30.1 1.4 %collective-permute-done.5.back_ref = bf16[160,1024]{1,0:T(8,128)(2,1)S(1)} collective-permute-done((bf16[160,1024]{1,0:T(8,128)(2,1)S(1)}, bf16[160,1024]{1,0:T(8,128)(2,1)S(1)}, u32[]{:S(2)}, u32[]{:S(2)}) %collective-permute-start.5) | collective-permute-done | bytes 327712 | tf_op jit(solution)/shard_map/ppermute | solution.py:26
  31.4 3.1 %backward.1 = (bf16[2,256,1024]{2,1,0:T(8,128)(2,1)S(1)}, bf16[32,1024]{1,0:T(8,128)(2,1)S(1)}) custom-call(bf16[3,256,1024]{2,1,0:T(8,128)(2,1)S(1)} %get-tuple-element.32.x_ref, f32[3,3,1024]{2,1,0:T(4,128)S(1)} %get-tuple-element.33.taps_ref, bf16[144,1024]{1,0:T(8,128)(2,1)S(1)} %collective-permute-done.halo_ref, ...), custom_call_target="tpu_custom_call" | custom-call | bytes 1024 | tf_op jit(solution)/shard_map/backward/pallas_call | solution.py:497
  34.5 4.3 %collective-permute-start.8 = (bf16[32,1024]{1,0:T(8,128)(2,1)S(1)}, bf16[32,1024]{1,0:T(8,128)(2,1)S(1)}, u32[]{:S(2)}, u32[]{:S(2)}) collective-permute-start(bf16[32,1024]{1,0:T(8,128)(2,1)S(1)} %get-tuple-element.50), channel_id=1, source_target_pairs={{0,12},{4,8},{8,4},{12,0},{16,28},{20,24},{24,20},{28,16},{1,13},{... | collective-permute-start | bytes 196616 | tf_op jit(solution)/shard_map/ppermute | solution.py:520
  38.8 0.0 collective-permute-start.7
  38.8 0.6 %collective-permute-start.6 = (bf16[32,1024]{1,0:T(8,128)(2,1)S(1)}, bf16[32,1024]{1,0:T(8,128)(2,1)S(1)}, u32[]{:S(2)}, u32[]{:S(2)}) collective-permute-start(bf16[32,1024]{1,0:T(8,128)(2,1)S(1)} %get-tuple-element.50), channel_id=1, source_target_pairs={{0,4},{4,0},{8,12},{12,8},{16,20},{20,16},{24,28},{28,24},{1,5},{5... | collective-permute-start | bytes 196616 | tf_op jit(solution)/shard_map/ppermute | solution.py:520
  39.4 2.3 %collective-permute-done.8 = bf16[32,1024]{1,0:T(8,128)(2,1)S(1)} collective-permute-done((bf16[32,1024]{1,0:T(8,128)(2,1)S(1)}, bf16[32,1024]{1,0:T(8,128)(2,1)S(1)}, u32[]{:S(2)}, u32[]{:S(2)}) %collective-permute-start.8) | collective-permute-done | bytes 65568 | tf_op jit(solution)/shard_map/ppermute | solution.py:520
  41.7 1.3 %collective-permute-done.7 = bf16[32,1024]{1,0:T(8,128)(2,1)S(1)} collective-permute-done((bf16[32,1024]{1,0:T(8,128)(2,1)S(1)}, bf16[32,1024]{1,0:T(8,128)(2,1)S(1)}, u32[]{:S(2)}, u32[]{:S(2)}) %collective-permute-start.7) | collective-permute-done | bytes 65568 | tf_op jit(solution)/shard_map/ppermute | solution.py:520
  43.1 0.0 collective-permute-done.6
  43.1 3.1 %collective-permute-start.9 = (bf16[32,1024]{1,0:T(8,128)(2,1)S(1)}, bf16[32,1024]{1,0:T(8,128)(2,1)S(1)}, u32[]{:S(2)}, u32[]{:S(2)}) collective-permute-start(bf16[32,1024]{1,0:T(8,128)(2,1)S(1)} %add_convert_fusion.4.refs_0_), channel_id=1, source_target_pairs={{0,16},{4,20},{8,24},{12,28},{16,0},{20,4},{24,8},{28,12},{1,17},{... | collective-permute-start | bytes 196616 | tf_op jit(solution)/shard_map/ppermute | solution.py:520
  46.2 3.6 %inputs.1 = bf16[3,256,1024]{2,1,0:T(8,128)(2,1)} custom-call(bf16[3,256,1024]{2,1,0:T(8,128)(2,1)S(1)} %get-tuple-element.32.x_ref, f32[3,3,1024]{2,1,0:T(4,128)S(1)} %get-tuple-element.33.taps_ref, bf16[64,128]{1,0:T(8,128)(2,1)S(1)} %get-tuple-element.34.filt_ref, bf16[384,1024]{1,0:T(8,128)(2,1)S(1)} %get-tuple-element.46.gext_ref, ...), custom_call_target="tpu_custom_call" | custom-call | bytes 1024 | tf_op jit(solution)/shard_map/inputs/pallas_call | solution.py:504
  49.8 0.0 collective-permute-done.9.refs_1_
  49.8 0.0 collective-permute-done.2
  49.8 0.0 collective-permute-done.4
  49.8 0.2 add_convert_fusion
  50.0 0.1 collective-permute-start.11
  50.0 0.2 add_convert_fusion.1
  50.2 0.6 %collective-permute-start.10 = (bf16[256,1024]{1,0:T(8,128)(2,1)S(1)}, bf16[256,1024]{1,0:T(8,128)(2,1)S(1)}, u32[]{:S(2)}, u32[]{:S(2)}) collective-permute-start(bf16[256,1024]{1,0:T(8,128)(2,1)S(1)} %add_convert_fusion.1), channel_id=1, source_target_pairs={{0,1},{1,0},{2,3},{3,2},{4,5},{5,4},{6,7},{7,6},{8,9},{9,8},{10,11... | collective-permute-start | bytes 1572872 | tf_op jit(solution)/shard_map/ppermute | solution.py:536
  50.8 0.6 %unpack.1 = (f32[3,3,1024]{2,1,0:T(4,128)}, f32[64,128]{1,0:T(8,128)}) custom-call(bf16[32,1024]{1,0:T(8,128)(2,1)S(1)} %add_convert_fusion.4.refs_0_, bf16[32,1024]{1,0:T(8,128)(2,1)S(1)} %collective-permute-done.9.refs_1_), custom_call_target="tpu_custom_call" | custom-call | bytes 1024 | tf_op jit(solution)/shard_map/unpack/pallas_call | solution.py:542
  51.5 0.5 collective-permute-done.11
  51.9 0.7 %collective-permute-done.10 = bf16[256,1024]{1,0:T(8,128)(2,1)S(1)} collective-permute-done((bf16[256,1024]{1,0:T(8,128)(2,1)S(1)}, bf16[256,1024]{1,0:T(8,128)(2,1)S(1)}, u32[]{:S(2)}, u32[]{:S(2)}) %collective-permute-start.10) | collective-permute-done | bytes 524320 | tf_op jit(solution)/shard_map/ppermute | solution.py:536
  52.7 1.6 %maximum_select_fusion = bf16[256,4096]{1,0:T(8,128)(2,1)} fusion(bf16[256,1024]{1,0:T(8,128)(2,1)S(1)} %collective-permute-done.11, bf16[256,1024]{1,0:T(8,128)(2,1)S(1)} %collective-permute-done.10, bf16[256,1024]{1,0:T(8,128)(2,1)S(1)} %add_convert_fusion, bf16[256,1024]{1,0:T(8,128)(2,1)S(1)} %add_convert_fusion.1, pred[]{:T(512)S(6)} %eq.3), kind=kLoop, calls=%fused_computation | loop fusion | flops 17825792 | bytes 4194305 | tf_op jit(solution)/shard_map/jit(_where)/select_n | solution.py:537
  (1 shorter events, 0.0 us)
Async XLA Ops:
  2.4 11.1 %collective-permute-start = (bf16[144,1024]{1,0:T(8,128)(2,1)S(1)}, bf16[144,1024]{1,0:T(8,128)(2,1)S(1)}, u32[]{:S(2)}, u32[]{:S(2)}) collective-permute-start(bf16[144,1024]{1,0:T(8,128)(2,1)S(1)} %get-tuple-element.35), channel_id=1, source_target_pairs={{0,4},{4,8},{8,12},{12,16},{16,20},{20,24},{24,28},{1,5},{5,9},{9,... | collective-permute-start | bytes 884744 | tf_op jit(solution)/shard_map/ppermute | solution.py:26
  18.5 3.2 %collective-permute-start.1 = (bf16[256,1024]{1,0:T(8,128)(2,1)S(1)}, bf16[256,1024]{1,0:T(8,128)(2,1)S(1)}, u32[]{:S(2)}, u32[]{:S(2)}) collective-permute-start(bf16[256,1024]{1,0:T(8,128)(2,1)S(1)} %get-tuple-element.39), channel_id=1, source_target_pairs={{0,1},{1,0},{2,3},{3,2},{4,5},{5,4},{6,7},{7,6},{8,9},{9,8},{10,11... | collective-permute-start | bytes 1572872 | tf_op jit(solution)/shard_map/ppermute | solution.py:471
  18.6 4.9 %collective-permute-start.3 = (bf16[256,1024]{1,0:T(8,128)(2,1)S(1)}, bf16[256,1024]{1,0:T(8,128)(2,1)S(1)}, u32[]{:S(2)}, u32[]{:S(2)}) collective-permute-start(bf16[256,1024]{1,0:T(8,128)(2,1)S(1)} %get-tuple-element.41), channel_id=1, source_target_pairs={{0,1},{1,0},{2,3},{3,2},{4,5},{5,4},{6,7},{7,6},{8,9},{9,8},{10,11... | collective-permute-start | bytes 1572872 | tf_op jit(solution)/shard_map/ppermute | solution.py:471
  19.1 12.3 %collective-permute-start.5 = (bf16[160,1024]{1,0:T(8,128)(2,1)S(1)}, bf16[160,1024]{1,0:T(8,128)(2,1)S(1)}, u32[]{:S(2)}, u32[]{:S(2)}) collective-permute-start(bf16[160,1024]{1,0:T(8,128)(2,1)S(1)} %get-tuple-element.43), channel_id=1, source_target_pairs={{4,0},{8,4},{12,8},{16,12},{20,16},{24,20},{28,24},{5,1},{9,5},{13... | collective-permute-start | bytes 983048 | tf_op jit(solution)/shard_map/ppermute | solution.py:26
  21.9 27.9 %collective-permute-start.2 = (bf16[256,1024]{1,0:T(8,128)(2,1)S(1)}, bf16[256,1024]{1,0:T(8,128)(2,1)S(1)}, u32[]{:S(2)}, u32[]{:S(2)}) collective-permute-start(bf16[256,1024]{1,0:T(8,128)(2,1)S(1)} %add_convert_fusion.3), channel_id=1, source_target_pairs={{0,2},{1,3},{2,0},{3,1},{4,6},{5,7},{6,4},{7,5},{8,10},{9,11},{10,... | collective-permute-start | bytes 1572872 | tf_op jit(solution)/shard_map/ppermute | solution.py:479
  23.7 26.1 %collective-permute-start.4 = (bf16[256,1024]{1,0:T(8,128)(2,1)S(1)}, bf16[256,1024]{1,0:T(8,128)(2,1)S(1)}, u32[]{:S(2)}, u32[]{:S(2)}) collective-permute-start(bf16[256,1024]{1,0:T(8,128)(2,1)S(1)} %add_convert_fusion.2), channel_id=1, source_target_pairs={{0,2},{1,3},{2,0},{3,1},{4,6},{5,7},{6,4},{7,5},{8,10},{9,11},{10,... | collective-permute-start | bytes 1572872 | tf_op jit(solution)/shard_map/ppermute | solution.py:479
  34.5 7.2 %collective-permute-start.8 = (bf16[32,1024]{1,0:T(8,128)(2,1)S(1)}, bf16[32,1024]{1,0:T(8,128)(2,1)S(1)}, u32[]{:S(2)}, u32[]{:S(2)}) collective-permute-start(bf16[32,1024]{1,0:T(8,128)(2,1)S(1)} %get-tuple-element.50), channel_id=1, source_target_pairs={{0,12},{4,8},{8,4},{12,0},{16,28},{20,24},{24,20},{28,16},{1,13},{... | collective-permute-start | bytes 196616 | tf_op jit(solution)/shard_map/ppermute | solution.py:520
  38.8 4.3 %collective-permute-start.7 = (bf16[32,1024]{1,0:T(8,128)(2,1)S(1)}, bf16[32,1024]{1,0:T(8,128)(2,1)S(1)}, u32[]{:S(2)}, u32[]{:S(2)}) collective-permute-start(bf16[32,1024]{1,0:T(8,128)(2,1)S(1)} %get-tuple-element.50), channel_id=1, source_target_pairs={{0,8},{4,12},{8,0},{12,4},{16,24},{20,28},{24,16},{28,20},{1,9},{5... | collective-permute-start | bytes 196616 | tf_op jit(solution)/shard_map/ppermute | solution.py:520
  38.8 4.3 %collective-permute-start.6 = (bf16[32,1024]{1,0:T(8,128)(2,1)S(1)}, bf16[32,1024]{1,0:T(8,128)(2,1)S(1)}, u32[]{:S(2)}, u32[]{:S(2)}) collective-permute-start(bf16[32,1024]{1,0:T(8,128)(2,1)S(1)} %get-tuple-element.50), channel_id=1, source_target_pairs={{0,4},{4,0},{8,12},{12,8},{16,20},{20,16},{24,28},{28,24},{1,5},{5... | collective-permute-start | bytes 196616 | tf_op jit(solution)/shard_map/ppermute | solution.py:520
  43.1 6.7 %collective-permute-start.9 = (bf16[32,1024]{1,0:T(8,128)(2,1)S(1)}, bf16[32,1024]{1,0:T(8,128)(2,1)S(1)}, u32[]{:S(2)}, u32[]{:S(2)}) collective-permute-start(bf16[32,1024]{1,0:T(8,128)(2,1)S(1)} %add_convert_fusion.4.refs_0_), channel_id=1, source_target_pairs={{0,16},{4,20},{8,24},{12,28},{16,0},{20,4},{24,8},{28,12},{1,17},{... | collective-permute-start | bytes 196616 | tf_op jit(solution)/shard_map/ppermute | solution.py:520
  50.0 2.0 %collective-permute-start.11 = (bf16[256,1024]{1,0:T(8,128)(2,1)S(1)}, bf16[256,1024]{1,0:T(8,128)(2,1)S(1)}, u32[]{:S(2)}, u32[]{:S(2)}) collective-permute-start(bf16[256,1024]{1,0:T(8,128)(2,1)S(1)} %add_convert_fusion), channel_id=1, source_target_pairs={{0,1},{1,0},{2,3},{3,2},{4,5},{5,4},{6,7},{7,6},{8,9},{9,8},{10,11... | collective-permute-start | bytes 1572872 | tf_op jit(solution)/shard_map/ppermute | solution.py:536
  50.2 2.4 %collective-permute-start.10 = (bf16[256,1024]{1,0:T(8,128)(2,1)S(1)}, bf16[256,1024]{1,0:T(8,128)(2,1)S(1)}, u32[]{:S(2)}, u32[]{:S(2)}) collective-permute-start(bf16[256,1024]{1,0:T(8,128)(2,1)S(1)} %add_convert_fusion.1), channel_id=1, source_target_pairs={{0,1},{1,0},{2,3},{3,2},{4,5},{5,4},{6,7},{7,6},{8,9},{9,8},{10,11... | collective-permute-start | bytes 1572872 | tf_op jit(solution)/shard_map/ppermute | solution.py:536

commit v5 on v4

--- a/solution.py
+++ b/solution.py
@@ -9,6 +9,7 @@
 
 LANES = 128
 RIM = 16
+SUB = 32
 COST = 1024
 PIECES = 2
 F32 = jnp.float32
@@ -46,12 +47,9 @@
     return jax.ShapeDtypeStruct(dims, dtype)
 
 
-def each_tile(chans, body):
-    def step(j, carry):
-        body(j, pl.ds(pl.multiple_of(j * LANES, LANES), LANES))
-        return carry
-
-    lax.fori_loop(0, chans // LANES, step, 0, unroll=2)
+def each_tile(chans, body, *scratch):
+    for j in range(chans // LANES):
+        body(j, slice(j * LANES, (j + 1) * LANES), *[ref.at[j] for ref in scratch])
 
 
 def feature(ext_ref, taps_ref, lanes, part, start, rows):
@@ -67,33 +65,37 @@
     return lax.broadcasted_iota(jnp.int32, (rows, LANES), 1) // group
 
 
-def square(axis):
-    return lax.broadcasted_iota(jnp.int32, (LANES, LANES), axis)
+def grid_of(rows, axis):
+    return lax.broadcasted_iota(jnp.int32, (rows, LANES), axis)
 
 
 def fill_table(table_ref, taps, forward):
-    early = (square(1) > square(0)) if forward else (square(1) >= square(0))
+    row, col = grid_of(SUB, 0), grid_of(SUB, 1)
+    early = (col > row) if forward else (col >= row)
     for g in range(taps.shape[0]):
-        wide = jnp.broadcast_to(taps[g : g + 1, :], (LANES, LANES))
+        wide = jnp.broadcast_to(taps[g : g + 1, :], (SUB, LANES))
         ring = pltpu.roll(wide, 0, 1, stride=1, stride_axis=0)
-        table_ref[g * LANES : (g + 1) * LANES, 0:LANES] = jnp.where(early, ring, 0.0).astype(BF16)
-        table_ref[g * LANES : (g + 1) * LANES, LANES:] = jnp.where(early, 0.0, ring).astype(BF16)
+        rows = slice(g * SUB, (g + 1) * SUB)
+        table_ref[rows, 0:LANES] = jnp.where(early, ring, 0.0).astype(BF16)
+        table_ref[rows, LANES:] = jnp.where(early, 0.0, ring)[:, 0:SUB].astype(BF16)
 
 
 def pick_groups(wide, group, blocks):
-    lane = group_of_lane(LANES, group)
+    lane = group_of_lane(SUB, group)
     outs = []
     for b in range(blocks):
-        total = wide[0:LANES, b * LANES : (b + 1) * LANES]
+        cols = slice(b * LANES, (b + 1) * LANES)
+        total = wide[0:SUB, cols]
         for g in range(1, LANES // group):
-            part = wide[g * LANES : (g + 1) * LANES, b * LANES : (b + 1) * LANES]
-            total = jnp.where(lane == g, part, total)
+            total = jnp.where(lane == g, wide[g * SUB : (g + 1) * SUB, cols], total)
         outs.append(total)
     return jnp.concatenate(outs, axis=0)
 
 
-def side_by_side(ref, blocks, lanes):
-    return jnp.concatenate([ref[b * LANES : (b + 2) * LANES, lanes] for b in range(blocks)], axis=1)
+def windows(ref, blocks, lanes):
+    return jnp.concatenate(
+        [ref[b * SUB : (b + 1) * SUB + LANES, lanes] for b in range(blocks)], axis=1
+    )
 
 
 def spread_taps(filt, group, reverse):
@@ -102,13 +104,13 @@
         group_of_lane(count, group) == lax.broadcasted_iota(jnp.int32, (count, LANES), 0)
     ).astype(BF16)
     if reverse:
-        flip = (square(0) + square(1) == LANES - 1).astype(BF16)
+        flip = (grid_of(LANES, 0) + grid_of(LANES, 1) == LANES - 1).astype(BF16)
         filt = jnp.dot(filt, flip, preferred_element_type=F32).astype(BF16)
     return lax.dot_general(filt, owner, (((0,), (0,)), ((), ())), preferred_element_type=F32)
 
 
 def tail_kernel(
-    x_hbm, taps_hbm, filt_hbm, sent_ref, x_ref, taps_ref, filt_ref, ext, sems
+    x_hbm, taps_hbm, filt_hbm, sent_ref, x_ref, taps_ref, filt_ref, ext_ref, sems
 ):
     _, rows, chans = x_ref.shape
     first = rows - LANES - RIM
@@ -127,7 +129,7 @@
     for copy in copies[:3]:
         copy.wait()
 
-    def tile(j, lanes):
+    def tile(j, lanes, ext):
         for part in range(3):
             ext[part, 8:, :] = x_ref[part, first:, lanes].astype(F32)
         keyed = feature(ext, taps_ref, lanes, 1, RIM, LANES)
@@ -138,13 +140,13 @@
         rim.append(jnp.zeros((RIM - 6, LANES), F32))
         sent_ref[LANES:, lanes] = jnp.concatenate(rim, axis=0).astype(BF16)
 
-    each_tile(chans, tile)
+    each_tile(chans, tile, ext_ref)
     for copy in copies[3:]:
         copy.wait()
 
 
 def grad_gate_kernel(
-    c_hbm, w_hbm, x_ref, taps_ref, gg_ref, back_ref, w_ref, c_ref, ext, c_sem, w_sems
+    c_hbm, w_hbm, x_ref, taps_ref, gg_ref, back_ref, w_ref, c_ref, ext_ref, c_sem, w_sems
 ):
     chans = w_ref.shape[0]
     chunks = w_sems.shape[0]
@@ -176,7 +178,7 @@
 
     lax.fori_loop(0, chunks, product, 0)
 
-    def tile(j, lanes):
+    def tile(j, lanes, ext):
         ext[0, 0:8, :] = jnp.zeros((8, LANES), F32)
         ext[0, 8:, :] = x_ref[0, 0:span, lanes].astype(F32)
         query = feature(ext, taps_ref, lanes, 0, 0, span)
@@ -187,19 +189,19 @@
         rim += [high, grad - high, jnp.zeros((RIM - 10, LANES), F32)]
         back_ref[span:, lanes] = jnp.concatenate(rim, axis=0).astype(BF16)
 
-    each_tile(chans, tile)
+    each_tile(chans, tile, ext_ref)
 
 
 def forward_kernel(
     group, which_ref, x_ref, taps_ref, filt_ref, halo_ref, w_ref,
     *refs,
 ):
-    sends, (gate_ref, mixed_ref, feat_ref, gext_ref, ext, table) = refs[:PIECES], refs[PIECES:]
+    sends, (gate_ref, mixed_ref, feat_ref, gext_ref, ext_ref, table_ref) = refs[:PIECES], refs[PIECES:]
     _, rows, chans = x_ref.shape
-    blocks = rows // LANES
+    blocks = rows // SUB
     count = LANES // group
 
-    def tile(j, lanes):
+    def tile(j, lanes, ext, table):
         for part in range(3):
             at = LANES + 2 * part
             ext[part, 6:8, :] = halo_ref[at : at + 2, lanes].astype(F32)
@@ -210,11 +212,11 @@
         feat_ref[2, :, lanes] = valued
         gext_ref[0:LANES, lanes] = halo_ref[0:LANES, lanes]
         gext_ref[LANES:, lanes] = (keyed * valued).astype(BF16)
-        filt = filt_ref[pl.ds(pl.multiple_of(j * count, count), count), :]
-        turned = ((square(0) + square(1)) % LANES == 0).astype(BF16)
+        filt = filt_ref[j * count : (j + 1) * count, :]
+        turned = ((grid_of(LANES, 0) + grid_of(LANES, 1)) % LANES == 0).astype(BF16)
         fill_table(table, jnp.dot(filt, turned, preferred_element_type=F32), True)
         wide = jnp.dot(
-            table[...], side_by_side(gext_ref, blocks, lanes), preferred_element_type=F32
+            table[...], windows(gext_ref, blocks, lanes), preferred_element_type=F32
         )
         mixed = pick_groups(wide, group, blocks)
         mixed_ref[:, lanes] = mixed
@@ -222,7 +224,7 @@
         feat_ref[0, :, lanes] = query
         gate_ref[:, lanes] = (query * mixed).astype(BF16)
 
-    each_tile(chans, tile)
+    each_tile(chans, tile, ext_ref, table_ref)
     project(which_ref[0], gate_ref, w_ref, sends)
 
 
@@ -250,14 +252,14 @@
 
 def lags_kernel(
     group, filt_ref, x_ref, halo_ref, gg_ref, mixed_ref, feat_ref, gext_ref,
-    gm_ref, gq_ref, lags_ref, tables_ref, left, ext,
+    gm_ref, gq_ref, lags_ref, tables_ref, left_ref, upside_ref, ext_ref,
 ):
     rows, chans = gg_ref.shape
-    blocks = rows // LANES
+    blocks = rows // SUB
     count = LANES // group
 
-    def tile(j, lanes):
-        filt = filt_ref[pl.ds(pl.multiple_of(j * count, count), count), :]
+    def tile(j, lanes, left, upside, ext):
+        filt = filt_ref[j * count : (j + 1) * count, :]
         fill_table(tables_ref.at[j], filt.astype(F32), False)
         grad_mixed = (gg_ref[:, lanes] * feat_ref[0, :, lanes]).astype(BF16)
         gm_ref[:, lanes] = grad_mixed
@@ -266,25 +268,42 @@
         ext[0, 6:8, :] = halo_ref[LANES : LANES + 2, lanes].astype(F32)
         ext[0, 8:, :] = x_ref[0, :, lanes].astype(F32)
         sums = short_sums(grad_query.astype(F32), ext, 0)
-        lane = group_of_lane(LANES, group)
+        lane = group_of_lane(SUB, group)
         for g in range(count):
             for b in range(blocks):
-                left[g * LANES : (g + 1) * LANES, b * LANES : (b + 1) * LANES] = jnp.where(
-                    lane == g, grad_mixed[b * LANES : (b + 1) * LANES, :], jnp.zeros((), BF16)
+                left[g * SUB : (g + 1) * SUB, b * LANES : (b + 1) * LANES] = jnp.where(
+                    lane == g, grad_mixed[b * SUB : (b + 1) * SUB, :], jnp.zeros((), BF16)
                 )
-        ends = [gext_ref[b * LANES : (b + 1) * LANES, lanes] for b in range(blocks + 1)]
-        flip = (square(0) + square(1) == LANES - 1).astype(BF16)
-        upside = jnp.dot(
-            flip, jnp.concatenate(ends, axis=1), preferred_element_type=F32
+        ends = rows // LANES + 1
+        flip = (grid_of(LANES, 0) + grid_of(LANES, 1) == LANES - 1).astype(BF16)
+        turned = jnp.dot(
+            flip,
+            jnp.concatenate(
+                [gext_ref[b * LANES : (b + 1) * LANES, lanes] for b in range(ends)], axis=1
+            ),
+            preferred_element_type=F32,
         ).astype(BF16)
-        right = jnp.concatenate([upside[:, 0 : blocks * LANES], upside[:, LANES:]], axis=0)
+        upside[0:LANES, :] = jnp.zeros((LANES, LANES), BF16)
+        for b in range(ends):
+            upside[LANES * (ends - b) : LANES * (ends - b + 1), :] = turned[
+                :, b * LANES : (b + 1) * LANES
+            ]
+        rights = []
+        for b in range(blocks):
+            at = rows + LANES - b * SUB
+            rights.append(
+                jnp.concatenate([upside[at : at + LANES], upside[at - LANES : at]], axis=0)
+            )
         products = lax.dot_general(
-            left[...], right, (((1,), (1,)), ((), ())), preferred_element_type=F32
+            left[...],
+            jnp.concatenate(rights, axis=1),
+            (((1,), (1,)), ((), ())),
+            preferred_element_type=F32,
         )
-        early = square(0) + square(1) < LANES - 1
+        early = grid_of(SUB, 0) + grid_of(SUB, 1) < LANES - 1
         lag_rows = []
         for g in range(count):
-            own = products[g * LANES : (g + 1) * LANES, :]
+            own = products[g * SUB : (g + 1) * SUB, :]
             ring = jnp.where(early, own[:, 0:LANES], own[:, LANES:])
             ring = pltpu.roll(ring, 0, 1, stride=1, stride_axis=0)
             lag_rows.append(jnp.sum(ring, axis=0, keepdims=True))
@@ -292,7 +311,7 @@
         sums.append(jnp.zeros((16 - count - 3, LANES), F32))
         lags_ref[:, lanes] = jnp.concatenate([lags] + sums, axis=0)
 
-    each_tile(chans, tile)
+    each_tile(chans, tile, left_ref, upside_ref, ext_ref)
 
 
 def next_rows(ext_ref, taps_ref, x_ref, back_ref, lanes, parts):
@@ -318,13 +337,13 @@
 
 def backward_kernel(
     group, x_ref, taps_ref, halo_ref, feat_ref, back_ref, gm_ref, lags_ref, tables_ref,
-    gkv_ref, sums_ref, ext, mext, near,
+    gkv_ref, sums_ref, ext_ref, mext_ref, near_ref,
 ):
     _, rows, chans = x_ref.shape
-    blocks = rows // LANES
+    blocks = rows // SUB
     count = LANES // group
 
-    def tile(j, lanes):
+    def tile(j, lanes, ext, mext, near):
         for part in range(1, 3):
             at = LANES + 2 * part
             ext[part, 6:8, :] = halo_ref[at : at + 2, lanes].astype(F32)
@@ -334,7 +353,7 @@
         mext[0:rows, :] = gm_ref[:, lanes]
         mext[rows:, :] = head[0:LANES].astype(BF16)
         wide = jnp.dot(
-            tables_ref[j], side_by_side(mext, blocks, slice(None)), preferred_element_type=F32
+            tables_ref[j], windows(mext, blocks, slice(None)), preferred_element_type=F32
         )
         grad_gated = pick_groups(wide, group, blocks)
         sums = [None] * 3
@@ -349,21 +368,21 @@
         flat.append(jnp.zeros((32 - count - 9, LANES), F32))
         sums_ref[:, lanes] = jnp.concatenate(flat, axis=0).astype(sums_ref.dtype)
 
-    each_tile(chans, tile)
+    each_tile(chans, tile, ext_ref, mext_ref, near_ref)
 
 
 def inputs_kernel(
-    group, x_ref, taps_ref, filt_ref, gext_ref, back_ref, gq_ref, gkv_ref, gin_ref, near, gf
+    group, x_ref, taps_ref, filt_ref, gext_ref, back_ref, gq_ref, gkv_ref, gin_ref, near_ref, gf_ref
 ):
     _, rows, chans = x_ref.shape
     count = LANES // group
 
-    def tile(j, lanes):
+    def tile(j, lanes, near, gf):
         (query, keyed, valued), grad = next_rows(
             near, taps_ref, x_ref, back_ref, lanes, (0, 1, 2)
         )
         head = next_mixed(back_ref, lanes, grad, query)
-        filt = filt_ref[pl.ds(pl.multiple_of(j * count, count), count), :]
+        filt = filt_ref[j * count : (j + 1) * count, :]
         taps = spread_taps(filt, group, False)
         taps_turned = spread_taps(filt, group, True)
         recent = gext_ref[rows:, lanes].astype(F32)
@@ -386,7 +405,7 @@
                 total = total + tap * gf[part, lag : lag + rows, :]
             gin_ref[part, :, lanes] = total.astype(BF16)
 
-    each_tile(chans, tile)
+    each_tile(chans, tile, near_ref, gf_ref)
 
 
 def unpack_kernel(group, short_scale, long_scale, *refs):
@@ -412,6 +431,7 @@
     width = out_weight.shape[1]
     group = chans // groups
     count = LANES // group
+    tiles = chans // LANES
     tokens_all = rows * lax.axis_size("ctx")
     n_tp = lax.axis_size("tp")
     signal = inputs.transpose(1, 0, 2)
@@ -419,7 +439,7 @@
         pltpu.with_memory_space_constraint(value, pltpu.HBM)
         for value in (signal, short_filter, long_filter, out_weight, out_cotangent)
     ]
-    table = pltpu.VMEM((count * LANES, 2 * LANES), BF16)
+    table = pltpu.VMEM((tiles, count * SUB, LANES + SUB), BF16)
 
     sent, signal, short_filter, long_filter = call(
         tail_kernel,
@@ -430,7 +450,7 @@
             shape(short_filter.shape, F32),
             shape(long_filter.shape, BF16),
         ),
-        [pltpu.VMEM((3, 8 + RIM + LANES, LANES), F32), pltpu.SemaphoreType.DMA((5,))],
+        [pltpu.VMEM((tiles, 3, 8 + RIM + LANES, LANES), F32), pltpu.SemaphoreType.DMA((5,))],
         far=3,
     )(signal, short_filter, long_filter)
     halo = shifted(sent, "ctx", 1)
@@ -444,7 +464,7 @@
         ),
         [
             pltpu.VMEM(out_cotangent.shape, BF16),
-            pltpu.VMEM((1, 8 + RIM + LANES, LANES), F32),
+            pltpu.VMEM((tiles, 1, 8 + RIM + LANES, LANES), F32),
             pltpu.SemaphoreType.DMA,
             pltpu.SemaphoreType.DMA((max(1, chans // 256),)),
         ],
@@ -464,7 +484,7 @@
             shape((3, rows, chans), F32),
             shape((LANES + rows, chans), BF16),
         ),
-        [pltpu.VMEM((3, 8 + rows, LANES), F32), table],
+        [pltpu.VMEM((tiles, 3, 8 + rows, LANES), F32), table],
         scalars=1,
         operands=5,
     )(jnp.reshape(1 - core, (1,)), signal, short_filter, long_filter, halo, out_weight)
@@ -478,8 +498,8 @@
     step = 2
     got = [lax.ppermute(value, "tp", pairwise("tp", step)) for value in mine]
 
-    ext = pltpu.VMEM((3, rows + 8, LANES), F32)
-    near = pltpu.VMEM((3, 16, LANES), F32)
+    ext = pltpu.VMEM((tiles, 3, rows + 8, LANES), F32)
+    near = pltpu.VMEM((tiles, 3, 16, LANES), F32)
     grad_mixed, grad_query, lags, tables = call(
         functools.partial(lags_kernel, group),
         "lags",
@@ -487,9 +507,13 @@
             shape((rows, chans), BF16),
             shape((rows, chans), BF16),
             shape((16, chans), F32),
-            shape((chans // LANES, count * LANES, 2 * LANES), BF16),
+            shape((chans // LANES, count * SUB, LANES + SUB), BF16),
         ),
-        [pltpu.VMEM((count * LANES, (rows // LANES) * LANES), BF16), ext],
+        [
+            pltpu.VMEM((tiles, count * SUB, rows // SUB * LANES), BF16),
+            pltpu.VMEM((tiles, rows + 2 * LANES, LANES), BF16),
+            ext,
+        ],
         operands=7,
     )(long_filter, signal, halo, grad_gate, mixed, feat, gated)
     n_ctx = lax.axis_size("ctx")
@@ -498,14 +522,14 @@
         functools.partial(backward_kernel, group),
         "backward",
         (shape((2, rows, chans), BF16), shape((32, chans), BF16 if by_pairs else F32)),
-        [ext, pltpu.VMEM((rows + LANES, LANES), BF16), near],
+        [ext, pltpu.VMEM((tiles, rows + LANES, LANES), BF16), near],
         operands=8,
     )(signal, short_filter, halo, feat, back, grad_mixed, lags, tables)
     grad_in = call(
         functools.partial(inputs_kernel, group),
         "inputs",
         shape((3, rows, chans), BF16),
-        [near, pltpu.VMEM((3, rows + 8, LANES), F32)],
+        [near, pltpu.VMEM((tiles, 3, rows + 8, LANES), F32)],
         operands=7,
     )(signal, short_filter, long_filter, gated, back, grad_query, grad_rest)
     if by_pairs:

time: 54.5 us -> 52.8 us (0.969)
  the two profiles are of different devices: /device:TPU:0 before, /device:TPU:25 now
where the time goes in v5:
time: 52.8 us; the launch traced here: 52.5 us
  Pallas kernels  21.9 us (41%)
  starting transfers between devices  14.7 us (28%)
  waiting for transfers between devices  12.8 us (24%)
  other arithmetic  2.36 us (4%)
  between operations  0.75 us (1%)
    pallas_call x1, Pallas kernels, local(): call(grad_gate_kernel, 'grad_gate', (shape((rows, chans), F32), shape((LA...  5.75 us
    ppermute x2, starting transfers between devices, shifted(): lax.ppermute(value, axis, [(source, source + steps) for source in range(i...  5.39 us
    ppermute x2, waiting for transfers between devices, local(): got = [lax.ppermute(value, 'tp', pairwise('tp', step)) for value in mine]  5.3 us
    pallas_call x1, Pallas kernels, local(): call(functools.partial(forward_kernel, group), 'forward', (piece,) * PIEC...  4.33 us
    ppermute x4, starting transfers between devices, local(): lax.ppermute(terms[0], 'ctx', pairwise('ctx', i * hop))  4.33 us
    ppermute x2, waiting for transfers between devices, shifted(): lax.ppermute(value, axis, [(source, source + steps) for source in range(i...  3.78 us
    pallas_call x1, Pallas kernels, local(): call(functools.partial(inputs_kernel, group), 'inputs', shape((3, rows, c...  3.27 us
    pallas_call x1, Pallas kernels, local(): call(functools.partial(lags_kernel, group), 'lags', (shape((rows, chans),...  3.17 us
  transfers between devices with their start and end apart: 12, of which 8 were waited for; matrix products, arithmetic and copies ran while one was open for 1% of the time, Pallas kernels for 30%

profile of v5, /device:TPU:25, one launch (start us, length us, event | category | flops | bytes accessed | tf_op | source)
XLA Modules:
  0.0 52.5 jit_solution(1205679282790581083)
XLA Ops:
  0.6 1.7 %tail.1 = (bf16[144,1024]{1,0:T(8,128)(2,1)S(1)}, bf16[3,256,1024]{2,1,0:T(8,128)(2,1)S(1)}, f32[3,3,1024]{2,1,0:T(4,128)S(1)}, bf16[64,128]{1,0:T(8,128)(2,1)S(1)}) custom-call(bf16[3,256,1024]{2,1,0:T(8,128)(2,1)} %bitcast.4, f32[3,3,1024]{2,1,0:T(4,128)} %taps_hbm.1, bf16[64,128]{1,0:T(8,128)(2,1)} %filt_hbm.1), custom_call_target="tpu_custom_call" | custom-call | bytes 1024 | tf_op jit(solution)/shard_map/tail/pallas_call | solution.py:444
  2.3 3.1 %collective-permute-start = (bf16[144,1024]{1,0:T(8,128)(2,1)S(1)}, bf16[144,1024]{1,0:T(8,128)(2,1)S(1)}, u32[]{:S(2)}, u32[]{:S(2)}) collective-permute-start(bf16[144,1024]{1,0:T(8,128)(2,1)S(1)} %get-tuple-element.35), channel_id=1, source_target_pairs={{0,4},{4,8},{8,12},{12,16},{16,20},{20,24},{24,28},{1,5},{5,9},{9,... | collective-permute-start | bytes 884744 | tf_op jit(solution)/shard_map/ppermute | solution.py:27
  5.5 5.8 %grad_gate.1 = (f32[256,1024]{1,0:T(8,128)S(1)}, bf16[160,1024]{1,0:T(8,128)(2,1)S(1)}, bf16[1024,4096]{1,0:T(8,128)(2,1)S(1)}) custom-call(bf16[256,4096]{1,0:T(8,128)(2,1)} %c_hbm.1, bf16[1024,4096]{1,0:T(8,128)(2,1)} %w_hbm.1, bf16[3,256,1024]{2,1,0:T(8,128)(2,1)S(1)} %get-tuple-element.32.x_ref, f32[3,3,1024]{2,1,0:T(4,128)S(1)} %get-tuple-element.33.taps_ref), custom_call_target="tpu_custom_call" | custom-call | bytes 1024 | tf_op jit(solution)/shard_map/grad_gate/pallas_call | solution.py:457
  11.2 1.8 %collective-permute-done.halo_ref = bf16[144,1024]{1,0:T(8,128)(2,1)S(1)} collective-permute-done((bf16[144,1024]{1,0:T(8,128)(2,1)S(1)}, bf16[144,1024]{1,0:T(8,128)(2,1)S(1)}, u32[]{:S(2)}, u32[]{:S(2)}) %collective-permute-start) | collective-permute-done | bytes 294944 | tf_op jit(solution)/shard_map/ppermute | solution.py:27
  13.0 4.3 %forward.1 = (bf16[256,1024]{1,0:T(8,128)(2,1)S(1)}, bf16[256,1024]{1,0:T(8,128)(2,1)S(1)}, bf16[256,1024]{1,0:T(8,128)(2,1)S(1)}, f32[256,1024]{1,0:T(8,128)S(1...) custom-call(s32[1]{0:T(128)} %bitcast.1.which_ref, bf16[3,256,1024]{2,1,0:T(8,128)(2,1)S(1)} %get-tuple-element.32.x_ref, ...), custom_call_target="tpu_custom_call" | custom-call | bytes 1024 | tf_op jit(solution)/shard_map/forward/pallas_call | solution.py:477
  17.3 1.6 %collective-permute-start.1 = (bf16[256,1024]{1,0:T(8,128)(2,1)S(1)}, bf16[256,1024]{1,0:T(8,128)(2,1)S(1)}, u32[]{:S(2)}, u32[]{:S(2)}) collective-permute-start(bf16[256,1024]{1,0:T(8,128)(2,1)S(1)} %get-tuple-element.39), channel_id=1, source_target_pairs={{0,1},{1,0},{2,3},{3,2},{4,5},{5,4},{6,7},{7,6},{8,9},{9,8},{10,11... | collective-permute-start | bytes 1572872 | tf_op jit(solution)/shard_map/ppermute | solution.py:491
  18.9 0.1 collective-permute-start.3
  19.0 2.3 %collective-permute-start.5 = (bf16[160,1024]{1,0:T(8,128)(2,1)S(1)}, bf16[160,1024]{1,0:T(8,128)(2,1)S(1)}, u32[]{:S(2)}, u32[]{:S(2)}) collective-permute-start(bf16[160,1024]{1,0:T(8,128)(2,1)S(1)} %get-tuple-element.43), channel_id=1, source_target_pairs={{4,0},{8,4},{12,8},{16,12},{20,16},{24,20},{28,24},{5,1},{9,5},{13... | collective-permute-start | bytes 983048 | tf_op jit(solution)/shard_map/ppermute | solution.py:27
  21.3 1.3 %keep.1 = (bf16[256,1024]{1,0:T(8,128)(2,1)S(1)}, bf16[256,1024]{1,0:T(8,128)(2,1)S(1)}) custom-call(s32[1]{0:T(128)} %bitcast.which_ref, bf16[256,1024]{1,0:T(8,128)(2,1)S(1)} %get-tuple-element.37.gate_ref, bf16[1024,4096]{1,0:T(8,128)(2,1)S(1)} %get-tuple-element.36.w_ref), custom_call_target="tpu_custom_call" | custom-call | bytes 1024 | tf_op jit(solution)/shard_map/keep/pallas_call | solution.py:492
  22.6 0.0 collective-permute-done.1
  22.6 0.2 add_convert_fusion.3
  22.8 1.3 %collective-permute-start.2 = (bf16[256,1024]{1,0:T(8,128)(2,1)S(1)}, bf16[256,1024]{1,0:T(8,128)(2,1)S(1)}, u32[]{:S(2)}, u32[]{:S(2)}) collective-permute-start(bf16[256,1024]{1,0:T(8,128)(2,1)S(1)} %add_convert_fusion.3), channel_id=1, source_target_pairs={{0,2},{1,3},{2,0},{3,1},{4,6},{5,7},{6,4},{7,5},{8,10},{9,11},{10,... | collective-permute-start | bytes 1572872 | tf_op jit(solution)/shard_map/ppermute | solution.py:499
  24.1 0.0 collective-permute-done.3
  24.1 0.2 add_convert_fusion.2
  24.3 0.3 collective-permute-start.4
  24.6 3.2 %lags.1 = (bf16[256,1024]{1,0:T(8,128)(2,1)S(1)}, bf16[256,1024]{1,0:T(8,128)(2,1)S(1)}, f32[16,1024]{1,0:T(8,128)S(1)}, bf16[8,256,160]{2,1,0:T(8,128)(2,1)S(1)}) custom-call(bf16[64,128]{1,0:T(8,128)(2,1)S(1)} %get-tuple-element.34.filt_ref, bf16[3,256,1024]{2,1,0:T(8,128)(2,1)S(1)} %get-tuple-element.32.x_ref, ...), custom_call_target="tpu_custom_call" | custom-call | bytes 1024 | tf_op jit(solution)/shard_map/lags/pallas_call | solution.py:503
  27.8 2.0 %collective-permute-done.5.back_ref = bf16[160,1024]{1,0:T(8,128)(2,1)S(1)} collective-permute-done((bf16[160,1024]{1,0:T(8,128)(2,1)S(1)}, bf16[160,1024]{1,0:T(8,128)(2,1)S(1)}, u32[]{:S(2)}, u32[]{:S(2)}) %collective-permute-start.5) | collective-permute-done | bytes 327712 | tf_op jit(solution)/shard_map/ppermute | solution.py:27
  29.8 1.8 %backward.1 = (bf16[2,256,1024]{2,1,0:T(8,128)(2,1)S(1)}, bf16[32,1024]{1,0:T(8,128)(2,1)S(1)}) custom-call(bf16[3,256,1024]{2,1,0:T(8,128)(2,1)S(1)} %get-tuple-element.32.x_ref, f32[3,3,1024]{2,1,0:T(4,128)S(1)} %get-tuple-element.33.taps_ref, bf16[144,1024]{1,0:T(8,128)(2,1)S(1)} %collective-permute-done.halo_ref, ...), custom_call_target="tpu_custom_call" | custom-call | bytes 1024 | tf_op jit(solution)/shard_map/backward/pallas_call | solution.py:521
  31.5 1.2 %collective-permute-start.8 = (bf16[32,1024]{1,0:T(8,128)(2,1)S(1)}, bf16[32,1024]{1,0:T(8,128)(2,1)S(1)}, u32[]{:S(2)}, u32[]{:S(2)}) collective-permute-start(bf16[32,1024]{1,0:T(8,128)(2,1)S(1)} %get-tuple-element.50), channel_id=1, source_target_pairs={{0,12},{4,8},{8,4},{12,0},{16,28},{20,24},{24,20},{28,16},{1,13},{... | collective-permute-start | bytes 196616 | tf_op jit(solution)/shard_map/ppermute | solution.py:544
  32.7 0.0 collective-permute-start.7
  32.7 1.6 %collective-permute-start.6 = (bf16[32,1024]{1,0:T(8,128)(2,1)S(1)}, bf16[32,1024]{1,0:T(8,128)(2,1)S(1)}, u32[]{:S(2)}, u32[]{:S(2)}) collective-permute-start(bf16[32,1024]{1,0:T(8,128)(2,1)S(1)} %get-tuple-element.50), channel_id=1, source_target_pairs={{0,4},{4,0},{8,12},{12,8},{16,20},{20,16},{24,28},{28,24},{1,5},{5... | collective-permute-start | bytes 196616 | tf_op jit(solution)/shard_map/ppermute | solution.py:544
  34.2 1.4 %collective-permute-done.8 = bf16[32,1024]{1,0:T(8,128)(2,1)S(1)} collective-permute-done((bf16[32,1024]{1,0:T(8,128)(2,1)S(1)}, bf16[32,1024]{1,0:T(8,128)(2,1)S(1)}, u32[]{:S(2)}, u32[]{:S(2)}) %collective-permute-start.8) | collective-permute-done | bytes 65568 | tf_op jit(solution)/shard_map/ppermute | solution.py:544
  35.6 0.8 %collective-permute-done.7 = bf16[32,1024]{1,0:T(8,128)(2,1)S(1)} collective-permute-done((bf16[32,1024]{1,0:T(8,128)(2,1)S(1)}, bf16[32,1024]{1,0:T(8,128)(2,1)S(1)}, u32[]{:S(2)}, u32[]{:S(2)}) %collective-permute-start.7) | collective-permute-done | bytes 65568 | tf_op jit(solution)/shard_map/ppermute | solution.py:544
  36.4 0.2 collective-permute-done.6
  36.6 1.6 %collective-permute-start.9 = (bf16[32,1024]{1,0:T(8,128)(2,1)S(1)}, bf16[32,1024]{1,0:T(8,128)(2,1)S(1)}, u32[]{:S(2)}, u32[]{:S(2)}) collective-permute-start(bf16[32,1024]{1,0:T(8,128)(2,1)S(1)} %add_convert_fusion.4.refs_0_), channel_id=1, source_target_pairs={{0,16},{4,20},{8,24},{12,28},{16,0},{20,4},{24,8},{28,12},{1,17},{... | collective-permute-start | bytes 196616 | tf_op jit(solution)/shard_map/ppermute | solution.py:544
  38.3 3.3 %inputs.1 = bf16[3,256,1024]{2,1,0:T(8,128)(2,1)} custom-call(bf16[3,256,1024]{2,1,0:T(8,128)(2,1)S(1)} %get-tuple-element.32.x_ref, f32[3,3,1024]{2,1,0:T(4,128)S(1)} %get-tuple-element.33.taps_ref, bf16[64,128]{1,0:T(8,128)(2,1)S(1)} %get-tuple-element.34.filt_ref, bf16[384,1024]{1,0:T(8,128)(2,1)S(1)} %get-tuple-element.46.gext_ref, ...), custom_call_target="tpu_custom_call" | custom-call | bytes 1024 | tf_op jit(solution)/shard_map/inputs/pallas_call | solution.py:528
  41.5 0.0 collective-permute-done.9.refs_1_
  41.5 0.0 collective-permute-done.2
  41.5 5.3 %collective-permute-done.4 = bf16[256,1024]{1,0:T(8,128)(2,1)S(1)} collective-permute-done((bf16[256,1024]{1,0:T(8,128)(2,1)S(1)}, bf16[256,1024]{1,0:T(8,128)(2,1)S(1)}, u32[]{:S(2)}, u32[]{:S(2)}) %collective-permute-start.4) | collective-permute-done | bytes 524320 | tf_op jit(solution)/shard_map/ppermute | solution.py:499
  46.8 0.2 add_convert_fusion
  47.0 1.7 %collective-permute-start.11 = (bf16[256,1024]{1,0:T(8,128)(2,1)S(1)}, bf16[256,1024]{1,0:T(8,128)(2,1)S(1)}, u32[]{:S(2)}, u32[]{:S(2)}) collective-permute-start(bf16[256,1024]{1,0:T(8,128)(2,1)S(1)} %add_convert_fusion), channel_id=1, source_target_pairs={{0,1},{1,0},{2,3},{3,2},{4,5},{5,4},{6,7},{7,6},{8,9},{9,8},{10,11... | collective-permute-start | bytes 1572872 | tf_op jit(solution)/shard_map/ppermute | solution.py:560
  48.7 0.2 add_convert_fusion.1
  48.9 0.1 collective-permute-start.10
  49.0 0.6 %unpack.1 = (f32[3,3,1024]{2,1,0:T(4,128)}, f32[64,128]{1,0:T(8,128)}) custom-call(bf16[32,1024]{1,0:T(8,128)(2,1)S(1)} %add_convert_fusion.4.refs_0_, bf16[32,1024]{1,0:T(8,128)(2,1)S(1)} %collective-permute-done.9.refs_1_), custom_call_target="tpu_custom_call" | custom-call | bytes 1024 | tf_op jit(solution)/shard_map/unpack/pallas_call | solution.py:566
  49.6 0.6 %collective-permute-done.11 = bf16[256,1024]{1,0:T(8,128)(2,1)S(1)} collective-permute-done((bf16[256,1024]{1,0:T(8,128)(2,1)S(1)}, bf16[256,1024]{1,0:T(8,128)(2,1)S(1)}, u32[]{:S(2)}, u32[]{:S(2)}) %collective-permute-start.11) | collective-permute-done | bytes 524320 | tf_op jit(solution)/shard_map/ppermute | solution.py:560
  50.2 0.7 %collective-permute-done.10 = bf16[256,1024]{1,0:T(8,128)(2,1)S(1)} collective-permute-done((bf16[256,1024]{1,0:T(8,128)(2,1)S(1)}, bf16[256,1024]{1,0:T(8,128)(2,1)S(1)}, u32[]{:S(2)}, u32[]{:S(2)}) %collective-permute-start.10) | collective-permute-done | bytes 524320 | tf_op jit(solution)/shard_map/ppermute | solution.py:560
  51.0 1.6 %maximum_select_fusion = bf16[256,4096]{1,0:T(8,128)(2,1)} fusion(bf16[256,1024]{1,0:T(8,128)(2,1)S(1)} %collective-permute-done.11, bf16[256,1024]{1,0:T(8,128)(2,1)S(1)} %collective-permute-done.10, bf16[256,1024]{1,0:T(8,128)(2,1)S(1)} %add_convert_fusion, bf16[256,1024]{1,0:T(8,128)(2,1)S(1)} %add_convert_fusion.1, pred[]{:T(512)S(6)} %eq.3), kind=kLoop, calls=%fused_computation | loop fusion | flops 17825792 | bytes 4194305 | tf_op jit(solution)/shard_map/jit(_where)/select_n | solution.py:561
  (1 shorter events, 0.0 us)
Async XLA Ops:
  2.3 10.7 %collective-permute-start = (bf16[144,1024]{1,0:T(8,128)(2,1)S(1)}, bf16[144,1024]{1,0:T(8,128)(2,1)S(1)}, u32[]{:S(2)}, u32[]{:S(2)}) collective-permute-start(bf16[144,1024]{1,0:T(8,128)(2,1)S(1)} %get-tuple-element.35), channel_id=1, source_target_pairs={{0,4},{4,8},{8,12},{12,16},{16,20},{20,24},{24,28},{1,5},{5,9},{9,... | collective-permute-start | bytes 884744 | tf_op jit(solution)/shard_map/ppermute | solution.py:27
  17.3 5.2 %collective-permute-start.1 = (bf16[256,1024]{1,0:T(8,128)(2,1)S(1)}, bf16[256,1024]{1,0:T(8,128)(2,1)S(1)}, u32[]{:S(2)}, u32[]{:S(2)}) collective-permute-start(bf16[256,1024]{1,0:T(8,128)(2,1)S(1)} %get-tuple-element.39), channel_id=1, source_target_pairs={{0,1},{1,0},{2,3},{3,2},{4,5},{5,4},{6,7},{7,6},{8,9},{9,8},{10,11... | collective-permute-start | bytes 1572872 | tf_op jit(solution)/shard_map/ppermute | solution.py:491
  18.9 5.1 %collective-permute-start.3 = (bf16[256,1024]{1,0:T(8,128)(2,1)S(1)}, bf16[256,1024]{1,0:T(8,128)(2,1)S(1)}, u32[]{:S(2)}, u32[]{:S(2)}) collective-permute-start(bf16[256,1024]{1,0:T(8,128)(2,1)S(1)} %get-tuple-element.41), channel_id=1, source_target_pairs={{0,1},{1,0},{2,3},{3,2},{4,5},{5,4},{6,7},{7,6},{8,9},{9,8},{10,11... | collective-permute-start | bytes 1572872 | tf_op jit(solution)/shard_map/ppermute | solution.py:491
  19.0 10.7 %collective-permute-start.5 = (bf16[160,1024]{1,0:T(8,128)(2,1)S(1)}, bf16[160,1024]{1,0:T(8,128)(2,1)S(1)}, u32[]{:S(2)}, u32[]{:S(2)}) collective-permute-start(bf16[160,1024]{1,0:T(8,128)(2,1)S(1)} %get-tuple-element.43), channel_id=1, source_target_pairs={{4,0},{8,4},{12,8},{16,12},{20,16},{24,20},{28,24},{5,1},{9,5},{13... | collective-permute-start | bytes 983048 | tf_op jit(solution)/shard_map/ppermute | solution.py:27
  22.8 18.7 %collective-permute-start.2 = (bf16[256,1024]{1,0:T(8,128)(2,1)S(1)}, bf16[256,1024]{1,0:T(8,128)(2,1)S(1)}, u32[]{:S(2)}, u32[]{:S(2)}) collective-permute-start(bf16[256,1024]{1,0:T(8,128)(2,1)S(1)} %add_convert_fusion.3), channel_id=1, source_target_pairs={{0,2},{1,3},{2,0},{3,1},{4,6},{5,7},{6,4},{7,5},{8,10},{9,11},{10,... | collective-permute-start | bytes 1572872 | tf_op jit(solution)/shard_map/ppermute | solution.py:499
  24.3 22.5 %collective-permute-start.4 = (bf16[256,1024]{1,0:T(8,128)(2,1)S(1)}, bf16[256,1024]{1,0:T(8,128)(2,1)S(1)}, u32[]{:S(2)}, u32[]{:S(2)}) collective-permute-start(bf16[256,1024]{1,0:T(8,128)(2,1)S(1)} %add_convert_fusion.2), channel_id=1, source_target_pairs={{0,2},{1,3},{2,0},{3,1},{4,6},{5,7},{6,4},{7,5},{8,10},{9,11},{10,... | collective-permute-start | bytes 1572872 | tf_op jit(solution)/shard_map/ppermute | solution.py:499
  31.5 4.1 %collective-permute-start.8 = (bf16[32,1024]{1,0:T(8,128)(2,1)S(1)}, bf16[32,1024]{1,0:T(8,128)(2,1)S(1)}, u32[]{:S(2)}, u32[]{:S(2)}) collective-permute-start(bf16[32,1024]{1,0:T(8,128)(2,1)S(1)} %get-tuple-element.50), channel_id=1, source_target_pairs={{0,12},{4,8},{8,4},{12,0},{16,28},{20,24},{24,20},{28,16},{1,13},{... | collective-permute-start | bytes 196616 | tf_op jit(solution)/shard_map/ppermute | solution.py:544
  32.7 3.8 %collective-permute-start.7 = (bf16[32,1024]{1,0:T(8,128)(2,1)S(1)}, bf16[32,1024]{1,0:T(8,128)(2,1)S(1)}, u32[]{:S(2)}, u32[]{:S(2)}) collective-permute-start(bf16[32,1024]{1,0:T(8,128)(2,1)S(1)} %get-tuple-element.50), channel_id=1, source_target_pairs={{0,8},{4,12},{8,0},{12,4},{16,24},{20,28},{24,16},{28,20},{1,9},{5... | collective-permute-start | bytes 196616 | tf_op jit(solution)/shard_map/ppermute | solution.py:544
  32.7 3.9 %collective-permute-start.6 = (bf16[32,1024]{1,0:T(8,128)(2,1)S(1)}, bf16[32,1024]{1,0:T(8,128)(2,1)S(1)}, u32[]{:S(2)}, u32[]{:S(2)}) collective-permute-start(bf16[32,1024]{1,0:T(8,128)(2,1)S(1)} %get-tuple-element.50), channel_id=1, source_target_pairs={{0,4},{4,0},{8,12},{12,8},{16,20},{20,16},{24,28},{28,24},{1,5},{5... | collective-permute-start | bytes 196616 | tf_op jit(solution)/shard_map/ppermute | solution.py:544
  36.6 4.9 %collective-permute-start.9 = (bf16[32,1024]{1,0:T(8,128)(2,1)S(1)}, bf16[32,1024]{1,0:T(8,128)(2,1)S(1)}, u32[]{:S(2)}, u32[]{:S(2)}) collective-permute-start(bf16[32,1024]{1,0:T(8,128)(2,1)S(1)} %add_convert_fusion.4.refs_0_), channel_id=1, source_target_pairs={{0,16},{4,20},{8,24},{12,28},{16,0},{20,4},{24,8},{28,12},{1,17},{... | collective-permute-start | bytes 196616 | tf_op jit(solution)/shard_map/ppermute | solution.py:544
  47.0 3.2 %collective-permute-start.11 = (bf16[256,1024]{1,0:T(8,128)(2,1)S(1)}, bf16[256,1024]{1,0:T(8,128)(2,1)S(1)}, u32[]{:S(2)}, u32[]{:S(2)}) collective-permute-start(bf16[256,1024]{1,0:T(8,128)(2,1)S(1)} %add_convert_fusion), channel_id=1, source_target_pairs={{0,1},{1,0},{2,3},{3,2},{4,5},{5,4},{6,7},{7,6},{8,9},{9,8},{10,11... | collective-permute-start | bytes 1572872 | tf_op jit(solution)/shard_map/ppermute | solution.py:560
  48.9 2.1 %collective-permute-start.10 = (bf16[256,1024]{1,0:T(8,128)(2,1)S(1)}, bf16[256,1024]{1,0:T(8,128)(2,1)S(1)}, u32[]{:S(2)}, u32[]{:S(2)}) collective-permute-start(bf16[256,1024]{1,0:T(8,128)(2,1)S(1)} %add_convert_fusion.1), channel_id=1, source_target_pairs={{0,1},{1,0},{2,3},{3,2},{4,5},{5,4},{6,7},{7,6},{8,9},{9,8},{10,11... | collective-permute-start | bytes 1572872 | tf_op jit(solution)/shard_map/ppermute | solution.py:560

commit v6 on v5

--- a/solution.py
+++ b/solution.py
@@ -9,6 +9,7 @@
 
 LANES = 128
 RIM = 16
+EDGE = 8
 SUB = 32
 COST = 1024
 PIECES = 2
@@ -114,30 +115,31 @@
 ):
     _, rows, chans = x_ref.shape
     first = rows - LANES - RIM
-    near = (pl.ds(1, 2), pl.ds(first, LANES + RIM))
-    copies = [
-        pltpu.make_async_copy(taps_hbm, taps_ref, sems.at[0]),
-        pltpu.make_async_copy(x_hbm.at[near], x_ref.at[near], sems.at[1]),
-        pltpu.make_async_copy(x_hbm.at[0], x_ref.at[0], sems.at[2]),
-        pltpu.make_async_copy(
-            x_hbm.at[1:3, 0:first], x_ref.at[1:3, 0:first], sems.at[3]
-        ),
-        pltpu.make_async_copy(filt_hbm, filt_ref, sems.at[4]),
-    ]
+    regions = (
+        (pl.ds(1, 2), pl.ds(first, LANES + RIM)),
+        (pl.ds(0, 1), pl.ds(rows - RIM, RIM)),
+        (pl.ds(0, 1), pl.ds(0, rows - RIM)),
+        (pl.ds(1, 2), pl.ds(0, first)),
+    )
+    copies = [pltpu.make_async_copy(taps_hbm, taps_ref, sems.at[0])]
+    for i, region in enumerate(regions):
+        copies.append(
+            pltpu.make_async_copy(x_hbm.at[region], x_ref.at[region], sems.at[1 + i])
+        )
+    copies.append(pltpu.make_async_copy(filt_hbm, filt_ref, sems.at[5]))
     for copy in copies:
         copy.start()
     for copy in copies[:3]:
         copy.wait()
 
     def tile(j, lanes, ext):
-        for part in range(3):
+        for part in range(1, 3):
             ext[part, 8:, :] = x_ref[part, first:, lanes].astype(F32)
         keyed = feature(ext, taps_ref, lanes, 1, RIM, LANES)
         valued = feature(ext, taps_ref, lanes, 2, RIM, LANES)
         sent_ref[0:LANES, lanes] = (keyed * valued).astype(BF16)
-        end = 8 + RIM + LANES
-        rim = [ext[part, end - 2 : end, :] for part in range(3)]
-        rim.append(jnp.zeros((RIM - 6, LANES), F32))
+        rim = [x_ref[part, rows - RIM :, lanes].astype(F32)[RIM - 2 :] for part in range(3)]
+        rim.append(jnp.zeros((EDGE - 6, LANES), F32))
         sent_ref[LANES:, lanes] = jnp.concatenate(rim, axis=0).astype(BF16)
 
     each_tile(chans, tile, ext_ref)
@@ -174,22 +176,25 @@
         gg_ref[:, cols] = lax.dot_general(
             c_ref[...], w_ref[cols, :], (((1,), (1,)), ((), ())), preferred_element_type=F32
         )
+        for i in range(wide // LANES):
+            at = pl.multiple_of(j * wide + i * LANES, LANES)
+            tile(pl.ds(at, LANES), ext_ref.at[i])
         return carry
 
-    lax.fori_loop(0, chunks, product, 0)
-
-    def tile(j, lanes, ext):
+    def tile(lanes, ext):
         ext[0, 0:8, :] = jnp.zeros((8, LANES), F32)
         ext[0, 8:, :] = x_ref[0, 0:span, lanes].astype(F32)
         query = feature(ext, taps_ref, lanes, 0, 0, span)
-        back_ref[0:span, lanes] = (gg_ref[0:span, lanes] * query).astype(BF16)
+        grad_mixed = (gg_ref[0:span, lanes] * query).astype(BF16).astype(F32)
+        back_ref[0:LANES, lanes] = grad_mixed[0:LANES].astype(BF16)
         grad = gg_ref[0:2, lanes]
         high = grad.astype(BF16).astype(F32)
         rim = [x_ref[part, 0:RIM, lanes].astype(F32)[0:2] for part in range(3)]
-        rim += [high, grad - high, jnp.zeros((RIM - 10, LANES), F32)]
-        back_ref[span:, lanes] = jnp.concatenate(rim, axis=0).astype(BF16)
-
-    each_tile(chans, tile, ext_ref)
+        rim += [high, grad - high, jnp.zeros((RIM - 11, LANES), F32)]
+        rim.insert(0, grad_mixed[LANES : LANES + 1])
+        back_ref[LANES:, lanes] = jnp.concatenate(rim, axis=0).astype(BF16)
+
+    lax.fori_loop(0, chunks, product, 0)
 
 
 def forward_kernel(
@@ -316,17 +321,14 @@
 
 def next_rows(ext_ref, taps_ref, x_ref, back_ref, lanes, parts):
     rows = x_ref.shape[1]
-    span = LANES + RIM
+    rim = back_ref[LANES:, lanes].astype(F32)
     outs = []
     for part in parts:
         recent = x_ref[part, rows - RIM :, lanes].astype(F32)
-        at = span + 2 * part
         ext_ref[part, 0:8, :] = recent[RIM - 8 :]
-        ext_ref[part, 8:10, :] = back_ref[at : at + 2, lanes].astype(F32)
+        ext_ref[part, 8:10, :] = rim[1 + 2 * part : 3 + 2 * part]
         outs.append(feature(ext_ref, taps_ref, lanes, part, 0, 2))
-    high = back_ref[span + 6 : span + 8, lanes].astype(F32)
-    low = back_ref[span + 8 : span + 10, lanes].astype(F32)
-    return outs, high + low
+    return outs, rim[7:9] + rim[9:11]
 
 
 def next_mixed(back_ref, lanes, grad, query):
@@ -425,6 +427,36 @@
             short_ref[lag, part : part + 1, :] = total[at : at + 1] * short_scale
 
 
+def place_kernel(first, which_ref, own_ref, sibling_ref, *refs):
+    out_ref, sems = refs[-2:]
+    half = out_ref.shape[1] // 2
+    copies = []
+    for i, ref in enumerate((own_ref, sibling_ref)):
+        side = which_ref[0] if i == 0 else 1 - which_ref[0]
+        cols = pl.ds(pl.multiple_of(side * half + first, LANES), ref.shape[1])
+        copies.append(pltpu.make_async_copy(ref, out_ref.at[:, cols], sems.at[i]))
+    for copy in copies:
+        copy.start()
+    for copy in copies:
+        copy.wait()
+
+
+def place(result, which, own, sibling, first, width):
+    far = pl.BlockSpec(memory_space=pltpu.HBM)
+    near = pl.BlockSpec(memory_space=pltpu.VMEM)
+    operands = (which, own, sibling) + (() if result is None else (result,))
+    return pl.pallas_call(
+        functools.partial(place_kernel, first),
+        out_shape=shape((own.shape[0], width), BF16),
+        in_specs=[pl.BlockSpec(memory_space=pltpu.SMEM), near, near, far][: len(operands)],
+        out_specs=far,
+        scratch_shapes=[pltpu.SemaphoreType.DMA((2,))],
+        compiler_params=pltpu.CompilerParams(vmem_limit_bytes=VMEM_LIMIT),
+        input_output_aliases={} if result is None else {3: 0},
+        name="place",
+    )(*operands)
+
+
 def local(inputs, short_filter, long_filter, out_weight, out_cotangent):
     rows, _, chans = inputs.shape
     groups, span = long_filter.shape
@@ -445,12 +477,12 @@
         tail_kernel,
         "tail",
         (
-            shape((LANES + RIM, chans), BF16),
+            shape((LANES + EDGE, chans), BF16),
             shape(signal.shape, BF16),
             shape(short_filter.shape, F32),
             shape(long_filter.shape, BF16),
         ),
-        [pltpu.VMEM((tiles, 3, 8 + RIM + LANES, LANES), F32), pltpu.SemaphoreType.DMA((5,))],
+        [pltpu.VMEM((tiles, 3, 8 + RIM + LANES, LANES), F32), pltpu.SemaphoreType.DMA((6,))],
         far=3,
     )(signal, short_filter, long_filter)
     halo = shifted(sent, "ctx", 1)
@@ -459,7 +491,7 @@
         "grad_gate",
         (
             shape((rows, chans), F32),
-            shape((LANES + 2 * RIM, chans), BF16),
+            shape((LANES + RIM, chans), BF16),
             shape(out_weight.shape, BF16),
         ),
         [
@@ -543,10 +575,12 @@
             terms += [
                 lax.ppermute(terms[0], "ctx", pairwise("ctx", i * hop)) for i in range(1, radix)
             ]
+            if hop == 1:
+                terms, grad_in = lax.optimization_barrier((terms, grad_in))
             hop *= radix
     else:
         terms = [lax.psum(sums, "ctx")]
-    got, terms, grad_in = lax.optimization_barrier((got, terms, grad_in))
+    got, terms = lax.optimization_barrier((got, terms))
     mine = [
         (a.astype(F32) + b.astype(F32)).astype(BF16) for a, b in zip(mine, got, strict=True)
     ]
@@ -558,11 +592,11 @@
         ]
         step *= 2
     sibling = [lax.ppermute(value, "tp", pairwise("tp", 1)) for value in mine]
-    result = jnp.where(
-        core == 0,
-        jnp.concatenate(mine + sibling, axis=1),
-        jnp.concatenate(sibling + mine, axis=1),
-    )
+    result = None
+    for i in reversed(range(PIECES)):
+        result = place(
+            result, jnp.reshape(core, (1,)), mine[i], sibling[i], i * (width // 2 // PIECES), width
+        )
     grad_short, grad_long = call(
         functools.partial(
             unpack_kernel, group, float(tokens_all) ** (-0.5), float(tokens_all * group) ** (-0.5)

time: 52.8 us -> 52.1 us (0.987)
  Pallas kernels: 21.9 us -> 23.5 us
  other arithmetic: 2.36 us -> 0.8 us
  starting transfers between devices: 14.7 us -> 13.8 us
    pallas_call x1 -> x3, Pallas kernels: 1.68 us -> 3.49 us  [the longest x2 1.97 us: place(): pl.pallas_call(functools.partial(place_kernel, first), out_shape=shape((o...]
    ppermute x4, waiting for transfers between devices: 2.36 us -> 4.11 us  [local(): lax.ppermute(terms[0], 'ctx', pairwise('ctx', i * hop))]
    select_n x1 -> x0, other arithmetic: 1.56 us -> none  [local(): jnp.where(core == 0, jnp.concatenate(mine + sibling, axis=1), jnp.concate...]
    ppermute x4, starting transfers between devices: 4.33 us -> 3.4 us  [local(): lax.ppermute(terms[0], 'ctx', pairwise('ctx', i * hop))]
    ppermute x2, waiting for transfers between devices: 3.78 us -> 2.93 us  [shifted(): lax.ppermute(value, axis, [(source, source + steps) for source in range(i...]
    ppermute x2, waiting for transfers between devices: 1.35 us -> 0.61 us  [local(): sibling = [lax.ppermute(value, 'tp', pairwise('tp', 1)) for value in mine]]
  transfers between devices with their start and end apart: 12 -> 12, of which waited for: 8 -> 5; matrix products, arithmetic and copies ran while one was open for 1% -> 1% of each run, Pallas kernels for 30% -> 32%
where the time goes in v6:
time: 52.1 us; the launch traced here: 51.9 us
  Pallas kernels  23.5 us (45%)
  starting transfers between devices  13.8 us (26%)
  waiting for transfers between devices  12.8 us (25%)
  between operations  0.93 us (2%)
  other arithmetic  0.8 us (2%)
    pallas_call x1, Pallas kernels, local(): call(grad_gate_kernel, 'grad_gate', (shape((rows, chans), F32), shape((LA...  5.55 us
    ppermute x2, starting transfers between devices, shifted(): lax.ppermute(value, axis, [(source, source + steps) for source in range(i...  5.38 us
    ppermute x2, waiting for transfers between devices, local(): got = [lax.ppermute(value, 'tp', pairwise('tp', step)) for value in mine]  5.18 us
    pallas_call x1, Pallas kernels, local(): call(functools.partial(forward_kernel, group), 'forward', (piece,) * PIEC...  4.33 us
    ppermute x4, waiting for transfers between devices, local(): lax.ppermute(terms[0], 'ctx', pairwise('ctx', i * hop))  4.11 us
    ppermute x4, starting transfers between devices, local(): lax.ppermute(terms[0], 'ctx', pairwise('ctx', i * hop))  3.4 us
    pallas_call x1, Pallas kernels, local(): call(functools.partial(inputs_kernel, group), 'inputs', shape((3, rows, c...  3.27 us
    pallas_call x1, Pallas kernels, local(): call(functools.partial(lags_kernel, group), 'lags', (shape((rows, chans),...  3.17 us
  transfers between devices with their start and end apart: 12, of which 5 were waited for; matrix products, arithmetic and copies ran while one was open for 1% of the time, Pallas kernels for 32%

profile of v6, /device:TPU:25, one launch (start us, length us, event | category | flops | bytes accessed | tf_op | source)
XLA Modules:
  0.0 51.9 jit_solution(12076879228521081409)
XLA Ops:
  0.6 1.5 %tail.1 = (bf16[136,1024]{1,0:T(8,128)(2,1)S(1)}, bf16[3,256,1024]{2,1,0:T(8,128)(2,1)S(1)}, f32[3,3,1024]{2,1,0:T(4,128)S(1)}, bf16[64,128]{1,0:T(8,128)(2,1)S(1)}) custom-call(bf16[3,256,1024]{2,1,0:T(8,128)(2,1)} %bitcast.4, f32[3,3,1024]{2,1,0:T(4,128)} %taps_hbm.1, bf16[64,128]{1,0:T(8,128)(2,1)} %filt_hbm.1), custom_call_target="tpu_custom_call" | custom-call | bytes 1024 | tf_op jit(solution)/shard_map/tail/pallas_call | solution.py:476
  2.2 3.1 %collective-permute-start = (bf16[136,1024]{1,0:T(8,128)(2,1)S(1)}, bf16[136,1024]{1,0:T(8,128)(2,1)S(1)}, u32[]{:S(2)}, u32[]{:S(2)}) collective-permute-start(bf16[136,1024]{1,0:T(8,128)(2,1)S(1)} %get-tuple-element.39), channel_id=1, source_target_pairs={{0,4},{4,8},{8,12},{12,16},{16,20},{20,24},{24,28},{1,5},{5,9},{9,... | collective-permute-start | bytes 835592 | tf_op jit(solution)/shard_map/ppermute | solution.py:28
  5.3 5.6 %grad_gate.1 = (f32[256,1024]{1,0:T(8,128)S(1)}, bf16[144,1024]{1,0:T(8,128)(2,1)S(1)}, bf16[1024,4096]{1,0:T(8,128)(2,1)S(1)}) custom-call(bf16[256,4096]{1,0:T(8,128)(2,1)} %c_hbm.1, bf16[1024,4096]{1,0:T(8,128)(2,1)} %w_hbm.1, bf16[3,256,1024]{2,1,0:T(8,128)(2,1)S(1)} %get-tuple-element.36.x_ref, f32[3,3,1024]{2,1,0:T(4,128)S(1)} %get-tuple-element.37.taps_ref), custom_call_target="tpu_custom_call" | custom-call | bytes 1024 | tf_op jit(solution)/shard_map/grad_gate/pallas_call | solution.py:489
  10.8 1.6 %collective-permute-done.halo_ref = bf16[136,1024]{1,0:T(8,128)(2,1)S(1)} collective-permute-done((bf16[136,1024]{1,0:T(8,128)(2,1)S(1)}, bf16[136,1024]{1,0:T(8,128)(2,1)S(1)}, u32[]{:S(2)}, u32[]{:S(2)}) %collective-permute-start) | collective-permute-done | bytes 278560 | tf_op jit(solution)/shard_map/ppermute | solution.py:28
  12.5 4.3 %forward.1 = (bf16[256,1024]{1,0:T(8,128)(2,1)S(1)}, bf16[256,1024]{1,0:T(8,128)(2,1)S(1)}, bf16[256,1024]{1,0:T(8,128)(2,1)S(1)}, f32[256,1024]{1,0:T(8,128)S(1...) custom-call(s32[1]{0:T(128)} %bitcast.1.which_ref, bf16[3,256,1024]{2,1,0:T(8,128)(2,1)S(1)} %get-tuple-element.36.x_ref, ...), custom_call_target="tpu_custom_call" | custom-call | bytes 1024 | tf_op jit(solution)/shard_map/forward/pallas_call | solution.py:509
  16.8 1.6 %collective-permute-start.1 = (bf16[256,1024]{1,0:T(8,128)(2,1)S(1)}, bf16[256,1024]{1,0:T(8,128)(2,1)S(1)}, u32[]{:S(2)}, u32[]{:S(2)}) collective-permute-start(bf16[256,1024]{1,0:T(8,128)(2,1)S(1)} %get-tuple-element.43), channel_id=1, source_target_pairs={{0,1},{1,0},{2,3},{3,2},{4,5},{5,4},{6,7},{7,6},{8,9},{9,8},{10,11... | collective-permute-start | bytes 1572872 | tf_op jit(solution)/shard_map/ppermute | solution.py:523
  18.4 0.1 collective-permute-start.3
  18.5 2.3 %collective-permute-start.5 = (bf16[144,1024]{1,0:T(8,128)(2,1)S(1)}, bf16[144,1024]{1,0:T(8,128)(2,1)S(1)}, u32[]{:S(2)}, u32[]{:S(2)}) collective-permute-start(bf16[144,1024]{1,0:T(8,128)(2,1)S(1)} %get-tuple-element.47), channel_id=1, source_target_pairs={{4,0},{8,4},{12,8},{16,12},{20,16},{24,20},{28,24},{5,1},{9,5},{13... | collective-permute-start | bytes 884744 | tf_op jit(solution)/shard_map/ppermute | solution.py:28
  20.8 1.3 %keep.1 = (bf16[256,1024]{1,0:T(8,128)(2,1)S(1)}, bf16[256,1024]{1,0:T(8,128)(2,1)S(1)}) custom-call(s32[1]{0:T(128)} %bitcast.which_ref, bf16[256,1024]{1,0:T(8,128)(2,1)S(1)} %get-tuple-element.41.gate_ref, bf16[1024,4096]{1,0:T(8,128)(2,1)S(1)} %get-tuple-element.40.w_ref), custom_call_target="tpu_custom_call" | custom-call | bytes 1024 | tf_op jit(solution)/shard_map/keep/pallas_call | solution.py:524
  22.1 0.0 collective-permute-done.1
  22.1 0.2 add_convert_fusion.3
  22.3 1.3 %collective-permute-start.2 = (bf16[256,1024]{1,0:T(8,128)(2,1)S(1)}, bf16[256,1024]{1,0:T(8,128)(2,1)S(1)}, u32[]{:S(2)}, u32[]{:S(2)}) collective-permute-start(bf16[256,1024]{1,0:T(8,128)(2,1)S(1)} %add_convert_fusion.3), channel_id=1, source_target_pairs={{0,2},{1,3},{2,0},{3,1},{4,6},{5,7},{6,4},{7,5},{8,10},{9,11},{10,... | collective-permute-start | bytes 1572872 | tf_op jit(solution)/shard_map/ppermute | solution.py:531
  23.6 0.0 collective-permute-done.3
  23.6 0.2 add_convert_fusion.2
  23.8 0.3 collective-permute-start.4
  24.1 3.2 %lags.1 = (bf16[256,1024]{1,0:T(8,128)(2,1)S(1)}, bf16[256,1024]{1,0:T(8,128)(2,1)S(1)}, f32[16,1024]{1,0:T(8,128)S(1)}, bf16[8,256,160]{2,1,0:T(8,128)(2,1)S(1)}) custom-call(bf16[64,128]{1,0:T(8,128)(2,1)S(1)} %get-tuple-element.38.filt_ref, bf16[3,256,1024]{2,1,0:T(8,128)(2,1)S(1)} %get-tuple-element.36.x_ref, ...), custom_call_target="tpu_custom_call" | custom-call | bytes 1024 | tf_op jit(solution)/shard_map/lags/pallas_call | solution.py:535
  27.2 1.3 %collective-permute-done.5.back_ref = bf16[144,1024]{1,0:T(8,128)(2,1)S(1)} collective-permute-done((bf16[144,1024]{1,0:T(8,128)(2,1)S(1)}, bf16[144,1024]{1,0:T(8,128)(2,1)S(1)}, u32[]{:S(2)}, u32[]{:S(2)}) %collective-permute-start.5) | collective-permute-done | bytes 294944 | tf_op jit(solution)/shard_map/ppermute | solution.py:28
  28.5 1.8 %backward.1 = (bf16[2,256,1024]{2,1,0:T(8,128)(2,1)S(1)}, bf16[32,1024]{1,0:T(8,128)(2,1)S(1)}) custom-call(bf16[3,256,1024]{2,1,0:T(8,128)(2,1)S(1)} %get-tuple-element.36.x_ref, f32[3,3,1024]{2,1,0:T(4,128)S(1)} %get-tuple-element.37.taps_ref, bf16[136,1024]{1,0:T(8,128)(2,1)S(1)} %collective-permute-done.halo_ref, ...), custom_call_target="tpu_custom_call" | custom-call | bytes 1024 | tf_op jit(solution)/shard_map/backward/pallas_call | solution.py:553
  30.3 1.2 %collective-permute-start.8 = (bf16[32,1024]{1,0:T(8,128)(2,1)S(1)}, bf16[32,1024]{1,0:T(8,128)(2,1)S(1)}, u32[]{:S(2)}, u32[]{:S(2)}) collective-permute-start(bf16[32,1024]{1,0:T(8,128)(2,1)S(1)} %get-tuple-element.57), channel_id=1, source_target_pairs={{0,12},{4,8},{8,4},{12,0},{16,28},{20,24},{24,20},{28,16},{1,13},{... | collective-permute-start | bytes 196616 | tf_op jit(solution)/shard_map/ppermute | solution.py:576
  31.5 0.1 collective-permute-start.7
  31.6 1.5 %collective-permute-start.6 = (bf16[32,1024]{1,0:T(8,128)(2,1)S(1)}, bf16[32,1024]{1,0:T(8,128)(2,1)S(1)}, u32[]{:S(2)}, u32[]{:S(2)}) collective-permute-start(bf16[32,1024]{1,0:T(8,128)(2,1)S(1)} %get-tuple-element.57), channel_id=1, source_target_pairs={{0,4},{4,0},{8,12},{12,8},{16,20},{20,16},{24,28},{28,24},{1,5},{5... | collective-permute-start | bytes 196616 | tf_op jit(solution)/shard_map/ppermute | solution.py:576
  33.0 3.3 %inputs.1 = bf16[3,256,1024]{2,1,0:T(8,128)(2,1)} custom-call(bf16[3,256,1024]{2,1,0:T(8,128)(2,1)S(1)} %get-tuple-element.36.x_ref, f32[3,3,1024]{2,1,0:T(4,128)S(1)} %get-tuple-element.37.taps_ref, bf16[64,128]{1,0:T(8,128)(2,1)S(1)} %get-tuple-element.38.filt_ref, bf16[384,1024]{1,0:T(8,128)(2,1)S(1)} %get-tuple-element.50.gext_ref, ...), custom_call_target="tpu_custom_call" | custom-call | bytes 1024 | tf_op jit(solution)/shard_map/inputs/pallas_call | solution.py:560
  36.3 0.0 collective-permute-done.8
  36.3 0.0 collective-permute-done.7
  36.3 0.0 collective-permute-done.6
  36.4 0.7 %collective-permute-start.9 = (bf16[32,1024]{1,0:T(8,128)(2,1)S(1)}, bf16[32,1024]{1,0:T(8,128)(2,1)S(1)}, u32[]{:S(2)}, u32[]{:S(2)}) collective-permute-start(bf16[32,1024]{1,0:T(8,128)(2,1)S(1)} %add_convert_fusion.4.refs_0_), channel_id=1, source_target_pairs={{0,16},{4,20},{8,24},{12,28},{16,0},{20,4},{24,8},{28,12},{1,17},{... | collective-permute-start | bytes 196616 | tf_op jit(solution)/shard_map/ppermute | solution.py:576
  37.0 4.1 %collective-permute-done.9.refs_1_ = bf16[32,1024]{1,0:T(8,128)(2,1)S(1)} collective-permute-done((bf16[32,1024]{1,0:T(8,128)(2,1)S(1)}, bf16[32,1024]{1,0:T(8,128)(2,1)S(1)}, u32[]{:S(2)}, u32[]{:S(2)}) %collective-permute-start.9) | collective-permute-done | bytes 65568 | tf_op jit(solution)/shard_map/ppermute | solution.py:576
  41.1 0.0 collective-permute-done.2
  41.1 5.2 %collective-permute-done.4 = bf16[256,1024]{1,0:T(8,128)(2,1)S(1)} collective-permute-done((bf16[256,1024]{1,0:T(8,128)(2,1)S(1)}, bf16[256,1024]{1,0:T(8,128)(2,1)S(1)}, u32[]{:S(2)}, u32[]{:S(2)}) %collective-permute-start.4) | collective-permute-done | bytes 524320 | tf_op jit(solution)/shard_map/ppermute | solution.py:531
  46.3 0.2 add_convert_fusion.own_ref
  46.5 1.7 %collective-permute-start.11 = (bf16[256,1024]{1,0:T(8,128)(2,1)S(1)}, bf16[256,1024]{1,0:T(8,128)(2,1)S(1)}, u32[]{:S(2)}, u32[]{:S(2)}) collective-permute-start(bf16[256,1024]{1,0:T(8,128)(2,1)S(1)} %add_convert_fusion.own_ref), channel_id=1, source_target_pairs={{0,1},{1,0},{2,3},{3,2},{4,5},{5,4},{6,7},{7,6},{8,9},{9,8},{10,11... | collective-permute-start | bytes 1572872 | tf_op jit(solution)/shard_map/ppermute | solution.py:594
  48.2 0.2 add_convert_fusion.1.own_ref
  48.4 0.1 collective-permute-start.10
  48.4 0.6 %unpack.1 = (f32[3,3,1024]{2,1,0:T(4,128)}, f32[64,128]{1,0:T(8,128)}) custom-call(bf16[32,1024]{1,0:T(8,128)(2,1)S(1)} %add_convert_fusion.4.refs_0_, bf16[32,1024]{1,0:T(8,128)(2,1)S(1)} %collective-permute-done.9.refs_1_), custom_call_target="tpu_custom_call" | custom-call | bytes 1024 | tf_op jit(solution)/shard_map/unpack/pallas_call | solution.py:600
  49.1 0.6 %collective-permute-done.11.sibling_ref = bf16[256,1024]{1,0:T(8,128)(2,1)S(1)} collective-permute-done((bf16[256,1024]{1,0:T(8,128)(2,1)S(1)}, bf16[256,1024]{1,0:T(8,128)(2,1)S(1)}, u32[]{:S(2)}, u32[]{:S(2)}) %collective-permute-start.11) | collective-permute-done | bytes 524320 | tf_op jit(solution)/shard_map/ppermute | solution.py:594
  49.7 1.0 %place.2.refs_0_ = bf16[256,4096]{1,0:T(8,128)(2,1)} custom-call(s32[1]{0:T(128)} %bitcast.which_ref, bf16[256,1024]{1,0:T(8,128)(2,1)S(1)} %add_convert_fusion.own_ref, bf16[256,1024]{1,0:T(8,128)(2,1)S(1)} %collective-permute-done.11.sibling_ref), custom_call_target="tpu_custom_call" | custom-call | tf_op jit(solution)/shard_map/place/pallas_call | solution.py:448
  50.7 0.0 collective-permute-done.10.sibling_ref
  50.7 1.0 %place.3 = bf16[256,4096]{1,0:T(8,128)(2,1)} custom-call(s32[1]{0:T(128)} %bitcast.which_ref, bf16[256,1024]{1,0:T(8,128)(2,1)S(1)} %add_convert_fusion.1.own_ref, bf16[256,1024]{1,0:T(8,128)(2,1)S(1)} %collective-permute-done.10.sibling_ref, bf16[256,4096]{1,0:T(8,128)(2,1)} %place.2.refs_0_), custom_call_target="tpu_custom_call", output_to_operand_aliasing={{}: (3, {})} | custom-call | tf_op jit(solution)/shard_map/place/pallas_call | solution.py:448
  (1 shorter events, 0.0 us)
Async XLA Ops:
  2.2 10.3 %collective-permute-start = (bf16[136,1024]{1,0:T(8,128)(2,1)S(1)}, bf16[136,1024]{1,0:T(8,128)(2,1)S(1)}, u32[]{:S(2)}, u32[]{:S(2)}) collective-permute-start(bf16[136,1024]{1,0:T(8,128)(2,1)S(1)} %get-tuple-element.39), channel_id=1, source_target_pairs={{0,4},{4,8},{8,12},{12,16},{16,20},{20,24},{24,28},{1,5},{5,9},{9,... | collective-permute-start | bytes 835592 | tf_op jit(solution)/shard_map/ppermute | solution.py:28
  16.8 5.2 %collective-permute-start.1 = (bf16[256,1024]{1,0:T(8,128)(2,1)S(1)}, bf16[256,1024]{1,0:T(8,128)(2,1)S(1)}, u32[]{:S(2)}, u32[]{:S(2)}) collective-permute-start(bf16[256,1024]{1,0:T(8,128)(2,1)S(1)} %get-tuple-element.43), channel_id=1, source_target_pairs={{0,1},{1,0},{2,3},{3,2},{4,5},{5,4},{6,7},{7,6},{8,9},{9,8},{10,11... | collective-permute-start | bytes 1572872 | tf_op jit(solution)/shard_map/ppermute | solution.py:523
  18.4 5.1 %collective-permute-start.3 = (bf16[256,1024]{1,0:T(8,128)(2,1)S(1)}, bf16[256,1024]{1,0:T(8,128)(2,1)S(1)}, u32[]{:S(2)}, u32[]{:S(2)}) collective-permute-start(bf16[256,1024]{1,0:T(8,128)(2,1)S(1)} %get-tuple-element.45), channel_id=1, source_target_pairs={{0,1},{1,0},{2,3},{3,2},{4,5},{5,4},{6,7},{7,6},{8,9},{9,8},{10,11... | collective-permute-start | bytes 1572872 | tf_op jit(solution)/shard_map/ppermute | solution.py:523
  18.5 10.0 %collective-permute-start.5 = (bf16[144,1024]{1,0:T(8,128)(2,1)S(1)}, bf16[144,1024]{1,0:T(8,128)(2,1)S(1)}, u32[]{:S(2)}, u32[]{:S(2)}) collective-permute-start(bf16[144,1024]{1,0:T(8,128)(2,1)S(1)} %get-tuple-element.47), channel_id=1, source_target_pairs={{4,0},{8,4},{12,8},{16,12},{20,16},{24,20},{28,24},{5,1},{9,5},{13... | collective-permute-start | bytes 884744 | tf_op jit(solution)/shard_map/ppermute | solution.py:28
  22.3 18.9 %collective-permute-start.2 = (bf16[256,1024]{1,0:T(8,128)(2,1)S(1)}, bf16[256,1024]{1,0:T(8,128)(2,1)S(1)}, u32[]{:S(2)}, u32[]{:S(2)}) collective-permute-start(bf16[256,1024]{1,0:T(8,128)(2,1)S(1)} %add_convert_fusion.3), channel_id=1, source_target_pairs={{0,2},{1,3},{2,0},{3,1},{4,6},{5,7},{6,4},{7,5},{8,10},{9,11},{10,... | collective-permute-start | bytes 1572872 | tf_op jit(solution)/shard_map/ppermute | solution.py:531
  23.8 22.5 %collective-permute-start.4 = (bf16[256,1024]{1,0:T(8,128)(2,1)S(1)}, bf16[256,1024]{1,0:T(8,128)(2,1)S(1)}, u32[]{:S(2)}, u32[]{:S(2)}) collective-permute-start(bf16[256,1024]{1,0:T(8,128)(2,1)S(1)} %add_convert_fusion.2), channel_id=1, source_target_pairs={{0,2},{1,3},{2,0},{3,1},{4,6},{5,7},{6,4},{7,5},{8,10},{9,11},{10,... | collective-permute-start | bytes 1572872 | tf_op jit(solution)/shard_map/ppermute | solution.py:531
  30.3 6.0 %collective-permute-start.8 = (bf16[32,1024]{1,0:T(8,128)(2,1)S(1)}, bf16[32,1024]{1,0:T(8,128)(2,1)S(1)}, u32[]{:S(2)}, u32[]{:S(2)}) collective-permute-start(bf16[32,1024]{1,0:T(8,128)(2,1)S(1)} %get-tuple-element.57), channel_id=1, source_target_pairs={{0,12},{4,8},{8,4},{12,0},{16,28},{20,24},{24,20},{28,16},{1,13},{... | collective-permute-start | bytes 196616 | tf_op jit(solution)/shard_map/ppermute | solution.py:576
  31.5 4.8 %collective-permute-start.7 = (bf16[32,1024]{1,0:T(8,128)(2,1)S(1)}, bf16[32,1024]{1,0:T(8,128)(2,1)S(1)}, u32[]{:S(2)}, u32[]{:S(2)}) collective-permute-start(bf16[32,1024]{1,0:T(8,128)(2,1)S(1)} %get-tuple-element.57), channel_id=1, source_target_pairs={{0,8},{4,12},{8,0},{12,4},{16,24},{20,28},{24,16},{28,20},{1,9},{5... | collective-permute-start | bytes 196616 | tf_op jit(solution)/shard_map/ppermute | solution.py:576
  31.6 4.8 %collective-permute-start.6 = (bf16[32,1024]{1,0:T(8,128)(2,1)S(1)}, bf16[32,1024]{1,0:T(8,128)(2,1)S(1)}, u32[]{:S(2)}, u32[]{:S(2)}) collective-permute-start(bf16[32,1024]{1,0:T(8,128)(2,1)S(1)} %get-tuple-element.57), channel_id=1, source_target_pairs={{0,4},{4,0},{8,12},{12,8},{16,20},{20,16},{24,28},{28,24},{1,5},{5... | collective-permute-start | bytes 196616 | tf_op jit(solution)/shard_map/ppermute | solution.py:576
  36.4 4.8 %collective-permute-start.9 = (bf16[32,1024]{1,0:T(8,128)(2,1)S(1)}, bf16[32,1024]{1,0:T(8,128)(2,1)S(1)}, u32[]{:S(2)}, u32[]{:S(2)}) collective-permute-start(bf16[32,1024]{1,0:T(8,128)(2,1)S(1)} %add_convert_fusion.4.refs_0_), channel_id=1, source_target_pairs={{0,16},{4,20},{8,24},{12,28},{16,0},{20,4},{24,8},{28,12},{1,17},{... | collective-permute-start | bytes 196616 | tf_op jit(solution)/shard_map/ppermute | solution.py:576
  46.5 3.2 %collective-permute-start.11 = (bf16[256,1024]{1,0:T(8,128)(2,1)S(1)}, bf16[256,1024]{1,0:T(8,128)(2,1)S(1)}, u32[]{:S(2)}, u32[]{:S(2)}) collective-permute-start(bf16[256,1024]{1,0:T(8,128)(2,1)S(1)} %add_convert_fusion.own_ref), channel_id=1, source_target_pairs={{0,1},{1,0},{2,3},{3,2},{4,5},{5,4},{6,7},{7,6},{8,9},{9,8},{10,11... | collective-permute-start | bytes 1572872 | tf_op jit(solution)/shard_map/ppermute | solution.py:594
  48.4 2.3 %collective-permute-start.10 = (bf16[256,1024]{1,0:T(8,128)(2,1)S(1)}, bf16[256,1024]{1,0:T(8,128)(2,1)S(1)}, u32[]{:S(2)}, u32[]{:S(2)}) collective-permute-start(bf16[256,1024]{1,0:T(8,128)(2,1)S(1)} %add_convert_fusion.1.own_ref), channel_id=1, source_target_pairs={{0,1},{1,0},{2,3},{3,2},{4,5},{5,4},{6,7},{7,6},{8,9},{9,8},{10,11... | collective-permute-start | bytes 1572872 | tf_op jit(solution)/shard_map/ppermute | solution.py:594

commit v7 on v6

--- a/solution.py
+++ b/solution.py
@@ -201,7 +201,7 @@
     group, which_ref, x_ref, taps_ref, filt_ref, halo_ref, w_ref,
     *refs,
 ):
-    sends, (gate_ref, mixed_ref, feat_ref, gext_ref, ext_ref, table_ref) = refs[:PIECES], refs[PIECES:]
+    sends, (gate_ref, mixed_ref, gext_ref, ext_ref, table_ref) = refs[:PIECES], refs[PIECES:]
     _, rows, chans = x_ref.shape
     blocks = rows // SUB
     count = LANES // group
@@ -213,8 +213,6 @@
             ext[part, 8:, :] = x_ref[part, :, lanes].astype(F32)
         keyed = feature(ext, taps_ref, lanes, 1, 0, rows)
         valued = feature(ext, taps_ref, lanes, 2, 0, rows)
-        feat_ref[1, :, lanes] = keyed
-        feat_ref[2, :, lanes] = valued
         gext_ref[0:LANES, lanes] = halo_ref[0:LANES, lanes]
         gext_ref[LANES:, lanes] = (keyed * valued).astype(BF16)
         filt = filt_ref[j * count : (j + 1) * count, :]
@@ -226,7 +224,6 @@
         mixed = pick_groups(wide, group, blocks)
         mixed_ref[:, lanes] = mixed
         query = feature(ext, taps_ref, lanes, 0, 0, rows)
-        feat_ref[0, :, lanes] = query
         gate_ref[:, lanes] = (query * mixed).astype(BF16)
 
     each_tile(chans, tile, ext_ref, table_ref)
@@ -256,7 +253,7 @@
 
 
 def lags_kernel(
-    group, filt_ref, x_ref, halo_ref, gg_ref, mixed_ref, feat_ref, gext_ref,
+    group, filt_ref, x_ref, taps_ref, halo_ref, gg_ref, mixed_ref, gext_ref,
     gm_ref, gq_ref, lags_ref, tables_ref, left_ref, upside_ref, ext_ref,
 ):
     rows, chans = gg_ref.shape
@@ -266,12 +263,13 @@
     def tile(j, lanes, left, upside, ext):
         filt = filt_ref[j * count : (j + 1) * count, :]
         fill_table(tables_ref.at[j], filt.astype(F32), False)
-        grad_mixed = (gg_ref[:, lanes] * feat_ref[0, :, lanes]).astype(BF16)
+        ext[0, 6:8, :] = halo_ref[LANES : LANES + 2, lanes].astype(F32)
+        ext[0, 8:, :] = x_ref[0, :, lanes].astype(F32)
+        query = feature(ext, taps_ref, lanes, 0, 0, rows)
+        grad_mixed = (gg_ref[:, lanes] * query).astype(BF16)
         gm_ref[:, lanes] = grad_mixed
         grad_query = (gg_ref[:, lanes] * mixed_ref[:, lanes]).astype(BF16)
         gq_ref[:, lanes] = grad_query
-        ext[0, 6:8, :] = halo_ref[LANES : LANES + 2, lanes].astype(F32)
-        ext[0, 8:, :] = x_ref[0, :, lanes].astype(F32)
         sums = short_sums(grad_query.astype(F32), ext, 0)
         lane = group_of_lane(SUB, group)
         for g in range(count):
@@ -338,7 +336,7 @@
 
 
 def backward_kernel(
-    group, x_ref, taps_ref, halo_ref, feat_ref, back_ref, gm_ref, lags_ref, tables_ref,
+    group, x_ref, taps_ref, halo_ref, back_ref, gm_ref, lags_ref, tables_ref,
     gkv_ref, sums_ref, ext_ref, mext_ref, near_ref,
 ):
     _, rows, chans = x_ref.shape
@@ -360,7 +358,7 @@
         grad_gated = pick_groups(wide, group, blocks)
         sums = [None] * 3
         for part in range(1, 3):
-            grad = (grad_gated * feat_ref[3 - part, :, lanes]).astype(BF16)
+            grad = (grad_gated * feature(ext, taps_ref, lanes, 3 - part, 0, rows)).astype(BF16)
             gkv_ref[part - 1, :, lanes] = grad
             sums[part] = short_sums(grad.astype(F32), ext, part)
         early = lags_ref[:, lanes]
@@ -506,14 +504,13 @@
     back = shifted(sent_back, "ctx", -1)
     core = lax.rem(lax.axis_index("tp"), 2)
     piece = shape((rows, width // 2 // PIECES), BF16)
-    *other, gate_out, mixed, feat, gated = call(
+    *other, gate_out, mixed, gated = call(
         functools.partial(forward_kernel, group),
         "forward",
         (piece,) * PIECES
         + (
             shape((rows, chans), BF16),
             shape((rows, chans), F32),
-            shape((3, rows, chans), F32),
             shape((LANES + rows, chans), BF16),
         ),
         [pltpu.VMEM((tiles, 3, 8 + rows, LANES), F32), table],
@@ -547,7 +544,7 @@
             ext,
         ],
         operands=7,
-    )(long_filter, signal, halo, grad_gate, mixed, feat, gated)
+    )(long_filter, signal, short_filter, halo, grad_gate, mixed, gated)
     n_ctx = lax.axis_size("ctx")
     by_pairs = n_ctx & (n_ctx - 1) == 0
     grad_rest, sums = call(
@@ -555,8 +552,8 @@
         "backward",
         (shape((2, rows, chans), BF16), shape((32, chans), BF16 if by_pairs else F32)),
         [ext, pltpu.VMEM((tiles, rows + LANES, LANES), BF16), near],
-        operands=8,
-    )(signal, short_filter, halo, feat, back, grad_mixed, lags, tables)
+        operands=7,
+    )(signal, short_filter, halo, back, grad_mixed, lags, tables)
     grad_in = call(
         functools.partial(inputs_kernel, group),
         "inputs",

time: 52.1 us -> 52.1 us (level)
    pallas_call x1, Pallas kernels: 1.76 us -> 2.37 us  [local(): call(functools.partial(backward_kernel, group), 'backward', (shape((2, ro...]
    ppermute x2, waiting for transfers between devices: 5.18 us -> 4.58 us  [local(): got = [lax.ppermute(value, 'tp', pairwise('tp', step)) for value in mine]]
  transfers between devices with their start and end apart: 12 -> 12, of which waited for: 5 -> 5; matrix products, arithmetic and copies ran while one was open for 1% -> 1% of each run, Pallas kernels for 32% -> 33%
where the time goes in v7:
time: 52.1 us; the launch traced here: 51.8 us
  Pallas kernels  23.8 us (46%)
  starting transfers between devices  13.8 us (26%)
  waiting for transfers between devices  12.4 us (24%)
  between operations  0.93 us (2%)
  other arithmetic  0.8 us (2%)
    pallas_call x1, Pallas kernels, local(): call(grad_gate_kernel, 'grad_gate', (shape((rows, chans), F32), shape((LA...  5.55 us
    ppermute x2, starting transfers between devices, shifted(): lax.ppermute(value, axis, [(source, source + steps) for source in range(i...  5.4 us
    ppermute x2, waiting for transfers between devices, local(): got = [lax.ppermute(value, 'tp', pairwise('tp', step)) for value in mine]  4.58 us
    pallas_call x1, Pallas kernels, local(): call(functools.partial(forward_kernel, group), 'forward', (piece,) * PIEC...  4.3 us
    ppermute x4, waiting for transfers between devices, local(): lax.ppermute(terms[0], 'ctx', pairwise('ctx', i * hop))  4.11 us
    ppermute x4, starting transfers between devices, local(): lax.ppermute(terms[0], 'ctx', pairwise('ctx', i * hop))  3.4 us
    pallas_call x1, Pallas kernels, local(): call(functools.partial(inputs_kernel, group), 'inputs', shape((3, rows, c...  3.27 us
    ppermute x2, waiting for transfers between devices, shifted(): lax.ppermute(value, axis, [(source, source + steps) for source in range(i...  3.14 us
  transfers between devices with their start and end apart: 12, of which 5 were waited for; matrix products, arithmetic and copies ran while one was open for 1% of the time, Pallas kernels for 33%

profile of v7, /device:TPU:25, one launch (start us, length us, event | category | flops | bytes accessed | tf_op | source)
XLA Modules:
  0.0 51.8 jit_solution(12153882664600807673)
XLA Ops:
  0.6 1.5 %tail.1 = (bf16[136,1024]{1,0:T(8,128)(2,1)S(1)}, bf16[3,256,1024]{2,1,0:T(8,128)(2,1)S(1)}, f32[3,3,1024]{2,1,0:T(4,128)S(1)}, bf16[64,128]{1,0:T(8,128)(2,1)S(1)}) custom-call(bf16[3,256,1024]{2,1,0:T(8,128)(2,1)} %bitcast.4, f32[3,3,1024]{2,1,0:T(4,128)} %taps_hbm.1, bf16[64,128]{1,0:T(8,128)(2,1)} %filt_hbm.1), custom_call_target="tpu_custom_call" | custom-call | bytes 1024 | tf_op jit(solution)/shard_map/tail/pallas_call | solution.py:474
  2.2 3.1 %collective-permute-start = (bf16[136,1024]{1,0:T(8,128)(2,1)S(1)}, bf16[136,1024]{1,0:T(8,128)(2,1)S(1)}, u32[]{:S(2)}, u32[]{:S(2)}) collective-permute-start(bf16[136,1024]{1,0:T(8,128)(2,1)S(1)} %get-tuple-element.38), channel_id=1, source_target_pairs={{0,4},{4,8},{8,12},{12,16},{16,20},{20,24},{24,28},{1,5},{5,9},{9,... | collective-permute-start | bytes 835592 | tf_op jit(solution)/shard_map/ppermute | solution.py:28
  5.3 5.5 %grad_gate.1 = (f32[256,1024]{1,0:T(8,128)S(1)}, bf16[144,1024]{1,0:T(8,128)(2,1)S(1)}, bf16[1024,4096]{1,0:T(8,128)(2,1)S(1)}) custom-call(bf16[256,4096]{1,0:T(8,128)(2,1)} %c_hbm.1, bf16[1024,4096]{1,0:T(8,128)(2,1)} %w_hbm.1, bf16[3,256,1024]{2,1,0:T(8,128)(2,1)S(1)} %get-tuple-element.35.x_ref, f32[3,3,1024]{2,1,0:T(4,128)S(1)} %get-tuple-element.36.taps_ref), custom_call_target="tpu_custom_call" | custom-call | bytes 1024 | tf_op jit(solution)/shard_map/grad_gate/pallas_call | solution.py:487
  10.8 1.6 %collective-permute-done.halo_ref = bf16[136,1024]{1,0:T(8,128)(2,1)S(1)} collective-permute-done((bf16[136,1024]{1,0:T(8,128)(2,1)S(1)}, bf16[136,1024]{1,0:T(8,128)(2,1)S(1)}, u32[]{:S(2)}, u32[]{:S(2)}) %collective-permute-start) | collective-permute-done | bytes 278560 | tf_op jit(solution)/shard_map/ppermute | solution.py:28
  12.5 4.3 %forward.1 = (bf16[256,1024]{1,0:T(8,128)(2,1)S(1)}, bf16[256,1024]{1,0:T(8,128)(2,1)S(1)}, bf16[256,1024]{1,0:T(8,128)(2,1)S(1)}, f32[256,1024]{1,0:T(8,128)S(1)}, bf16[384,1024]{1,0:T(8,128)(2,1)S(1)}) custom-call(s32[1]{0:T(128)} %bitcast.1.which_ref, bf16[3,256,1024]{2,1,0:T(8,128)(2,1)S(1)} %get-tuple-element.35.x_ref, ...), custom_call_target="tpu_custom_call" | custom-call | bytes 1024 | tf_op jit(solution)/shard_map/forward/pallas_call | solution.py:507
  16.8 1.6 %collective-permute-start.1 = (bf16[256,1024]{1,0:T(8,128)(2,1)S(1)}, bf16[256,1024]{1,0:T(8,128)(2,1)S(1)}, u32[]{:S(2)}, u32[]{:S(2)}) collective-permute-start(bf16[256,1024]{1,0:T(8,128)(2,1)S(1)} %get-tuple-element.42), channel_id=1, source_target_pairs={{0,1},{1,0},{2,3},{3,2},{4,5},{5,4},{6,7},{7,6},{8,9},{9,8},{10,11... | collective-permute-start | bytes 1572872 | tf_op jit(solution)/shard_map/ppermute | solution.py:520
  18.4 0.1 collective-permute-start.3
  18.5 2.3 %collective-permute-start.5 = (bf16[144,1024]{1,0:T(8,128)(2,1)S(1)}, bf16[144,1024]{1,0:T(8,128)(2,1)S(1)}, u32[]{:S(2)}, u32[]{:S(2)}) collective-permute-start(bf16[144,1024]{1,0:T(8,128)(2,1)S(1)} %get-tuple-element.45), channel_id=1, source_target_pairs={{4,0},{8,4},{12,8},{16,12},{20,16},{24,20},{28,24},{5,1},{9,5},{13... | collective-permute-start | bytes 884744 | tf_op jit(solution)/shard_map/ppermute | solution.py:28
  20.8 1.3 %keep.1 = (bf16[256,1024]{1,0:T(8,128)(2,1)S(1)}, bf16[256,1024]{1,0:T(8,128)(2,1)S(1)}) custom-call(s32[1]{0:T(128)} %bitcast.which_ref, bf16[256,1024]{1,0:T(8,128)(2,1)S(1)} %get-tuple-element.40.gate_ref, bf16[1024,4096]{1,0:T(8,128)(2,1)S(1)} %get-tuple-element.39.w_ref), custom_call_target="tpu_custom_call" | custom-call | bytes 1024 | tf_op jit(solution)/shard_map/keep/pallas_call | solution.py:521
  22.0 0.0 collective-permute-done.1
  22.0 0.2 add_convert_fusion.3
  22.2 1.3 %collective-permute-start.2 = (bf16[256,1024]{1,0:T(8,128)(2,1)S(1)}, bf16[256,1024]{1,0:T(8,128)(2,1)S(1)}, u32[]{:S(2)}, u32[]{:S(2)}) collective-permute-start(bf16[256,1024]{1,0:T(8,128)(2,1)S(1)} %add_convert_fusion.3), channel_id=1, source_target_pairs={{0,2},{1,3},{2,0},{3,1},{4,6},{5,7},{6,4},{7,5},{8,10},{9,11},{10,... | collective-permute-start | bytes 1572872 | tf_op jit(solution)/shard_map/ppermute | solution.py:528
  23.5 0.0 collective-permute-done.3
  23.6 0.2 add_convert_fusion.2
  23.7 0.3 collective-permute-start.4
  24.0 2.9 %lags.1 = (bf16[256,1024]{1,0:T(8,128)(2,1)S(1)}, bf16[256,1024]{1,0:T(8,128)(2,1)S(1)}, f32[16,1024]{1,0:T(8,128)S(1)}, bf16[8,256,160]{2,1,0:T(8,128)(2,1)S(1)}) custom-call(bf16[64,128]{1,0:T(8,128)(2,1)S(1)} %get-tuple-element.37.filt_ref, bf16[3,256,1024]{2,1,0:T(8,128)(2,1)S(1)} %get-tuple-element.35.x_ref, ...), custom_call_target="tpu_custom_call" | custom-call | bytes 1024 | tf_op jit(solution)/shard_map/lags/pallas_call | solution.py:532
  27.0 1.5 %collective-permute-done.5.back_ref = bf16[144,1024]{1,0:T(8,128)(2,1)S(1)} collective-permute-done((bf16[144,1024]{1,0:T(8,128)(2,1)S(1)}, bf16[144,1024]{1,0:T(8,128)(2,1)S(1)}, u32[]{:S(2)}, u32[]{:S(2)}) %collective-permute-start.5) | collective-permute-done | bytes 294944 | tf_op jit(solution)/shard_map/ppermute | solution.py:28
  28.5 2.4 %backward.1 = (bf16[2,256,1024]{2,1,0:T(8,128)(2,1)S(1)}, bf16[32,1024]{1,0:T(8,128)(2,1)S(1)}) custom-call(bf16[3,256,1024]{2,1,0:T(8,128)(2,1)S(1)} %get-tuple-element.35.x_ref, f32[3,3,1024]{2,1,0:T(4,128)S(1)} %get-tuple-element.36.taps_ref, bf16[136,1024]{1,0:T(8,128)(2,1)S(1)} %collective-permute-done.halo_ref, ...), custom_call_target="tpu_custom_call" | custom-call | bytes 1024 | tf_op jit(solution)/shard_map/backward/pallas_call | solution.py:550
  30.9 1.2 %collective-permute-start.8 = (bf16[32,1024]{1,0:T(8,128)(2,1)S(1)}, bf16[32,1024]{1,0:T(8,128)(2,1)S(1)}, u32[]{:S(2)}, u32[]{:S(2)}) collective-permute-start(bf16[32,1024]{1,0:T(8,128)(2,1)S(1)} %get-tuple-element.55), channel_id=1, source_target_pairs={{0,12},{4,8},{8,4},{12,0},{16,28},{20,24},{24,20},{28,16},{1,13},{... | collective-permute-start | bytes 196616 | tf_op jit(solution)/shard_map/ppermute | solution.py:573
  32.0 0.0 collective-permute-start.7
  32.0 1.6 %collective-permute-start.6 = (bf16[32,1024]{1,0:T(8,128)(2,1)S(1)}, bf16[32,1024]{1,0:T(8,128)(2,1)S(1)}, u32[]{:S(2)}, u32[]{:S(2)}) collective-permute-start(bf16[32,1024]{1,0:T(8,128)(2,1)S(1)} %get-tuple-element.55), channel_id=1, source_target_pairs={{0,4},{4,0},{8,12},{12,8},{16,20},{20,16},{24,28},{28,24},{1,5},{5... | collective-permute-start | bytes 196616 | tf_op jit(solution)/shard_map/ppermute | solution.py:573
  33.6 3.3 %inputs.1 = bf16[3,256,1024]{2,1,0:T(8,128)(2,1)} custom-call(bf16[3,256,1024]{2,1,0:T(8,128)(2,1)S(1)} %get-tuple-element.35.x_ref, f32[3,3,1024]{2,1,0:T(4,128)S(1)} %get-tuple-element.36.taps_ref, bf16[64,128]{1,0:T(8,128)(2,1)S(1)} %get-tuple-element.37.filt_ref, bf16[384,1024]{1,0:T(8,128)(2,1)S(1)} %get-tuple-element.48.gext_ref, ...), custom_call_target="tpu_custom_call" | custom-call | bytes 1024 | tf_op jit(solution)/shard_map/inputs/pallas_call | solution.py:557
  36.9 0.0 collective-permute-done.8
  36.9 0.0 collective-permute-done.7
  36.9 0.0 collective-permute-done.6
  36.9 0.7 %collective-permute-start.9 = (bf16[32,1024]{1,0:T(8,128)(2,1)S(1)}, bf16[32,1024]{1,0:T(8,128)(2,1)S(1)}, u32[]{:S(2)}, u32[]{:S(2)}) collective-permute-start(bf16[32,1024]{1,0:T(8,128)(2,1)S(1)} %add_convert_fusion.4.refs_0_), channel_id=1, source_target_pairs={{0,16},{4,20},{8,24},{12,28},{16,0},{20,4},{24,8},{28,12},{1,17},{... | collective-permute-start | bytes 196616 | tf_op jit(solution)/shard_map/ppermute | solution.py:573
  37.6 4.1 %collective-permute-done.9.refs_1_ = bf16[32,1024]{1,0:T(8,128)(2,1)S(1)} collective-permute-done((bf16[32,1024]{1,0:T(8,128)(2,1)S(1)}, bf16[32,1024]{1,0:T(8,128)(2,1)S(1)}, u32[]{:S(2)}, u32[]{:S(2)}) %collective-permute-start.9) | collective-permute-done | bytes 65568 | tf_op jit(solution)/shard_map/ppermute | solution.py:573
  41.7 0.0 collective-permute-done.2
  41.7 4.6 %collective-permute-done.4 = bf16[256,1024]{1,0:T(8,128)(2,1)S(1)} collective-permute-done((bf16[256,1024]{1,0:T(8,128)(2,1)S(1)}, bf16[256,1024]{1,0:T(8,128)(2,1)S(1)}, u32[]{:S(2)}, u32[]{:S(2)}) %collective-permute-start.4) | collective-permute-done | bytes 524320 | tf_op jit(solution)/shard_map/ppermute | solution.py:528
  46.3 0.2 add_convert_fusion.own_ref
  46.5 1.7 %collective-permute-start.11 = (bf16[256,1024]{1,0:T(8,128)(2,1)S(1)}, bf16[256,1024]{1,0:T(8,128)(2,1)S(1)}, u32[]{:S(2)}, u32[]{:S(2)}) collective-permute-start(bf16[256,1024]{1,0:T(8,128)(2,1)S(1)} %add_convert_fusion.own_ref), channel_id=1, source_target_pairs={{0,1},{1,0},{2,3},{3,2},{4,5},{5,4},{6,7},{7,6},{8,9},{9,8},{10,11... | collective-permute-start | bytes 1572872 | tf_op jit(solution)/shard_map/ppermute | solution.py:591
  48.1 0.2 add_convert_fusion.1.own_ref
  48.3 0.1 collective-permute-start.10
  48.4 0.6 %unpack.1 = (f32[3,3,1024]{2,1,0:T(4,128)}, f32[64,128]{1,0:T(8,128)}) custom-call(bf16[32,1024]{1,0:T(8,128)(2,1)S(1)} %add_convert_fusion.4.refs_0_, bf16[32,1024]{1,0:T(8,128)(2,1)S(1)} %collective-permute-done.9.refs_1_), custom_call_target="tpu_custom_call" | custom-call | bytes 1024 | tf_op jit(solution)/shard_map/unpack/pallas_call | solution.py:597
  49.1 0.6 %collective-permute-done.11.sibling_ref = bf16[256,1024]{1,0:T(8,128)(2,1)S(1)} collective-permute-done((bf16[256,1024]{1,0:T(8,128)(2,1)S(1)}, bf16[256,1024]{1,0:T(8,128)(2,1)S(1)}, u32[]{:S(2)}, u32[]{:S(2)}) %collective-permute-start.11) | collective-permute-done | bytes 524320 | tf_op jit(solution)/shard_map/ppermute | solution.py:591
  49.7 1.0 %place.2.refs_0_ = bf16[256,4096]{1,0:T(8,128)(2,1)} custom-call(s32[1]{0:T(128)} %bitcast.which_ref, bf16[256,1024]{1,0:T(8,128)(2,1)S(1)} %add_convert_fusion.own_ref, bf16[256,1024]{1,0:T(8,128)(2,1)S(1)} %collective-permute-done.11.sibling_ref), custom_call_target="tpu_custom_call" | custom-call | tf_op jit(solution)/shard_map/place/pallas_call | solution.py:446
  50.7 0.0 collective-permute-done.10.sibling_ref
  50.7 1.0 %place.3 = bf16[256,4096]{1,0:T(8,128)(2,1)} custom-call(s32[1]{0:T(128)} %bitcast.which_ref, bf16[256,1024]{1,0:T(8,128)(2,1)S(1)} %add_convert_fusion.1.own_ref, bf16[256,1024]{1,0:T(8,128)(2,1)S(1)} %collective-permute-done.10.sibling_ref, bf16[256,4096]{1,0:T(8,128)(2,1)} %place.2.refs_0_), custom_call_target="tpu_custom_call", output_to_operand_aliasing={{}: (3, {})} | custom-call | tf_op jit(solution)/shard_map/place/pallas_call | solution.py:446
  (1 shorter events, 0.0 us)
Async XLA Ops:
  2.2 10.3 %collective-permute-start = (bf16[136,1024]{1,0:T(8,128)(2,1)S(1)}, bf16[136,1024]{1,0:T(8,128)(2,1)S(1)}, u32[]{:S(2)}, u32[]{:S(2)}) collective-permute-start(bf16[136,1024]{1,0:T(8,128)(2,1)S(1)} %get-tuple-element.38), channel_id=1, source_target_pairs={{0,4},{4,8},{8,12},{12,16},{16,20},{20,24},{24,28},{1,5},{5,9},{9,... | collective-permute-start | bytes 835592 | tf_op jit(solution)/shard_map/ppermute | solution.py:28
  16.8 5.2 %collective-permute-start.1 = (bf16[256,1024]{1,0:T(8,128)(2,1)S(1)}, bf16[256,1024]{1,0:T(8,128)(2,1)S(1)}, u32[]{:S(2)}, u32[]{:S(2)}) collective-permute-start(bf16[256,1024]{1,0:T(8,128)(2,1)S(1)} %get-tuple-element.42), channel_id=1, source_target_pairs={{0,1},{1,0},{2,3},{3,2},{4,5},{5,4},{6,7},{7,6},{8,9},{9,8},{10,11... | collective-permute-start | bytes 1572872 | tf_op jit(solution)/shard_map/ppermute | solution.py:520
  18.4 5.2 %collective-permute-start.3 = (bf16[256,1024]{1,0:T(8,128)(2,1)S(1)}, bf16[256,1024]{1,0:T(8,128)(2,1)S(1)}, u32[]{:S(2)}, u32[]{:S(2)}) collective-permute-start(bf16[256,1024]{1,0:T(8,128)(2,1)S(1)} %get-tuple-element.44), channel_id=1, source_target_pairs={{0,1},{1,0},{2,3},{3,2},{4,5},{5,4},{6,7},{7,6},{8,9},{9,8},{10,11... | collective-permute-start | bytes 1572872 | tf_op jit(solution)/shard_map/ppermute | solution.py:520
  18.5 10.0 %collective-permute-start.5 = (bf16[144,1024]{1,0:T(8,128)(2,1)S(1)}, bf16[144,1024]{1,0:T(8,128)(2,1)S(1)}, u32[]{:S(2)}, u32[]{:S(2)}) collective-permute-start(bf16[144,1024]{1,0:T(8,128)(2,1)S(1)} %get-tuple-element.45), channel_id=1, source_target_pairs={{4,0},{8,4},{12,8},{16,12},{20,16},{24,20},{28,24},{5,1},{9,5},{13... | collective-permute-start | bytes 884744 | tf_op jit(solution)/shard_map/ppermute | solution.py:28
  22.2 19.5 %collective-permute-start.2 = (bf16[256,1024]{1,0:T(8,128)(2,1)S(1)}, bf16[256,1024]{1,0:T(8,128)(2,1)S(1)}, u32[]{:S(2)}, u32[]{:S(2)}) collective-permute-start(bf16[256,1024]{1,0:T(8,128)(2,1)S(1)} %add_convert_fusion.3), channel_id=1, source_target_pairs={{0,2},{1,3},{2,0},{3,1},{4,6},{5,7},{6,4},{7,5},{8,10},{9,11},{10,... | collective-permute-start | bytes 1572872 | tf_op jit(solution)/shard_map/ppermute | solution.py:528
  23.7 22.5 %collective-permute-start.4 = (bf16[256,1024]{1,0:T(8,128)(2,1)S(1)}, bf16[256,1024]{1,0:T(8,128)(2,1)S(1)}, u32[]{:S(2)}, u32[]{:S(2)}) collective-permute-start(bf16[256,1024]{1,0:T(8,128)(2,1)S(1)} %add_convert_fusion.2), channel_id=1, source_target_pairs={{0,2},{1,3},{2,0},{3,1},{4,6},{5,7},{6,4},{7,5},{8,10},{9,11},{10,... | collective-permute-start | bytes 1572872 | tf_op jit(solution)/shard_map/ppermute | solution.py:528
  30.9 6.0 %collective-permute-start.8 = (bf16[32,1024]{1,0:T(8,128)(2,1)S(1)}, bf16[32,1024]{1,0:T(8,128)(2,1)S(1)}, u32[]{:S(2)}, u32[]{:S(2)}) collective-permute-start(bf16[32,1024]{1,0:T(8,128)(2,1)S(1)} %get-tuple-element.55), channel_id=1, source_target_pairs={{0,12},{4,8},{8,4},{12,0},{16,28},{20,24},{24,20},{28,16},{1,13},{... | collective-permute-start | bytes 196616 | tf_op jit(solution)/shard_map/ppermute | solution.py:573
  32.0 4.8 %collective-permute-start.7 = (bf16[32,1024]{1,0:T(8,128)(2,1)S(1)}, bf16[32,1024]{1,0:T(8,128)(2,1)S(1)}, u32[]{:S(2)}, u32[]{:S(2)}) collective-permute-start(bf16[32,1024]{1,0:T(8,128)(2,1)S(1)} %get-tuple-element.55), channel_id=1, source_target_pairs={{0,8},{4,12},{8,0},{12,4},{16,24},{20,28},{24,16},{28,20},{1,9},{5... | collective-permute-start | bytes 196616 | tf_op jit(solution)/shard_map/ppermute | solution.py:573
  32.0 4.8 %collective-permute-start.6 = (bf16[32,1024]{1,0:T(8,128)(2,1)S(1)}, bf16[32,1024]{1,0:T(8,128)(2,1)S(1)}, u32[]{:S(2)}, u32[]{:S(2)}) collective-permute-start(bf16[32,1024]{1,0:T(8,128)(2,1)S(1)} %get-tuple-element.55), channel_id=1, source_target_pairs={{0,4},{4,0},{8,12},{12,8},{16,20},{20,16},{24,28},{28,24},{1,5},{5... | collective-permute-start | bytes 196616 | tf_op jit(solution)/shard_map/ppermute | solution.py:573
  36.9 4.8 %collective-permute-start.9 = (bf16[32,1024]{1,0:T(8,128)(2,1)S(1)}, bf16[32,1024]{1,0:T(8,128)(2,1)S(1)}, u32[]{:S(2)}, u32[]{:S(2)}) collective-permute-start(bf16[32,1024]{1,0:T(8,128)(2,1)S(1)} %add_convert_fusion.4.refs_0_), channel_id=1, source_target_pairs={{0,16},{4,20},{8,24},{12,28},{16,0},{20,4},{24,8},{28,12},{1,17},{... | collective-permute-start | bytes 196616 | tf_op jit(solution)/shard_map/ppermute | solution.py:573
  46.5 3.2 %collective-permute-start.11 = (bf16[256,1024]{1,0:T(8,128)(2,1)S(1)}, bf16[256,1024]{1,0:T(8,128)(2,1)S(1)}, u32[]{:S(2)}, u32[]{:S(2)}) collective-permute-start(bf16[256,1024]{1,0:T(8,128)(2,1)S(1)} %add_convert_fusion.own_ref), channel_id=1, source_target_pairs={{0,1},{1,0},{2,3},{3,2},{4,5},{5,4},{6,7},{7,6},{8,9},{9,8},{10,11... | collective-permute-start | bytes 1572872 | tf_op jit(solution)/shard_map/ppermute | solution.py:591
  48.3 2.3 %collective-permute-start.10 = (bf16[256,1024]{1,0:T(8,128)(2,1)S(1)}, bf16[256,1024]{1,0:T(8,128)(2,1)S(1)}, u32[]{:S(2)}, u32[]{:S(2)}) collective-permute-start(bf16[256,1024]{1,0:T(8,128)(2,1)S(1)} %add_convert_fusion.1.own_ref), channel_id=1, source_target_pairs={{0,1},{1,0},{2,3},{3,2},{4,5},{5,4},{6,7},{7,6},{8,9},{9,8},{10,11... | collective-permute-start | bytes 1572872 | tf_op jit(solution)/shard_map/ppermute | solution.py:591

commit v8 on v7

--- a/solution.py
+++ b/solution.py
@@ -230,18 +230,19 @@
     project(which_ref[0], gate_ref, w_ref, sends)
 
 
-def project(which, gate_ref, w_ref, out_refs):
+def project(which, gate_ref, w_ref, out_refs, theirs=None):
     half = w_ref.shape[1] // 2
     part = half // len(out_refs)
     for i, out_ref in enumerate(out_refs):
         cols = pl.ds(pl.multiple_of(which * half + i * part, part), part)
-        out_ref[...] = jnp.dot(
-            gate_ref[...], w_ref[:, cols], preferred_element_type=F32
-        ).astype(BF16)
-
-
-def keep_kernel(which_ref, gate_ref, w_ref, *keep_refs):
-    project(which_ref[0], gate_ref, w_ref, keep_refs)
+        total = jnp.dot(gate_ref[...], w_ref[:, cols], preferred_element_type=F32)
+        if theirs is not None:
+            total = total.astype(BF16).astype(F32) + theirs[i][...].astype(F32)
+        out_ref[...] = total.astype(BF16)
+
+
+def keep_kernel(which_ref, gate_ref, w_ref, *refs):
+    project(which_ref[0], gate_ref, w_ref, refs[PIECES:], refs[:PIECES])
 
 
 def short_sums(grad, ext_ref, part):
@@ -518,12 +519,9 @@
         operands=5,
     )(jnp.reshape(1 - core, (1,)), signal, short_filter, long_filter, halo, out_weight)
     theirs = [lax.ppermute(value, "tp", pairwise("tp", 1)) for value in other]
-    kept = call(keep_kernel, "keep", (piece,) * PIECES, scalars=1, operands=2)(
-        jnp.reshape(core, (1,)), gate_out, out_weight
-    )
-    mine = [
-        (a.astype(F32) + b.astype(F32)).astype(BF16) for a, b in zip(kept, theirs, strict=True)
-    ]
+    mine = call(
+        keep_kernel, "keep", (piece,) * PIECES, scalars=1, operands=2 + PIECES
+    )(jnp.reshape(core, (1,)), gate_out, out_weight, *theirs)
     step = 2
     got = [lax.ppermute(value, "tp", pairwise("tp", step)) for value in mine]
 

time: 52.1 us -> 52 us (level)
  transfers between devices with their start and end apart: 12 -> 12, of which waited for: 5 -> 5; matrix products, arithmetic and copies ran while one was open for 1% -> 0% of each run, Pallas kernels for 33% -> 33%
where the time goes in v8:
time: 52 us; the launch traced here: 51.7 us
  Pallas kernels  23.9 us (46%)
  starting transfers between devices  13.8 us (27%)
  waiting for transfers between devices  12.7 us (24%)
  between operations  0.92 us (2%)
    pallas_call x1, Pallas kernels, local(): call(grad_gate_kernel, 'grad_gate', (shape((rows, chans), F32), shape((LA...  5.55 us
    ppermute x2, starting transfers between devices, shifted(): lax.ppermute(value, axis, [(source, source + steps) for source in range(i...  5.42 us
    ppermute x2, waiting for transfers between devices, local(): got = [lax.ppermute(value, 'tp', pairwise('tp', step)) for value in mine]  4.48 us
    pallas_call x1, Pallas kernels, local(): call(functools.partial(forward_kernel, group), 'forward', (piece,) * PIEC...  4.3 us
    ppermute x4, waiting for transfers between devices, local(): lax.ppermute(terms[0], 'ctx', pairwise('ctx', i * hop))  4.11 us
    ppermute x2, waiting for transfers between devices, shifted(): lax.ppermute(value, axis, [(source, source + steps) for source in range(i...  3.51 us
    ppermute x4, starting transfers between devices, local(): lax.ppermute(terms[0], 'ctx', pairwise('ctx', i * hop))  3.4 us
    pallas_call x1, Pallas kernels, local(): call(functools.partial(inputs_kernel, group), 'inputs', shape((3, rows, c...  3.27 us
  transfers between devices with their start and end apart: 12, of which 5 were waited for; matrix products, arithmetic and copies ran while one was open for 0% of the time, Pallas kernels for 33%

profile of v8, /device:TPU:25, one launch (start us, length us, event | category | flops | bytes accessed | tf_op | source)
XLA Modules:
  0.0 51.7 jit_solution(9729636298357064638)
XLA Ops:
  0.6 1.5 %tail.1 = (bf16[136,1024]{1,0:T(8,128)(2,1)S(1)}, bf16[3,256,1024]{2,1,0:T(8,128)(2,1)S(1)}, f32[3,3,1024]{2,1,0:T(4,128)S(1)}, bf16[64,128]{1,0:T(8,128)(2,1)S(1)}) custom-call(bf16[3,256,1024]{2,1,0:T(8,128)(2,1)} %bitcast.4, f32[3,3,1024]{2,1,0:T(4,128)} %taps_hbm.1, bf16[64,128]{1,0:T(8,128)(2,1)} %filt_hbm.1), custom_call_target="tpu_custom_call" | custom-call | bytes 1024 | tf_op jit(solution)/shard_map/tail/pallas_call | solution.py:475
  2.2 3.1 %collective-permute-start = (bf16[136,1024]{1,0:T(8,128)(2,1)S(1)}, bf16[136,1024]{1,0:T(8,128)(2,1)S(1)}, u32[]{:S(2)}, u32[]{:S(2)}) collective-permute-start(bf16[136,1024]{1,0:T(8,128)(2,1)S(1)} %get-tuple-element.38), channel_id=1, source_target_pairs={{0,4},{4,8},{8,12},{12,16},{16,20},{20,24},{24,28},{1,5},{5,9},{9,... | collective-permute-start | bytes 835592 | tf_op jit(solution)/shard_map/ppermute | solution.py:28
  5.3 5.6 %grad_gate.1 = (f32[256,1024]{1,0:T(8,128)S(1)}, bf16[144,1024]{1,0:T(8,128)(2,1)S(1)}, bf16[1024,4096]{1,0:T(8,128)(2,1)S(1)}) custom-call(bf16[256,4096]{1,0:T(8,128)(2,1)} %c_hbm.1, bf16[1024,4096]{1,0:T(8,128)(2,1)} %w_hbm.1, bf16[3,256,1024]{2,1,0:T(8,128)(2,1)S(1)} %get-tuple-element.35.x_ref, f32[3,3,1024]{2,1,0:T(4,128)S(1)} %get-tuple-element.36.taps_ref), custom_call_target="tpu_custom_call" | custom-call | bytes 1024 | tf_op jit(solution)/shard_map/grad_gate/pallas_call | solution.py:488
  10.8 1.6 %collective-permute-done.halo_ref = bf16[136,1024]{1,0:T(8,128)(2,1)S(1)} collective-permute-done((bf16[136,1024]{1,0:T(8,128)(2,1)S(1)}, bf16[136,1024]{1,0:T(8,128)(2,1)S(1)}, u32[]{:S(2)}, u32[]{:S(2)}) %collective-permute-start) | collective-permute-done | bytes 278560 | tf_op jit(solution)/shard_map/ppermute | solution.py:28
  12.5 4.3 %forward.1 = (bf16[256,1024]{1,0:T(8,128)(2,1)S(1)}, bf16[256,1024]{1,0:T(8,128)(2,1)S(1)}, bf16[256,1024]{1,0:T(8,128)(2,1)S(1)}, f32[256,1024]{1,0:T(8,128)S(1)}, bf16[384,1024]{1,0:T(8,128)(2,1)S(1)}) custom-call(s32[1]{0:T(128)} %bitcast.1.which_ref, bf16[3,256,1024]{2,1,0:T(8,128)(2,1)S(1)} %get-tuple-element.35.x_ref, ...), custom_call_target="tpu_custom_call" | custom-call | bytes 1024 | tf_op jit(solution)/shard_map/forward/pallas_call | solution.py:508
  16.8 1.6 %collective-permute-start.1 = (bf16[256,1024]{1,0:T(8,128)(2,1)S(1)}, bf16[256,1024]{1,0:T(8,128)(2,1)S(1)}, u32[]{:S(2)}, u32[]{:S(2)}) collective-permute-start(bf16[256,1024]{1,0:T(8,128)(2,1)S(1)} %get-tuple-element.41), channel_id=1, source_target_pairs={{0,1},{1,0},{2,3},{3,2},{4,5},{5,4},{6,7},{7,6},{8,9},{9,8},{10,11... | collective-permute-start | bytes 1572872 | tf_op jit(solution)/shard_map/ppermute | solution.py:521
  18.4 0.1 collective-permute-start.2
  18.5 2.3 %collective-permute-start.5 = (bf16[144,1024]{1,0:T(8,128)(2,1)S(1)}, bf16[144,1024]{1,0:T(8,128)(2,1)S(1)}, u32[]{:S(2)}, u32[]{:S(2)}) collective-permute-start(bf16[144,1024]{1,0:T(8,128)(2,1)S(1)} %get-tuple-element.45), channel_id=1, source_target_pairs={{4,0},{8,4},{12,8},{16,12},{20,16},{24,20},{28,24},{5,1},{9,5},{13... | collective-permute-start | bytes 884744 | tf_op jit(solution)/shard_map/ppermute | solution.py:28
  20.8 0.0 collective-permute-done.1.refs_0_
  20.8 0.0 collective-permute-done.2.refs_1_
  20.8 1.3 %keep.1 = (bf16[256,1024]{1,0:T(8,128)(2,1)S(1)}, bf16[256,1024]{1,0:T(8,128)(2,1)S(1)}) custom-call(s32[1]{0:T(128)} %bitcast.which_ref, bf16[256,1024]{1,0:T(8,128)(2,1)S(1)} %get-tuple-element.40.gate_ref, bf16[1024,4096]{1,0:T(8,128)(2,1)S(1)} %get-tuple-element.39.w_ref, bf16[256,1024]{1,0:T(8,128)(2,1)S(1)} %collective-permute-done.1.refs_0_, ...), custom_call_target="tpu_custom_call" | custom-call | bytes 1024 | tf_op jit(solution)/shard_map/keep/pallas_call | solution.py:522
  22.1 1.3 %collective-permute-start.3 = (bf16[256,1024]{1,0:T(8,128)(2,1)S(1)}, bf16[256,1024]{1,0:T(8,128)(2,1)S(1)}, u32[]{:S(2)}, u32[]{:S(2)}) collective-permute-start(bf16[256,1024]{1,0:T(8,128)(2,1)S(1)} %get-tuple-element.43), channel_id=1, source_target_pairs={{0,2},{1,3},{2,0},{3,1},{4,6},{5,7},{6,4},{7,5},{8,10},{9,11},{10,... | collective-permute-start | bytes 1572872 | tf_op jit(solution)/shard_map/ppermute | solution.py:526
  23.4 0.3 collective-permute-start.4
  23.7 2.9 %lags.1 = (bf16[256,1024]{1,0:T(8,128)(2,1)S(1)}, bf16[256,1024]{1,0:T(8,128)(2,1)S(1)}, f32[16,1024]{1,0:T(8,128)S(1)}, bf16[8,256,160]{2,1,0:T(8,128)(2,1)S(1)}) custom-call(bf16[64,128]{1,0:T(8,128)(2,1)S(1)} %get-tuple-element.37.filt_ref, bf16[3,256,1024]{2,1,0:T(8,128)(2,1)S(1)} %get-tuple-element.35.x_ref, ...), custom_call_target="tpu_custom_call" | custom-call | bytes 1024 | tf_op jit(solution)/shard_map/lags/pallas_call | solution.py:530
  26.6 1.9 %collective-permute-done.5.back_ref = bf16[144,1024]{1,0:T(8,128)(2,1)S(1)} collective-permute-done((bf16[144,1024]{1,0:T(8,128)(2,1)S(1)}, bf16[144,1024]{1,0:T(8,128)(2,1)S(1)}, u32[]{:S(2)}, u32[]{:S(2)}) %collective-permute-start.5) | collective-permute-done | bytes 294944 | tf_op jit(solution)/shard_map/ppermute | solution.py:28
  28.5 2.4 %backward.1 = (bf16[2,256,1024]{2,1,0:T(8,128)(2,1)S(1)}, bf16[32,1024]{1,0:T(8,128)(2,1)S(1)}) custom-call(bf16[3,256,1024]{2,1,0:T(8,128)(2,1)S(1)} %get-tuple-element.35.x_ref, f32[3,3,1024]{2,1,0:T(4,128)S(1)} %get-tuple-element.36.taps_ref, bf16[136,1024]{1,0:T(8,128)(2,1)S(1)} %collective-permute-done.halo_ref, ...), custom_call_target="tpu_custom_call" | custom-call | bytes 1024 | tf_op jit(solution)/shard_map/backward/pallas_call | solution.py:548
  30.9 1.2 %collective-permute-start.8 = (bf16[32,1024]{1,0:T(8,128)(2,1)S(1)}, bf16[32,1024]{1,0:T(8,128)(2,1)S(1)}, u32[]{:S(2)}, u32[]{:S(2)}) collective-permute-start(bf16[32,1024]{1,0:T(8,128)(2,1)S(1)} %get-tuple-element.55), channel_id=1, source_target_pairs={{0,12},{4,8},{8,4},{12,0},{16,28},{20,24},{24,20},{28,16},{1,13},{... | collective-permute-start | bytes 196616 | tf_op jit(solution)/shard_map/ppermute | solution.py:571
  32.1 0.0 collective-permute-start.7
  32.1 1.5 %collective-permute-start.6 = (bf16[32,1024]{1,0:T(8,128)(2,1)S(1)}, bf16[32,1024]{1,0:T(8,128)(2,1)S(1)}, u32[]{:S(2)}, u32[]{:S(2)}) collective-permute-start(bf16[32,1024]{1,0:T(8,128)(2,1)S(1)} %get-tuple-element.55), channel_id=1, source_target_pairs={{0,4},{4,0},{8,12},{12,8},{16,20},{20,16},{24,28},{28,24},{1,5},{5... | collective-permute-start | bytes 196616 | tf_op jit(solution)/shard_map/ppermute | solution.py:571
  33.6 3.3 %inputs.1 = bf16[3,256,1024]{2,1,0:T(8,128)(2,1)} custom-call(bf16[3,256,1024]{2,1,0:T(8,128)(2,1)S(1)} %get-tuple-element.35.x_ref, f32[3,3,1024]{2,1,0:T(4,128)S(1)} %get-tuple-element.36.taps_ref, bf16[64,128]{1,0:T(8,128)(2,1)S(1)} %get-tuple-element.37.filt_ref, bf16[384,1024]{1,0:T(8,128)(2,1)S(1)} %get-tuple-element.48.gext_ref, ...), custom_call_target="tpu_custom_call" | custom-call | bytes 1024 | tf_op jit(solution)/shard_map/inputs/pallas_call | solution.py:555
  36.9 0.0 collective-permute-done.8
  36.9 0.0 collective-permute-done.7
  36.9 0.0 collective-permute-done.6
  36.9 0.7 %collective-permute-start.9 = (bf16[32,1024]{1,0:T(8,128)(2,1)S(1)}, bf16[32,1024]{1,0:T(8,128)(2,1)S(1)}, u32[]{:S(2)}, u32[]{:S(2)}) collective-permute-start(bf16[32,1024]{1,0:T(8,128)(2,1)S(1)} %add_convert_fusion.2.refs_0_), channel_id=1, source_target_pairs={{0,16},{4,20},{8,24},{12,28},{16,0},{20,4},{24,8},{28,12},{1,17},{... | collective-permute-start | bytes 196616 | tf_op jit(solution)/shard_map/ppermute | solution.py:571
  37.6 4.1 %collective-permute-done.9.refs_1_ = bf16[32,1024]{1,0:T(8,128)(2,1)S(1)} collective-permute-done((bf16[32,1024]{1,0:T(8,128)(2,1)S(1)}, bf16[32,1024]{1,0:T(8,128)(2,1)S(1)}, u32[]{:S(2)}, u32[]{:S(2)}) %collective-permute-start.9) | collective-permute-done | bytes 65568 | tf_op jit(solution)/shard_map/ppermute | solution.py:571
  41.7 0.0 collective-permute-done.3
  41.7 4.5 %collective-permute-done.4 = bf16[256,1024]{1,0:T(8,128)(2,1)S(1)} collective-permute-done((bf16[256,1024]{1,0:T(8,128)(2,1)S(1)}, bf16[256,1024]{1,0:T(8,128)(2,1)S(1)}, u32[]{:S(2)}, u32[]{:S(2)}) %collective-permute-start.4) | collective-permute-done | bytes 524320 | tf_op jit(solution)/shard_map/ppermute | solution.py:526
  46.2 0.2 add_convert_fusion.own_ref
  46.4 1.7 %collective-permute-start.11 = (bf16[256,1024]{1,0:T(8,128)(2,1)S(1)}, bf16[256,1024]{1,0:T(8,128)(2,1)S(1)}, u32[]{:S(2)}, u32[]{:S(2)}) collective-permute-start(bf16[256,1024]{1,0:T(8,128)(2,1)S(1)} %add_convert_fusion.own_ref), channel_id=1, source_target_pairs={{0,1},{1,0},{2,3},{3,2},{4,5},{5,4},{6,7},{7,6},{8,9},{9,8},{10,11... | collective-permute-start | bytes 1572872 | tf_op jit(solution)/shard_map/ppermute | solution.py:589
  48.0 0.2 add_convert_fusion.1.own_ref
  48.2 0.1 collective-permute-start.10
  48.3 0.6 %unpack.1 = (f32[3,3,1024]{2,1,0:T(4,128)}, f32[64,128]{1,0:T(8,128)}) custom-call(bf16[32,1024]{1,0:T(8,128)(2,1)S(1)} %add_convert_fusion.2.refs_0_, bf16[32,1024]{1,0:T(8,128)(2,1)S(1)} %collective-permute-done.9.refs_1_), custom_call_target="tpu_custom_call" | custom-call | bytes 1024 | tf_op jit(solution)/shard_map/unpack/pallas_call | solution.py:595
  49.0 0.6 %collective-permute-done.11.sibling_ref = bf16[256,1024]{1,0:T(8,128)(2,1)S(1)} collective-permute-done((bf16[256,1024]{1,0:T(8,128)(2,1)S(1)}, bf16[256,1024]{1,0:T(8,128)(2,1)S(1)}, u32[]{:S(2)}, u32[]{:S(2)}) %collective-permute-start.11) | collective-permute-done | bytes 524320 | tf_op jit(solution)/shard_map/ppermute | solution.py:589
  49.6 1.0 %place.2.refs_0_ = bf16[256,4096]{1,0:T(8,128)(2,1)} custom-call(s32[1]{0:T(128)} %bitcast.which_ref, bf16[256,1024]{1,0:T(8,128)(2,1)S(1)} %add_convert_fusion.own_ref, bf16[256,1024]{1,0:T(8,128)(2,1)S(1)} %collective-permute-done.11.sibling_ref), custom_call_target="tpu_custom_call" | custom-call | tf_op jit(solution)/shard_map/place/pallas_call | solution.py:447
  50.6 0.0 collective-permute-done.10.sibling_ref
  50.6 1.0 %place.3 = bf16[256,4096]{1,0:T(8,128)(2,1)} custom-call(s32[1]{0:T(128)} %bitcast.which_ref, bf16[256,1024]{1,0:T(8,128)(2,1)S(1)} %add_convert_fusion.1.own_ref, bf16[256,1024]{1,0:T(8,128)(2,1)S(1)} %collective-permute-done.10.sibling_ref, bf16[256,4096]{1,0:T(8,128)(2,1)} %place.2.refs_0_), custom_call_target="tpu_custom_call", output_to_operand_aliasing={{}: (3, {})} | custom-call | tf_op jit(solution)/shard_map/place/pallas_call | solution.py:447
  (1 shorter events, 0.0 us)
Async XLA Ops:
  2.2 10.3 %collective-permute-start = (bf16[136,1024]{1,0:T(8,128)(2,1)S(1)}, bf16[136,1024]{1,0:T(8,128)(2,1)S(1)}, u32[]{:S(2)}, u32[]{:S(2)}) collective-permute-start(bf16[136,1024]{1,0:T(8,128)(2,1)S(1)} %get-tuple-element.38), channel_id=1, source_target_pairs={{0,4},{4,8},{8,12},{12,16},{16,20},{20,24},{24,28},{1,5},{5,9},{9,... | collective-permute-start | bytes 835592 | tf_op jit(solution)/shard_map/ppermute | solution.py:28
  16.8 4.0 %collective-permute-start.1 = (bf16[256,1024]{1,0:T(8,128)(2,1)S(1)}, bf16[256,1024]{1,0:T(8,128)(2,1)S(1)}, u32[]{:S(2)}, u32[]{:S(2)}) collective-permute-start(bf16[256,1024]{1,0:T(8,128)(2,1)S(1)} %get-tuple-element.41), channel_id=1, source_target_pairs={{0,1},{1,0},{2,3},{3,2},{4,5},{5,4},{6,7},{7,6},{8,9},{9,8},{10,11... | collective-permute-start | bytes 1572872 | tf_op jit(solution)/shard_map/ppermute | solution.py:521
  18.4 2.4 %collective-permute-start.2 = (bf16[256,1024]{1,0:T(8,128)(2,1)S(1)}, bf16[256,1024]{1,0:T(8,128)(2,1)S(1)}, u32[]{:S(2)}, u32[]{:S(2)}) collective-permute-start(bf16[256,1024]{1,0:T(8,128)(2,1)S(1)} %get-tuple-element.42), channel_id=1, source_target_pairs={{0,1},{1,0},{2,3},{3,2},{4,5},{5,4},{6,7},{7,6},{8,9},{9,8},{10,11... | collective-permute-start | bytes 1572872 | tf_op jit(solution)/shard_map/ppermute | solution.py:521
  18.5 10.0 %collective-permute-start.5 = (bf16[144,1024]{1,0:T(8,128)(2,1)S(1)}, bf16[144,1024]{1,0:T(8,128)(2,1)S(1)}, u32[]{:S(2)}, u32[]{:S(2)}) collective-permute-start(bf16[144,1024]{1,0:T(8,128)(2,1)S(1)} %get-tuple-element.45), channel_id=1, source_target_pairs={{4,0},{8,4},{12,8},{16,12},{20,16},{24,20},{28,24},{5,1},{9,5},{13... | collective-permute-start | bytes 884744 | tf_op jit(solution)/shard_map/ppermute | solution.py:28
  22.1 19.6 %collective-permute-start.3 = (bf16[256,1024]{1,0:T(8,128)(2,1)S(1)}, bf16[256,1024]{1,0:T(8,128)(2,1)S(1)}, u32[]{:S(2)}, u32[]{:S(2)}) collective-permute-start(bf16[256,1024]{1,0:T(8,128)(2,1)S(1)} %get-tuple-element.43), channel_id=1, source_target_pairs={{0,2},{1,3},{2,0},{3,1},{4,6},{5,7},{6,4},{7,5},{8,10},{9,11},{10,... | collective-permute-start | bytes 1572872 | tf_op jit(solution)/shard_map/ppermute | solution.py:526
  23.4 22.8 %collective-permute-start.4 = (bf16[256,1024]{1,0:T(8,128)(2,1)S(1)}, bf16[256,1024]{1,0:T(8,128)(2,1)S(1)}, u32[]{:S(2)}, u32[]{:S(2)}) collective-permute-start(bf16[256,1024]{1,0:T(8,128)(2,1)S(1)} %get-tuple-element.44), channel_id=1, source_target_pairs={{0,2},{1,3},{2,0},{3,1},{4,6},{5,7},{6,4},{7,5},{8,10},{9,11},{10,... | collective-permute-start | bytes 1572872 | tf_op jit(solution)/shard_map/ppermute | solution.py:526
  30.9 6.0 %collective-permute-start.8 = (bf16[32,1024]{1,0:T(8,128)(2,1)S(1)}, bf16[32,1024]{1,0:T(8,128)(2,1)S(1)}, u32[]{:S(2)}, u32[]{:S(2)}) collective-permute-start(bf16[32,1024]{1,0:T(8,128)(2,1)S(1)} %get-tuple-element.55), channel_id=1, source_target_pairs={{0,12},{4,8},{8,4},{12,0},{16,28},{20,24},{24,20},{28,16},{1,13},{... | collective-permute-start | bytes 196616 | tf_op jit(solution)/shard_map/ppermute | solution.py:571
  32.1 4.8 %collective-permute-start.7 = (bf16[32,1024]{1,0:T(8,128)(2,1)S(1)}, bf16[32,1024]{1,0:T(8,128)(2,1)S(1)}, u32[]{:S(2)}, u32[]{:S(2)}) collective-permute-start(bf16[32,1024]{1,0:T(8,128)(2,1)S(1)} %get-tuple-element.55), channel_id=1, source_target_pairs={{0,8},{4,12},{8,0},{12,4},{16,24},{20,28},{24,16},{28,20},{1,9},{5... | collective-permute-start | bytes 196616 | tf_op jit(solution)/shard_map/ppermute | solution.py:571
  32.1 4.8 %collective-permute-start.6 = (bf16[32,1024]{1,0:T(8,128)(2,1)S(1)}, bf16[32,1024]{1,0:T(8,128)(2,1)S(1)}, u32[]{:S(2)}, u32[]{:S(2)}) collective-permute-start(bf16[32,1024]{1,0:T(8,128)(2,1)S(1)} %get-tuple-element.55), channel_id=1, source_target_pairs={{0,4},{4,0},{8,12},{12,8},{16,20},{20,16},{24,28},{28,24},{1,5},{5... | collective-permute-start | bytes 196616 | tf_op jit(solution)/shard_map/ppermute | solution.py:571
  36.9 4.8 %collective-permute-start.9 = (bf16[32,1024]{1,0:T(8,128)(2,1)S(1)}, bf16[32,1024]{1,0:T(8,128)(2,1)S(1)}, u32[]{:S(2)}, u32[]{:S(2)}) collective-permute-start(bf16[32,1024]{1,0:T(8,128)(2,1)S(1)} %add_convert_fusion.2.refs_0_), channel_id=1, source_target_pairs={{0,16},{4,20},{8,24},{12,28},{16,0},{20,4},{24,8},{28,12},{1,17},{... | collective-permute-start | bytes 196616 | tf_op jit(solution)/shard_map/ppermute | solution.py:571
  46.4 3.2 %collective-permute-start.11 = (bf16[256,1024]{1,0:T(8,128)(2,1)S(1)}, bf16[256,1024]{1,0:T(8,128)(2,1)S(1)}, u32[]{:S(2)}, u32[]{:S(2)}) collective-permute-start(bf16[256,1024]{1,0:T(8,128)(2,1)S(1)} %add_convert_fusion.own_ref), channel_id=1, source_target_pairs={{0,1},{1,0},{2,3},{3,2},{4,5},{5,4},{6,7},{7,6},{8,9},{9,8},{10,11... | collective-permute-start | bytes 1572872 | tf_op jit(solution)/shard_map/ppermute | solution.py:589
  48.2 2.3 %collective-permute-start.10 = (bf16[256,1024]{1,0:T(8,128)(2,1)S(1)}, bf16[256,1024]{1,0:T(8,128)(2,1)S(1)}, u32[]{:S(2)}, u32[]{:S(2)}) collective-permute-start(bf16[256,1024]{1,0:T(8,128)(2,1)S(1)} %add_convert_fusion.1.own_ref), channel_id=1, source_target_pairs={{0,1},{1,0},{2,3},{3,2},{4,5},{5,4},{6,7},{7,6},{8,9},{9,8},{10,11... | collective-permute-start | bytes 1572872 | tf_op jit(solution)/shard_map/ppermute | solution.py:589

commit v9 on v7

--- a/solution.py
+++ b/solution.py
@@ -10,7 +10,7 @@
 LANES = 128
 RIM = 16
 EDGE = 8
-SUB = 32
+SUB = 16
 COST = 1024
 PIECES = 2
 F32 = jnp.float32

time: 52.1 us -> 51.9 us (level)
    ppermute x2, waiting for transfers between devices: 3.14 us -> 2.32 us  [shifted(): lax.ppermute(value, axis, [(source, source + steps) for source in range(i...]
    pallas_call x1, Pallas kernels: 2.95 us -> 3.77 us  [local(): call(functools.partial(lags_kernel, group), 'lags', (shape((rows, chans),...]
  transfers between devices with their start and end apart: 12 -> 12, of which waited for: 5 -> 5; matrix products, arithmetic and copies ran while one was open for 1% -> 1% of each run, Pallas kernels for 33% -> 34%
where the time goes in v9:
time: 51.9 us; the launch traced here: 51.7 us
  Pallas kernels  24.2 us (47%)
  starting transfers between devices  13.8 us (27%)
  waiting for transfers between devices  11.9 us (23%)
  between operations  0.93 us (2%)
  other arithmetic  0.8 us (2%)
    pallas_call x1, Pallas kernels, local(): call(grad_gate_kernel, 'grad_gate', (shape((rows, chans), F32), shape((LA...  5.55 us
    ppermute x2, starting transfers between devices, shifted(): lax.ppermute(value, axis, [(source, source + steps) for source in range(i...  5.4 us
    ppermute x2, waiting for transfers between devices, local(): got = [lax.ppermute(value, 'tp', pairwise('tp', step)) for value in mine]  4.86 us
    pallas_call x1, Pallas kernels, local(): call(functools.partial(forward_kernel, group), 'forward', (piece,) * PIEC...  4.15 us
    ppermute x4, waiting for transfers between devices, local(): lax.ppermute(terms[0], 'ctx', pairwise('ctx', i * hop))  4.1 us
    pallas_call x1, Pallas kernels, local(): call(functools.partial(lags_kernel, group), 'lags', (shape((rows, chans),...  3.77 us
    ppermute x4, starting transfers between devices, local(): lax.ppermute(terms[0], 'ctx', pairwise('ctx', i * hop))  3.41 us
    pallas_call x1, Pallas kernels, local(): call(functools.partial(inputs_kernel, group), 'inputs', shape((3, rows, c...  3.27 us
  transfers between devices with their start and end apart: 12, of which 5 were waited for; matrix products, arithmetic and copies ran while one was open for 1% of the time, Pallas kernels for 34%

profile of v9, /device:TPU:25, one launch (start us, length us, event | category | flops | bytes accessed | tf_op | source)
XLA Modules:
  0.0 51.7 jit_solution(12202473280146697660)
XLA Ops:
  0.6 1.5 %tail.1 = (bf16[136,1024]{1,0:T(8,128)(2,1)S(1)}, bf16[3,256,1024]{2,1,0:T(8,128)(2,1)S(1)}, f32[3,3,1024]{2,1,0:T(4,128)S(1)}, bf16[64,128]{1,0:T(8,128)(2,1)S(1)}) custom-call(bf16[3,256,1024]{2,1,0:T(8,128)(2,1)} %bitcast.4, f32[3,3,1024]{2,1,0:T(4,128)} %taps_hbm.1, bf16[64,128]{1,0:T(8,128)(2,1)} %filt_hbm.1), custom_call_target="tpu_custom_call" | custom-call | bytes 1024 | tf_op jit(solution)/shard_map/tail/pallas_call | solution.py:474
  2.2 3.1 %collective-permute-start = (bf16[136,1024]{1,0:T(8,128)(2,1)S(1)}, bf16[136,1024]{1,0:T(8,128)(2,1)S(1)}, u32[]{:S(2)}, u32[]{:S(2)}) collective-permute-start(bf16[136,1024]{1,0:T(8,128)(2,1)S(1)} %get-tuple-element.38), channel_id=1, source_target_pairs={{0,4},{4,8},{8,12},{12,16},{16,20},{20,24},{24,28},{1,5},{5,9},{9,... | collective-permute-start | bytes 835592 | tf_op jit(solution)/shard_map/ppermute | solution.py:28
  5.3 5.6 %grad_gate.1 = (f32[256,1024]{1,0:T(8,128)S(1)}, bf16[144,1024]{1,0:T(8,128)(2,1)S(1)}, bf16[1024,4096]{1,0:T(8,128)(2,1)S(1)}) custom-call(bf16[256,4096]{1,0:T(8,128)(2,1)} %c_hbm.1, bf16[1024,4096]{1,0:T(8,128)(2,1)} %w_hbm.1, bf16[3,256,1024]{2,1,0:T(8,128)(2,1)S(1)} %get-tuple-element.35.x_ref, f32[3,3,1024]{2,1,0:T(4,128)S(1)} %get-tuple-element.36.taps_ref), custom_call_target="tpu_custom_call" | custom-call | bytes 1024 | tf_op jit(solution)/shard_map/grad_gate/pallas_call | solution.py:487
  10.8 1.6 %collective-permute-done.halo_ref = bf16[136,1024]{1,0:T(8,128)(2,1)S(1)} collective-permute-done((bf16[136,1024]{1,0:T(8,128)(2,1)S(1)}, bf16[136,1024]{1,0:T(8,128)(2,1)S(1)}, u32[]{:S(2)}, u32[]{:S(2)}) %collective-permute-start) | collective-permute-done | bytes 278560 | tf_op jit(solution)/shard_map/ppermute | solution.py:28
  12.5 4.1 %forward.1 = (bf16[256,1024]{1,0:T(8,128)(2,1)S(1)}, bf16[256,1024]{1,0:T(8,128)(2,1)S(1)}, bf16[256,1024]{1,0:T(8,128)(2,1)S(1)}, f32[256,1024]{1,0:T(8,128)S(1)}, bf16[384,1024]{1,0:T(8,128)(2,1)S(1)}) custom-call(s32[1]{0:T(128)} %bitcast.1.which_ref, bf16[3,256,1024]{2,1,0:T(8,128)(2,1)S(1)} %get-tuple-element.35.x_ref, ...), custom_call_target="tpu_custom_call" | custom-call | bytes 1024 | tf_op jit(solution)/shard_map/forward/pallas_call | solution.py:507
  16.6 1.6 %collective-permute-start.1 = (bf16[256,1024]{1,0:T(8,128)(2,1)S(1)}, bf16[256,1024]{1,0:T(8,128)(2,1)S(1)}, u32[]{:S(2)}, u32[]{:S(2)}) collective-permute-start(bf16[256,1024]{1,0:T(8,128)(2,1)S(1)} %get-tuple-element.42), channel_id=1, source_target_pairs={{0,1},{1,0},{2,3},{3,2},{4,5},{5,4},{6,7},{7,6},{8,9},{9,8},{10,11... | collective-permute-start | bytes 1572872 | tf_op jit(solution)/shard_map/ppermute | solution.py:520
  18.2 0.1 collective-permute-start.3
  18.3 2.3 %collective-permute-start.5 = (bf16[144,1024]{1,0:T(8,128)(2,1)S(1)}, bf16[144,1024]{1,0:T(8,128)(2,1)S(1)}, u32[]{:S(2)}, u32[]{:S(2)}) collective-permute-start(bf16[144,1024]{1,0:T(8,128)(2,1)S(1)} %get-tuple-element.45), channel_id=1, source_target_pairs={{4,0},{8,4},{12,8},{16,12},{20,16},{24,20},{28,24},{5,1},{9,5},{13... | collective-permute-start | bytes 884744 | tf_op jit(solution)/shard_map/ppermute | solution.py:28
  20.6 1.3 %keep.1 = (bf16[256,1024]{1,0:T(8,128)(2,1)S(1)}, bf16[256,1024]{1,0:T(8,128)(2,1)S(1)}) custom-call(s32[1]{0:T(128)} %bitcast.which_ref, bf16[256,1024]{1,0:T(8,128)(2,1)S(1)} %get-tuple-element.40.gate_ref, bf16[1024,4096]{1,0:T(8,128)(2,1)S(1)} %get-tuple-element.39.w_ref), custom_call_target="tpu_custom_call" | custom-call | bytes 1024 | tf_op jit(solution)/shard_map/keep/pallas_call | solution.py:521
  21.9 0.0 collective-permute-done.1
  21.9 0.2 add_convert_fusion.3
  22.1 1.3 %collective-permute-start.2 = (bf16[256,1024]{1,0:T(8,128)(2,1)S(1)}, bf16[256,1024]{1,0:T(8,128)(2,1)S(1)}, u32[]{:S(2)}, u32[]{:S(2)}) collective-permute-start(bf16[256,1024]{1,0:T(8,128)(2,1)S(1)} %add_convert_fusion.3), channel_id=1, source_target_pairs={{0,2},{1,3},{2,0},{3,1},{4,6},{5,7},{6,4},{7,5},{8,10},{9,11},{10,... | collective-permute-start | bytes 1572872 | tf_op jit(solution)/shard_map/ppermute | solution.py:528
  23.4 0.0 collective-permute-done.3
  23.4 0.2 add_convert_fusion.2
  23.6 0.3 collective-permute-start.4
  23.9 3.8 %lags.1 = (bf16[256,1024]{1,0:T(8,128)(2,1)S(1)}, bf16[256,1024]{1,0:T(8,128)(2,1)S(1)}, f32[16,1024]{1,0:T(8,128)S(1)}, bf16[8,128,144]{2,1,0:T(8,128)(2,1)S(1)}) custom-call(bf16[64,128]{1,0:T(8,128)(2,1)S(1)} %get-tuple-element.37.filt_ref, bf16[3,256,1024]{2,1,0:T(8,128)(2,1)S(1)} %get-tuple-element.35.x_ref, ...), custom_call_target="tpu_custom_call" | custom-call | bytes 1024 | tf_op jit(solution)/shard_map/lags/pallas_call | solution.py:532
  27.7 0.7 %collective-permute-done.5.back_ref = bf16[144,1024]{1,0:T(8,128)(2,1)S(1)} collective-permute-done((bf16[144,1024]{1,0:T(8,128)(2,1)S(1)}, bf16[144,1024]{1,0:T(8,128)(2,1)S(1)}, u32[]{:S(2)}, u32[]{:S(2)}) %collective-permute-start.5) | collective-permute-done | bytes 294944 | tf_op jit(solution)/shard_map/ppermute | solution.py:28
  28.4 2.1 %backward.1 = (bf16[2,256,1024]{2,1,0:T(8,128)(2,1)S(1)}, bf16[32,1024]{1,0:T(8,128)(2,1)S(1)}) custom-call(bf16[3,256,1024]{2,1,0:T(8,128)(2,1)S(1)} %get-tuple-element.35.x_ref, f32[3,3,1024]{2,1,0:T(4,128)S(1)} %get-tuple-element.36.taps_ref, bf16[136,1024]{1,0:T(8,128)(2,1)S(1)} %collective-permute-done.halo_ref, ...), custom_call_target="tpu_custom_call" | custom-call | bytes 1024 | tf_op jit(solution)/shard_map/backward/pallas_call | solution.py:550
  30.4 1.2 %collective-permute-start.8 = (bf16[32,1024]{1,0:T(8,128)(2,1)S(1)}, bf16[32,1024]{1,0:T(8,128)(2,1)S(1)}, u32[]{:S(2)}, u32[]{:S(2)}) collective-permute-start(bf16[32,1024]{1,0:T(8,128)(2,1)S(1)} %get-tuple-element.55), channel_id=1, source_target_pairs={{0,12},{4,8},{8,4},{12,0},{16,28},{20,24},{24,20},{28,16},{1,13},{... | collective-permute-start | bytes 196616 | tf_op jit(solution)/shard_map/ppermute | solution.py:573
  31.6 0.7 %collective-permute-start.7 = (bf16[32,1024]{1,0:T(8,128)(2,1)S(1)}, bf16[32,1024]{1,0:T(8,128)(2,1)S(1)}, u32[]{:S(2)}, u32[]{:S(2)}) collective-permute-start(bf16[32,1024]{1,0:T(8,128)(2,1)S(1)} %get-tuple-element.55), channel_id=1, source_target_pairs={{0,8},{4,12},{8,0},{12,4},{16,24},{20,28},{24,16},{28,20},{1,9},{5... | collective-permute-start | bytes 196616 | tf_op jit(solution)/shard_map/ppermute | solution.py:573
  32.3 0.9 %collective-permute-start.6 = (bf16[32,1024]{1,0:T(8,128)(2,1)S(1)}, bf16[32,1024]{1,0:T(8,128)(2,1)S(1)}, u32[]{:S(2)}, u32[]{:S(2)}) collective-permute-start(bf16[32,1024]{1,0:T(8,128)(2,1)S(1)} %get-tuple-element.55), channel_id=1, source_target_pairs={{0,4},{4,0},{8,12},{12,8},{16,20},{20,16},{24,28},{28,24},{1,5},{5... | collective-permute-start | bytes 196616 | tf_op jit(solution)/shard_map/ppermute | solution.py:573
  33.2 3.3 %inputs.1 = bf16[3,256,1024]{2,1,0:T(8,128)(2,1)} custom-call(bf16[3,256,1024]{2,1,0:T(8,128)(2,1)S(1)} %get-tuple-element.35.x_ref, f32[3,3,1024]{2,1,0:T(4,128)S(1)} %get-tuple-element.36.taps_ref, bf16[64,128]{1,0:T(8,128)(2,1)S(1)} %get-tuple-element.37.filt_ref, bf16[384,1024]{1,0:T(8,128)(2,1)S(1)} %get-tuple-element.48.gext_ref, ...), custom_call_target="tpu_custom_call" | custom-call | bytes 1024 | tf_op jit(solution)/shard_map/inputs/pallas_call | solution.py:557
  36.4 0.0 collective-permute-done.8
  36.4 0.0 collective-permute-done.7
  36.4 0.0 collective-permute-done.6
  36.5 0.7 %collective-permute-start.9 = (bf16[32,1024]{1,0:T(8,128)(2,1)S(1)}, bf16[32,1024]{1,0:T(8,128)(2,1)S(1)}, u32[]{:S(2)}, u32[]{:S(2)}) collective-permute-start(bf16[32,1024]{1,0:T(8,128)(2,1)S(1)} %add_convert_fusion.4.refs_0_), channel_id=1, source_target_pairs={{0,16},{4,20},{8,24},{12,28},{16,0},{20,4},{24,8},{28,12},{1,17},{... | collective-permute-start | bytes 196616 | tf_op jit(solution)/shard_map/ppermute | solution.py:573
  37.2 4.1 %collective-permute-done.9.refs_1_ = bf16[32,1024]{1,0:T(8,128)(2,1)S(1)} collective-permute-done((bf16[32,1024]{1,0:T(8,128)(2,1)S(1)}, bf16[32,1024]{1,0:T(8,128)(2,1)S(1)}, u32[]{:S(2)}, u32[]{:S(2)}) %collective-permute-start.9) | collective-permute-done | bytes 65568 | tf_op jit(solution)/shard_map/ppermute | solution.py:573
  41.3 0.0 collective-permute-done.2
  41.3 4.9 %collective-permute-done.4 = bf16[256,1024]{1,0:T(8,128)(2,1)S(1)} collective-permute-done((bf16[256,1024]{1,0:T(8,128)(2,1)S(1)}, bf16[256,1024]{1,0:T(8,128)(2,1)S(1)}, u32[]{:S(2)}, u32[]{:S(2)}) %collective-permute-start.4) | collective-permute-done | bytes 524320 | tf_op jit(solution)/shard_map/ppermute | solution.py:528
  46.1 0.2 add_convert_fusion.own_ref
  46.3 1.7 %collective-permute-start.11 = (bf16[256,1024]{1,0:T(8,128)(2,1)S(1)}, bf16[256,1024]{1,0:T(8,128)(2,1)S(1)}, u32[]{:S(2)}, u32[]{:S(2)}) collective-permute-start(bf16[256,1024]{1,0:T(8,128)(2,1)S(1)} %add_convert_fusion.own_ref), channel_id=1, source_target_pairs={{0,1},{1,0},{2,3},{3,2},{4,5},{5,4},{6,7},{7,6},{8,9},{9,8},{10,11... | collective-permute-start | bytes 1572872 | tf_op jit(solution)/shard_map/ppermute | solution.py:591
  48.0 0.2 add_convert_fusion.1.own_ref
  48.2 0.1 collective-permute-start.10
  48.3 0.6 %unpack.1 = (f32[3,3,1024]{2,1,0:T(4,128)}, f32[64,128]{1,0:T(8,128)}) custom-call(bf16[32,1024]{1,0:T(8,128)(2,1)S(1)} %add_convert_fusion.4.refs_0_, bf16[32,1024]{1,0:T(8,128)(2,1)S(1)} %collective-permute-done.9.refs_1_), custom_call_target="tpu_custom_call" | custom-call | bytes 1024 | tf_op jit(solution)/shard_map/unpack/pallas_call | solution.py:597
  48.9 0.6 %collective-permute-done.11.sibling_ref = bf16[256,1024]{1,0:T(8,128)(2,1)S(1)} collective-permute-done((bf16[256,1024]{1,0:T(8,128)(2,1)S(1)}, bf16[256,1024]{1,0:T(8,128)(2,1)S(1)}, u32[]{:S(2)}, u32[]{:S(2)}) %collective-permute-start.11) | collective-permute-done | bytes 524320 | tf_op jit(solution)/shard_map/ppermute | solution.py:591
  49.5 1.0 %place.2.refs_0_ = bf16[256,4096]{1,0:T(8,128)(2,1)} custom-call(s32[1]{0:T(128)} %bitcast.which_ref, bf16[256,1024]{1,0:T(8,128)(2,1)S(1)} %add_convert_fusion.own_ref, bf16[256,1024]{1,0:T(8,128)(2,1)S(1)} %collective-permute-done.11.sibling_ref), custom_call_target="tpu_custom_call" | custom-call | tf_op jit(solution)/shard_map/place/pallas_call | solution.py:446
  50.5 0.0 collective-permute-done.10.sibling_ref
  50.5 1.0 %place.3 = bf16[256,4096]{1,0:T(8,128)(2,1)} custom-call(s32[1]{0:T(128)} %bitcast.which_ref, bf16[256,1024]{1,0:T(8,128)(2,1)S(1)} %add_convert_fusion.1.own_ref, bf16[256,1024]{1,0:T(8,128)(2,1)S(1)} %collective-permute-done.10.sibling_ref, bf16[256,4096]{1,0:T(8,128)(2,1)} %place.2.refs_0_), custom_call_target="tpu_custom_call", output_to_operand_aliasing={{}: (3, {})} | custom-call | tf_op jit(solution)/shard_map/place/pallas_call | solution.py:446
  (1 shorter events, 0.0 us)
Async XLA Ops:
  2.2 10.3 %collective-permute-start = (bf16[136,1024]{1,0:T(8,128)(2,1)S(1)}, bf16[136,1024]{1,0:T(8,128)(2,1)S(1)}, u32[]{:S(2)}, u32[]{:S(2)}) collective-permute-start(bf16[136,1024]{1,0:T(8,128)(2,1)S(1)} %get-tuple-element.38), channel_id=1, source_target_pairs={{0,4},{4,8},{8,12},{12,16},{16,20},{20,24},{24,28},{1,5},{5,9},{9,... | collective-permute-start | bytes 835592 | tf_op jit(solution)/shard_map/ppermute | solution.py:28
  16.6 5.2 %collective-permute-start.1 = (bf16[256,1024]{1,0:T(8,128)(2,1)S(1)}, bf16[256,1024]{1,0:T(8,128)(2,1)S(1)}, u32[]{:S(2)}, u32[]{:S(2)}) collective-permute-start(bf16[256,1024]{1,0:T(8,128)(2,1)S(1)} %get-tuple-element.42), channel_id=1, source_target_pairs={{0,1},{1,0},{2,3},{3,2},{4,5},{5,4},{6,7},{7,6},{8,9},{9,8},{10,11... | collective-permute-start | bytes 1572872 | tf_op jit(solution)/shard_map/ppermute | solution.py:520
  18.2 5.2 %collective-permute-start.3 = (bf16[256,1024]{1,0:T(8,128)(2,1)S(1)}, bf16[256,1024]{1,0:T(8,128)(2,1)S(1)}, u32[]{:S(2)}, u32[]{:S(2)}) collective-permute-start(bf16[256,1024]{1,0:T(8,128)(2,1)S(1)} %get-tuple-element.44), channel_id=1, source_target_pairs={{0,1},{1,0},{2,3},{3,2},{4,5},{5,4},{6,7},{7,6},{8,9},{9,8},{10,11... | collective-permute-start | bytes 1572872 | tf_op jit(solution)/shard_map/ppermute | solution.py:520
  18.3 10.0 %collective-permute-start.5 = (bf16[144,1024]{1,0:T(8,128)(2,1)S(1)}, bf16[144,1024]{1,0:T(8,128)(2,1)S(1)}, u32[]{:S(2)}, u32[]{:S(2)}) collective-permute-start(bf16[144,1024]{1,0:T(8,128)(2,1)S(1)} %get-tuple-element.45), channel_id=1, source_target_pairs={{4,0},{8,4},{12,8},{16,12},{20,16},{24,20},{28,24},{5,1},{9,5},{13... | collective-permute-start | bytes 884744 | tf_op jit(solution)/shard_map/ppermute | solution.py:28
  22.1 19.2 %collective-permute-start.2 = (bf16[256,1024]{1,0:T(8,128)(2,1)S(1)}, bf16[256,1024]{1,0:T(8,128)(2,1)S(1)}, u32[]{:S(2)}, u32[]{:S(2)}) collective-permute-start(bf16[256,1024]{1,0:T(8,128)(2,1)S(1)} %add_convert_fusion.3), channel_id=1, source_target_pairs={{0,2},{1,3},{2,0},{3,1},{4,6},{5,7},{6,4},{7,5},{8,10},{9,11},{10,... | collective-permute-start | bytes 1572872 | tf_op jit(solution)/shard_map/ppermute | solution.py:528
  23.6 22.5 %collective-permute-start.4 = (bf16[256,1024]{1,0:T(8,128)(2,1)S(1)}, bf16[256,1024]{1,0:T(8,128)(2,1)S(1)}, u32[]{:S(2)}, u32[]{:S(2)}) collective-permute-start(bf16[256,1024]{1,0:T(8,128)(2,1)S(1)} %add_convert_fusion.2), channel_id=1, source_target_pairs={{0,2},{1,3},{2,0},{3,1},{4,6},{5,7},{6,4},{7,5},{8,10},{9,11},{10,... | collective-permute-start | bytes 1572872 | tf_op jit(solution)/shard_map/ppermute | solution.py:528
  30.4 6.0 %collective-permute-start.8 = (bf16[32,1024]{1,0:T(8,128)(2,1)S(1)}, bf16[32,1024]{1,0:T(8,128)(2,1)S(1)}, u32[]{:S(2)}, u32[]{:S(2)}) collective-permute-start(bf16[32,1024]{1,0:T(8,128)(2,1)S(1)} %get-tuple-element.55), channel_id=1, source_target_pairs={{0,12},{4,8},{8,4},{12,0},{16,28},{20,24},{24,20},{28,16},{1,13},{... | collective-permute-start | bytes 196616 | tf_op jit(solution)/shard_map/ppermute | solution.py:573
  31.6 4.8 %collective-permute-start.7 = (bf16[32,1024]{1,0:T(8,128)(2,1)S(1)}, bf16[32,1024]{1,0:T(8,128)(2,1)S(1)}, u32[]{:S(2)}, u32[]{:S(2)}) collective-permute-start(bf16[32,1024]{1,0:T(8,128)(2,1)S(1)} %get-tuple-element.55), channel_id=1, source_target_pairs={{0,8},{4,12},{8,0},{12,4},{16,24},{20,28},{24,16},{28,20},{1,9},{5... | collective-permute-start | bytes 196616 | tf_op jit(solution)/shard_map/ppermute | solution.py:573
  32.3 4.2 %collective-permute-start.6 = (bf16[32,1024]{1,0:T(8,128)(2,1)S(1)}, bf16[32,1024]{1,0:T(8,128)(2,1)S(1)}, u32[]{:S(2)}, u32[]{:S(2)}) collective-permute-start(bf16[32,1024]{1,0:T(8,128)(2,1)S(1)} %get-tuple-element.55), channel_id=1, source_target_pairs={{0,4},{4,0},{8,12},{12,8},{16,20},{20,16},{24,28},{28,24},{1,5},{5... | collective-permute-start | bytes 196616 | tf_op jit(solution)/shard_map/ppermute | solution.py:573
  36.5 4.8 %collective-permute-start.9 = (bf16[32,1024]{1,0:T(8,128)(2,1)S(1)}, bf16[32,1024]{1,0:T(8,128)(2,1)S(1)}, u32[]{:S(2)}, u32[]{:S(2)}) collective-permute-start(bf16[32,1024]{1,0:T(8,128)(2,1)S(1)} %add_convert_fusion.4.refs_0_), channel_id=1, source_target_pairs={{0,16},{4,20},{8,24},{12,28},{16,0},{20,4},{24,8},{28,12},{1,17},{... | collective-permute-start | bytes 196616 | tf_op jit(solution)/shard_map/ppermute | solution.py:573
  46.3 3.2 %collective-permute-start.11 = (bf16[256,1024]{1,0:T(8,128)(2,1)S(1)}, bf16[256,1024]{1,0:T(8,128)(2,1)S(1)}, u32[]{:S(2)}, u32[]{:S(2)}) collective-permute-start(bf16[256,1024]{1,0:T(8,128)(2,1)S(1)} %add_convert_fusion.own_ref), channel_id=1, source_target_pairs={{0,1},{1,0},{2,3},{3,2},{4,5},{5,4},{6,7},{7,6},{8,9},{9,8},{10,11... | collective-permute-start | bytes 1572872 | tf_op jit(solution)/shard_map/ppermute | solution.py:591
  48.2 2.3 %collective-permute-start.10 = (bf16[256,1024]{1,0:T(8,128)(2,1)S(1)}, bf16[256,1024]{1,0:T(8,128)(2,1)S(1)}, u32[]{:S(2)}, u32[]{:S(2)}) collective-permute-start(bf16[256,1024]{1,0:T(8,128)(2,1)S(1)} %add_convert_fusion.1.own_ref), channel_id=1, source_target_pairs={{0,1},{1,0},{2,3},{3,2},{4,5},{5,4},{6,7},{7,6},{8,9},{9,8},{10,11... | collective-permute-start | bytes 1572872 | tf_op jit(solution)/shard_map/ppermute | solution.py:591
